TPU v7x, 128 devices: a whole 4x4x4 slice. The times are simulated.
128 devices in a mesh: tm: 8 (over y_hi, z), height: 4 (over x), head: 4 (over y_lo, core).
Axes of the slice: x: 4, y: 4 (y_hi: 2, y_lo: 2; y = y_hi * 2 + y_lo), z: 4, core: 2. Of those that a mesh axis runs over, the one named last changes fastest.
Arguments:
- query_in: bfloat16 [12, 32, 32, 16, 128], P('head', 'tm', 'height'), may hold values from -8 to 8
- key_in: bfloat16 [12, 32, 32, 16, 128], P('head', 'tm', 'height'), may hold values from -8 to 8
- value_in: bfloat16 [12, 32, 32, 16, 128], P('head', 'tm', 'height'), may hold values from -6 to 6
- out_grad: bfloat16 [12, 32, 32, 16, 128], P('head', 'tm', 'height'), may hold values from -6 to 6
Outputs:
- query_grad: bfloat16 [12, 32, 32, 16, 128], P('head', 'tm', 'height')
- key_grad: bfloat16 [12, 32, 32, 16, 128], P('head', 'tm', 'height')
- value_grad: bfloat16 [12, 32, 32, 16, 128], P('head', 'tm', 'height')
All inputs are finite; a program needn't handle non-finite values.
Results may differ from a plain program's by a relative error of at most 0.0093.
Values may be sent and summed in bfloat16 or wider, within the bound.
No kernel may reach another device: no remote copies, remote signals or barrier semaphores. Data moves between devices by JAX's collectives and lax.ppermute only.
A program may use at most 128 MiB of HBM per device.

v0:
```python
import jax
import jax.numpy as jnp
from jax import lax
from jax.sharding import PartitionSpec as P

TILE_C = 8


def shifted(block, axis, distance):
    devices = range(lax.axis_size(axis))
    route = [(i - distance, i) for i in devices if i - distance in devices]
    return lax.ppermute(block, axis, route)


def shortened(x):
    return jax.tree.map(lambda a: a.astype(jnp.bfloat16) if a.dtype == jnp.float32 else a, x)


def extended(x, sides, width):
    for axis, dim in sides:
        size, length = (lax.axis_size(axis), x.shape[dim])
        up = [(i, (i + 1) % size) for i in range(size - 1)]
        down = [(j, i) for i, j in up]
        last = lax.slice_in_dim(x, length - width, length, axis=dim)
        first = lax.slice_in_dim(x, 0, width, axis=dim)
        before = lax.ppermute(last, axis, up)
        after = lax.ppermute(first, axis, down)
        x = jnp.concatenate([before, x, after], axis=dim)
    return x


def neighbour_live():
    offsets = jnp.arange(3, dtype=jnp.int32) - 1
    frame_pos = lax.axis_index("tm") + offsets
    row_pos = lax.axis_index("height") + offsets
    frame_ok = (frame_pos >= 0) & (frame_pos < lax.axis_size("tm"))
    row_ok = (row_pos >= 0) & (row_pos < lax.axis_size("height"))
    return frame_ok[:, None] & row_ok[None, :]


def span_live(neighbour_ok, tile_index, span_start, frame_count, row_count, span_width, col_tile):
    columns = span_start + jnp.arange(span_width, dtype=jnp.int32)
    near_cols = jnp.abs(columns // col_tile - tile_index) <= 1
    live_mask = neighbour_ok[:, :, None, None, None] & near_cols[None, None, None, None, :]
    return jnp.broadcast_to(live_mask, (3, 3, frame_count, row_count, span_width)).reshape(-1)


def scores_of(left_rows, right_rows, live_mask, score_scale):
    raw_scores = (
        jnp.einsum("hqd,hkd->hqk", left_rows, right_rows, preferred_element_type=jnp.float32)
        * score_scale
    )
    return jnp.where(live_mask, raw_scores, -jnp.inf)


def whole_span(array, span_start, span_size, axis_pos):
    return isinstance(span_start, int) and span_start == 0 and (span_size == array.shape[axis_pos])


def cut_span(array, span_start, span_size, axis_pos):
    if whole_span(array, span_start, span_size, axis_pos):
        return array
    return lax.dynamic_slice_in_dim(array, jnp.asarray(span_start, jnp.int32), span_size, axis_pos)


def add_span(array, piece):
    return array + piece


def run_tiles(tile_step, tile_count, col_tile, carried):
    edge_width = 2 * col_tile
    carried = tile_step(0, 0, edge_width, carried)
    return tile_step(tile_count - 1, (tile_count - 2) * col_tile, edge_width, carried)


def send_rows(parts, offset):
    return (
        shifted(parts[0].astype(jnp.bfloat16), "height", offset).astype(jnp.float32),
        shifted(parts[1].astype(jnp.bfloat16), "height", offset).astype(jnp.float32),
    )


def send_frames(parts, offset):
    return shifted((shortened(parts[0]), shortened(parts[1])), "tm", offset)


def local(query_in, key_in, value_in, out_grad):
    head_count, frame_count, row_count, col_count, head_depth = query_in.shape
    col_tile = TILE_C
    tile_count = col_count // col_tile
    score_scale = head_depth ** (-0.5)
    spread_shape = (head_count, 1, 1, frame_count, row_count, col_count, head_depth)
    ext_shape = (head_count, 3, 3, frame_count, row_count, col_count, head_depth)
    stat_shape = (head_count, frame_count, row_count, col_tile)
    neighbour_ok = neighbour_live()
    keys_ext, values_ext = (
        extended(key_in.reshape(spread_shape), (("tm", 1), ("height", 2)), 1),
        extended(value_in.reshape(spread_shape), (("tm", 1), ("height", 2)), 1),
    )

    def query_step(tile_index, span_start, span_width, carried):
        grad_q, row_totals, row_deltas, grad_k, grad_v = carried
        own_start = jnp.asarray(tile_index * col_tile, jnp.int32)
        q_rows = cut_span(query_in, own_start, col_tile, 3).reshape(head_count, -1, head_depth)
        g_rows = cut_span(out_grad, own_start, col_tile, 3).reshape(head_count, -1, head_depth)
        k_span = cut_span(keys_ext, span_start, span_width, 5).reshape(head_count, -1, head_depth)
        v_span = cut_span(values_ext, span_start, span_width, 5).reshape(head_count, -1, head_depth)
        live_mask = span_live(
            neighbour_ok, tile_index, span_start, frame_count, row_count, span_width, col_tile
        )
        scores = scores_of(q_rows, k_span, live_mask[None, None, :], score_scale)
        row_max = jnp.max(scores, axis=-1, keepdims=True)
        log_total = row_max + jnp.log(jnp.sum(jnp.exp(scores - row_max), axis=-1, keepdims=True))
        weights = jnp.exp(scores - log_total)
        weight_bf = weights.astype(jnp.bfloat16)
        attended = jnp.einsum("hqk,hkd->hqd", weight_bf, v_span, preferred_element_type=jnp.float32)
        row_delta = jnp.sum(g_rows.astype(jnp.float32) * attended, axis=-1, keepdims=True)
        d_weights = jnp.einsum("hqd,hkd->hqk", g_rows, v_span, preferred_element_type=jnp.float32)
        d_scores = (weights * (d_weights - row_delta)).astype(jnp.bfloat16)
        grad_piece = (
            jnp.einsum("hqk,hkd->hqd", d_scores, k_span, preferred_element_type=jnp.float32)
            * score_scale
        )
        grad_q = lax.dynamic_update_slice_in_dim(
            grad_q, grad_piece.reshape(stat_shape + (head_depth,)), own_start, 3
        )
        row_totals = lax.dynamic_update_slice_in_dim(
            row_totals, log_total.reshape(stat_shape), own_start, 3
        )
        row_deltas = lax.dynamic_update_slice_in_dim(
            row_deltas, row_delta.reshape(stat_shape), own_start, 3
        )
        span_shape = (head_count, 3, 3, frame_count, row_count, span_width, head_depth)
        key_piece = (
            jnp.einsum("hqk,hqd->hkd", d_scores, q_rows, preferred_element_type=jnp.float32)
            * score_scale
        )
        value_piece = jnp.einsum(
            "hqk,hqd->hkd", weight_bf, g_rows, preferred_element_type=jnp.float32
        )
        grad_k = add_span(grad_k, key_piece.reshape(span_shape))
        grad_v = add_span(grad_v, value_piece.reshape(span_shape))
        return (grad_q, row_totals, row_deltas, grad_k, grad_v)

    stat_full = (head_count, frame_count, row_count, col_count)
    initial = (
        jnp.zeros(query_in.shape, jnp.float32),
        jnp.zeros(stat_full, jnp.float32),
        jnp.zeros(stat_full, jnp.float32),
        jnp.zeros(ext_shape, jnp.float32),
        jnp.zeros(ext_shape, jnp.float32),
    )
    grad_q, row_totals, row_deltas, grad_k, grad_v = run_tiles(
        query_step, tile_count, col_tile, initial
    )
    query_grad = grad_q.astype(jnp.bfloat16)
    from_above = send_rows((grad_k[:, :, 0], grad_v[:, :, 0]), -1)
    from_below = send_rows((grad_k[:, :, 2], grad_v[:, :, 2]), 1)
    part_k = grad_k[:, :, 1] + from_above[0] + from_below[0]
    part_v = grad_v[:, :, 1] + from_above[1] + from_below[1]
    from_next = send_frames((part_k[:, 0], part_v[:, 0]), -1)
    from_prev = send_frames((part_k[:, 2], part_v[:, 2]), 1)
    key_total = part_k[:, 1] + from_next[0] + from_prev[0]
    value_total = part_v[:, 1] + from_next[1] + from_prev[1]
    return (query_grad, key_total.astype(jnp.bfloat16), value_total.astype(jnp.bfloat16))


def solution(mesh):
    return jax.shard_map(
        local,
        mesh=mesh,
        in_specs=(
            P("head", "tm", "height", None, None),
            P("head", "tm", "height", None, None),
            P("head", "tm", "height", None, None),
            P("head", "tm", "height", None, None),
        ),
        out_specs=(
            P("head", "tm", "height", None, None),
            P("head", "tm", "height", None, None),
            P("head", "tm", "height", None, None),
        ),
        check_vma=False,
    )
```

profile of v0, /device:TPU:18, one launch (start us, length us, event | category | flops | bytes accessed | tf_op | source)
XLA Modules:
  0.0 219.7 jit_solution(4156342760646788153)
XLA Ops:
  0.6 0.0 copy-start.9
  0.6 0.0 copy-start.10
  0.7 4.0 %collective-permute-start = (bf16[3,1,1,4,8,16,128]{6,5,4,3,0,2,1:T(8,128)(2,1)}, bf16[3,1,1,4,8,16,128]{6,5,4,3,0,2,1:T(8,128)(2,1)S(1)}, u32[]{:S(2)}, u32[]{:S(2)}) collective-permute-start(bf16[3,1,1,4,8,16,128]{6,5,4,3,0,2,1:T(8,128)(2,1)} %bitcast.154), channel_id=1, source_target_pairs={{0,16},{16,32},{32,48},{48,64},{64,80},{80,96},{96,112},{1,17},{17... | collective-permute-start | bytes 1179656 | tf_op jit(solution)/shard_map/ppermute | solution.py:26
  4.6 5.6 %collective-permute-start.1 = (bf16[3,1,1,4,8,16,128]{6,5,4,3,0,2,1:T(8,128)(2,1)}, bf16[3,1,1,4,8,16,128]{6,5,4,3,0,2,1:T(8,128)(2,1)S(1)}, u32[]{:S(2)}, u32[]{:S(2)}) collective-permute-start(bf16[3,1,1,4,8,16,128]{6,5,4,3,0,2,1:T(8,128)(2,1)} %bitcast.155), channel_id=1, source_target_pairs={{16,0},{32,16},{48,32},{64,48},{80,64},{96,80},{112,96},{17,1},{33... | collective-permute-start | bytes 1179656 | tf_op jit(solution)/shard_map/ppermute | solution.py:27
  10.3 1.9 collective-permute-start.4
  12.2 7.5 %collective-permute-start.5 = (bf16[3,1,1,4,8,16,128]{6,5,4,3,0,2,1:T(8,128)(2,1)}, bf16[3,1,1,4,8,16,128]{6,5,4,3,0,2,1:T(8,128)(2,1)S(1)}, u32[]{:S(2)}, u32[]{:S(2)}) collective-permute-start(bf16[3,1,1,4,8,16,128]{6,5,4,3,0,2,1:T(8,128)(2,1)} %bitcast.159), channel_id=1, source_target_pairs={{16,0},{32,16},{48,32},{64,48},{80,64},{96,80},{112,96},{17,1},{33... | collective-permute-start | bytes 1179656 | tf_op jit(solution)/shard_map/ppermute | solution.py:27
  19.8 0.0 collective-permute-done.1
  19.8 2.2 pad_maximum_fusion.2
  21.9 3.4 %collective-permute-start.2 = (bf16[3,3,1,4,8,16,128]{6,5,4,3,0,2,1:T(8,128)(2,1)}, bf16[3,3,1,4,8,16,128]{6,5,4,3,0,2,1:T(8,128)(2,1)}, u32[]{:S(2)}, u32[]{:S(2)}) collective-permute-start(bf16[3,3,1,4,8,16,128]{6,5,4,3,0,2,1:T(8,128)(2,1)} %pad_maximum_fusion.2), channel_id=1, source_target_pairs={{0,4},{4,8},{8,12},{1,5},{5,9},{9,13},{2,6},{6,10},{10,14},{3,7},{... | collective-permute-start | bytes 3538952 | tf_op jit(solution)/shard_map/ppermute | solution.py:26
  25.3 3.4 %collective-permute-start.3 = (bf16[3,3,1,4,8,16,128]{6,5,4,3,0,2,1:T(8,128)(2,1)}, bf16[3,3,1,4,8,16,128]{6,5,4,3,0,2,1:T(8,128)(2,1)}, u32[]{:S(2)}, u32[]{:S(2)}) collective-permute-start(bf16[3,3,1,4,8,16,128]{6,5,4,3,0,2,1:T(8,128)(2,1)} %pad_maximum_fusion.2), channel_id=1, source_target_pairs={{4,0},{8,4},{12,8},{5,1},{9,5},{13,9},{6,2},{10,6},{14,10},{7,3},{... | collective-permute-start | bytes 3538952 | tf_op jit(solution)/shard_map/ppermute | solution.py:27
  28.8 0.1 broadcast_and_fusion.2
  28.9 0.1 broadcast_and_fusion.1
  29.0 0.1 broadcast_in_dim.46
  29.1 0.1 broadcast_in_dim.50
  29.3 1.7 fusion.47
  31.0 0.1 fusion.46
  31.1 0.0 copy-start.11
  31.1 0.0 collective-permute-done.5
  31.1 0.0 copy-start.12
  31.2 1.3 pad_maximum_fusion.3
  32.4 2.4 %collective-permute-start.6 = (bf16[3,3,1,4,8,16,128]{6,5,4,3,0,2,1:T(8,128)(2,1)}, bf16[3,3,1,4,8,16,128]{6,5,4,3,0,2,1:T(8,128)(2,1)}, u32[]{:S(2)}, u32[]{:S(2)}) collective-permute-start(bf16[3,3,1,4,8,16,128]{6,5,4,3,0,2,1:T(8,128)(2,1)} %pad_maximum_fusion.3), channel_id=1, source_target_pairs={{0,4},{4,8},{8,12},{1,5},{5,9},{9,13},{2,6},{6,10},{10,14},{3,7},{... | collective-permute-start | bytes 3538952 | tf_op jit(solution)/shard_map/ppermute | solution.py:26
  34.8 4.4 %collective-permute-start.7 = (bf16[3,3,1,4,8,16,128]{6,5,4,3,0,2,1:T(8,128)(2,1)}, bf16[3,3,1,4,8,16,128]{6,5,4,3,0,2,1:T(8,128)(2,1)}, u32[]{:S(2)}, u32[]{:S(2)}) collective-permute-start(bf16[3,3,1,4,8,16,128]{6,5,4,3,0,2,1:T(8,128)(2,1)} %pad_maximum_fusion.3), channel_id=1, source_target_pairs={{4,0},{8,4},{12,8},{5,1},{9,5},{13,9},{6,2},{10,6},{14,10},{7,3},{... | collective-permute-start | bytes 3538952 | tf_op jit(solution)/shard_map/ppermute | solution.py:27
  39.3 13.8 %collective-permute-done.2 = bf16[3,3,1,4,8,16,128]{6,5,4,3,0,2,1:T(8,128)(2,1)} collective-permute-done((bf16[3,3,1,4,8,16,128]{6,5,4,3,0,2,1:T(8,128)(2,1)}, bf16[3,3,1,4,8,16,128]{6,5,4,3,0,2,1:T(8,128)(2,1)}, u32[]{:S(2)}, u32[]{:S(2)}) %collective-permute-start.2) | collective-permute-done | bytes 1179680 | tf_op jit(solution)/shard_map/ppermute | solution.py:26
  53.0 3.4 %collective-permute-done.3 = bf16[3,3,1,4,8,16,128]{6,5,4,3,0,2,1:T(8,128)(2,1)} collective-permute-done((bf16[3,3,1,4,8,16,128]{6,5,4,3,0,2,1:T(8,128)(2,1)}, bf16[3,3,1,4,8,16,128]{6,5,4,3,0,2,1:T(8,128)(2,1)}, u32[]{:S(2)}, u32[]{:S(2)}) %collective-permute-start.3) | collective-permute-done | bytes 1179680 | tf_op jit(solution)/shard_map/ppermute | solution.py:27
  56.5 1.8 pad_maximum_fusion
  58.3 1.2 copy.7
  59.6 4.3 %bitcast_reduce_fusion.1 = (f32[3,256]{1,0:T(4,128)S(1)}, f32[3,4608,256]{2,1,0:T(8,128)S(1)}) fusion(bf16[3,4608,128]{2,1,0:T(8,128)(2,1)S(1)} %bitcast.134, bf16[3,256,128]{2,1,0:T(8,128)(2,1)S(1)} %bitcast.152, pred[4608]{0:T(1024)(128)(4,1)S(1)} %broadcast_in_dim.46), kind=kOutput, calls=%fused_computation.12 | convolution fusion | flops 916585728 | bytes 17899008 | tf_op jit(solution)/shard_map/hqd,hkd->hqk/dot_general | solution.py:50
  63.9 1.8 fusion.6
  65.7 9.7 %bitcast_reduce_fusion = (f32[3,256]{1,0:T(4,128)S(1)}, f32[3,4608,256]{2,1,0:T(8,128)}) fusion(bf16[3,4608,128]{2,1,0:T(8,128)(2,1)} %bitcast.135, bf16[3,256,128]{2,1,0:T(8,128)(2,1)} %bitcast.150, pred[4608]{0:T(1024)(128)(4,1)S(1)} %broadcast_in_dim.50), kind=kOutput, calls=%fused_computation.4 | convolution fusion | flops 916585728 | bytes 17899008 | tf_op jit(solution)/shard_map/hqd,hkd->hqk/dot_general | solution.py:50
  75.4 6.9 %fusion.2 = f32[3,256]{1,0:T(4,128)S(1)} fusion(f32[3,4608,256]{2,1,0:T(8,128)} %get-tuple-element.22, f32[3,256]{1,0:T(4,128)S(1)} %get-tuple-element.21), kind=kLoop, calls=%fused_computation.6 | loop fusion | flops 7077120 | bytes 14161920 | tf_op jit(solution)/shard_map/reduce_sum | solution.py:113
  82.3 2.4 %pad_maximum_fusion.1 = bf16[3,3,3,4,8,16,128]{6,5,4,3,0,2,1:T(8,128)(2,1)S(1)} fusion(bf16[3,3,1,4,8,16,128]{6,5,4,3,0,2,1:T(8,128)(2,1)} %collective-permute-done.7, bf16[3,1,1,4,8,16,128]{6,5,4,3,0,2,1:T(8,128)(2,1)} %copy-done.12, bf16[3,1,1,4,8,16,128]{6,5,4,3,0,2,1:T(8,128)(2,1)} %bitcast.160, bf16[3,1,1,4,8,16,128]{6,5,4,3,0,2,1:T(8,128)(2,1)} %copy-done.11, ...), kind=kLoop, calls=%fused_computation.24 | loop fusion | flops 7077888 | bytes 7077888 | tf_op jit(solution)/shard_map/concatenate | solution.py:28
  84.7 2.7 %copy.8 = bf16[3,3,3,4,8,16,128]{6,5,4,3,2,1,0:T(8,128)(2,1)} copy(bf16[3,3,3,4,8,16,128]{6,5,4,3,0,2,1:T(8,128)(2,1)S(1)} %pad_maximum_fusion.1) | data formatting | bytes 7077888 | tf_op jit(solution)/shard_map/concatenate | solution.py:28
  87.5 4.9 %fusion.18 = f32[3,4608,128]{2,1,0:T(8,128)} fusion(bf16[3,256,128]{2,1,0:T(8,128)(2,1)S(1)} %bitcast.147, f32[3,4608,256]{2,1,0:T(8,128)S(1)} %get-tuple-element.24, f32[3,256]{1,0:T(4,128)S(1)} %log_add_fusion.1), kind=kOutput, calls=%fused_computation.32 | convolution fusion | flops 913047552 | bytes 21433344 | tf_op jit(solution)/shard_map/hqk,hqd->hkd/dot_general | solution.py:138
  92.3 9.3 %fusion.33 = f32[3,256]{1,0:T(4,128)S(1)} fusion(bf16[3,4608,128]{2,1,0:T(8,128)(2,1)} %bitcast.130, f32[3,4608,256]{2,1,0:T(8,128)} %copy-done, f32[3,256]{1,0:T(4,128)S(1)} %log_add_fusion.1, bf16[3,256,128]{2,1,0:T(8,128)(2,1)S(1)} %bitcast.148), kind=kOutput, calls=%fused_computation.47 | convolution fusion | flops 913341696 | bytes 17897472 | tf_op jit(solution)/shard_map/hqk,hkd->hqd/dot_general | solution.py:116
  101.7 8.3 %fusion.30 = f32[3,256]{1,0:T(4,128)S(1)} fusion(bf16[3,4608,128]{2,1,0:T(8,128)(2,1)S(1)} %bitcast.131, f32[3,4608,256]{2,1,0:T(8,128)} %get-tuple-element.22, f32[3,256]{1,0:T(4,128)S(1)} %log_add_fusion, bf16[3,256,128]{2,1,0:T(8,128)(2,1)S(1)} %bitcast.144), kind=kOutput, calls=%fused_computation.46 | convolution fusion | flops 913341696 | bytes 17897472 | tf_op jit(solution)/shard_map/hqk,hkd->hqd/dot_general | solution.py:116
  109.9 12.0 %convolution_add_fusion = f32[3,4608,128]{2,1,0:T(8,128)} fusion(f32[3,4608,128]{2,1,0:T(8,128)} %fusion.18, bf16[3,256,128]{2,1,0:T(8,128)(2,1)S(1)} %bitcast.145, f32[3,4608,256]{2,1,0:T(8,128)} %get-tuple-element.22, f32[3,256]{1,0:T(4,128)S(1)} %log_add_fusion), kind=kOutput, calls=%fused_computation.20 | convolution fusion | flops 914817024 | bytes 28511232 | tf_op jit(solution)/shard_map/hqk,hqd->hkd/dot_general | solution.py:138
  121.9 3.8 %slice_bitcast_fusion.3 = (bf16[3,3,4,8,16,128]{5,4,3,2,0,1:T(8,128)(2,1)}, bf16[3,3,4,8,16,128]{5,4,3,2,0,1:T(8,128)(2,1)S(1)}) fusion(f32[3,3,3,4,8,16,128]{6,5,4,3,2,1,0:T(8,128)} %bitcast.140), kind=kLoop, calls=%fused_computation.39 | loop fusion | bytes 4718592 | tf_op jit(solution)/shard_map/convert_element_type | solution.py:79
  125.7 3.4 %collective-permute-start.12 = (bf16[3,3,4,8,16,128]{5,4,3,2,0,1:T(8,128)(2,1)}, bf16[3,3,4,8,16,128]{5,4,3,2,0,1:T(8,128)(2,1)S(1)}, u32[]{:S(2)}, u32[]{:S(2)}) collective-permute-start(bf16[3,3,4,8,16,128]{5,4,3,2,0,1:T(8,128)(2,1)} %get-tuple-element.7), channel_id=1, source_target_pairs={{4,0},{8,4},{12,8},{5,1},{9,5},{13,9},{6,2},{10,6},{14,10},{7,3},{... | collective-permute-start | bytes 3538952 | tf_op jit(solution)/shard_map/ppermute | solution.py:12
  129.1 2.6 %collective-permute-start.13 = (bf16[3,3,4,8,16,128]{5,4,3,2,0,1:T(8,128)(2,1)S(1)}, bf16[3,3,4,8,16,128]{5,4,3,2,0,1:T(8,128)(2,1)}, u32[]{:S(2)}, u32[]{:S(2)}) collective-permute-start(bf16[3,3,4,8,16,128]{5,4,3,2,0,1:T(8,128)(2,1)S(1)} %get-tuple-element.8), channel_id=1, source_target_pairs={{0,4},{4,8},{8,12},{1,5},{5,9},{9,13},{2,6},{6,10},{10,14},{3,7},{... | collective-permute-start | bytes 3538952 | tf_op jit(solution)/shard_map/ppermute | solution.py:12
  131.7 8.6 %fusion.4 = bf16[3,256,4608]{1,2,0:T(8,128)(2,1)} fusion(f32[3,4608,256]{2,1,0:T(8,128)} %copy-done, bf16[3,4608,128]{2,1,0:T(8,128)(2,1)S(1)} %bitcast.132, bf16[3,256,128]{2,1,0:T(8,128)(2,1)S(1)} %bitcast.149, f32[3,256]{1,0:T(4,128)S(1)} %fusion.33, f32[3,256]{1,0:T(4,128)S(1)} %log_add_fusion.1), kind=kOutput, calls=%fused_computation.9 | convolution fusion | flops 920125440 | bytes 24975360 | tf_op jit(solution)/shard_map/hqd,hkd->hqk/dot_general | solution.py:118
  140.2 7.9 %fusion.48 = f32[3,4608,128]{2,1,0:T(8,128)} fusion(bf16[3,256,4608]{1,2,0:T(8,128)(2,1)} %fusion.4, bf16[3,256,128]{2,1,0:T(8,128)(2,1)S(1)} %bitcast.153), kind=kOutput, calls=%fused_computation.81 | convolution fusion | flops 905969664 | bytes 14352384 | tf_op jit(solution)/shard_map/hqk,hqd->hkd/dot_general | solution.py:135
  148.2 8.3 %fusion = bf16[3,256,4608]{1,2,0:T(8,128)(2,1)} fusion(f32[3,4608,256]{2,1,0:T(8,128)} %get-tuple-element.22, bf16[3,4608,128]{2,1,0:T(8,128)(2,1)S(1)} %bitcast.133, bf16[3,256,128]{2,1,0:T(8,128)(2,1)S(1)} %bitcast.146, f32[3,256]{1,0:T(4,128)S(1)} %fusion.30, f32[3,256]{1,0:T(4,128)S(1)} %log_add_fusion), kind=kOutput, calls=%fused_computation.1 | convolution fusion | flops 920125440 | bytes 24975360 | tf_op jit(solution)/shard_map/hqd,hkd->hqk/dot_general | solution.py:118
  156.5 7.2 %fusion.10 = f32[3,4608,128]{2,1,0:T(8,128)S(1)} fusion(f32[3,4608,128]{2,1,0:T(8,128)} %fusion.48, bf16[3,256,4608]{1,2,0:T(8,128)(2,1)} %fusion, bf16[3,256,128]{2,1,0:T(8,128)(2,1)S(1)} %bitcast.151), kind=kOutput, calls=%fused_computation.22 | convolution fusion | flops 909508608 | bytes 21430272 | tf_op jit(solution)/shard_map/hqk,hqd->hkd/dot_general | solution.py:135
  163.7 1.6 slice_bitcast_fusion.5
  165.3 2.4 %copy-done.5 = f32[3,4608,128]{2,1,0:T(8,128)} copy-done((f32[3,4608,128]{2,1,0:T(8,128)}, f32[3,4608,128]{2,1,0:T(8,128)S(1)}, u32[]{:S(2)}) %copy-start.5) | copy-done | bytes 7077912
  167.7 4.2 %collective-permute-start.8 = (bf16[3,3,4,8,16,128]{5,4,3,2,0,1:T(8,128)(2,1)}, bf16[3,3,4,8,16,128]{5,4,3,2,0,1:T(8,128)(2,1)S(1)}, u32[]{:S(2)}, u32[]{:S(2)}) collective-permute-start(bf16[3,3,4,8,16,128]{5,4,3,2,0,1:T(8,128)(2,1)} %get-tuple-element.9), channel_id=1, source_target_pairs={{4,0},{8,4},{12,8},{5,1},{9,5},{13,9},{6,2},{10,6},{14,10},{7,3},{... | collective-permute-start | bytes 3538952 | tf_op jit(solution)/shard_map/ppermute | solution.py:12
  171.9 2.6 %collective-permute-start.9 = (bf16[3,3,4,8,16,128]{5,4,3,2,0,1:T(8,128)(2,1)S(1)}, bf16[3,3,4,8,16,128]{5,4,3,2,0,1:T(8,128)(2,1)}, u32[]{:S(2)}, u32[]{:S(2)}) collective-permute-start(bf16[3,3,4,8,16,128]{5,4,3,2,0,1:T(8,128)(2,1)S(1)} %get-tuple-element.10), channel_id=1, source_target_pairs={{0,4},{4,8},{8,12},{1,5},{5,9},{9,13},{2,6},{6,10},{10,14},{3,7},{... | collective-permute-start | bytes 3538952 | tf_op jit(solution)/shard_map/ppermute | solution.py:12
  174.5 2.6 %fusion.28 = bf16[3,256,128]{2,1,0:T(8,128)(2,1)S(1)} fusion(bf16[3,256,4608]{1,2,0:T(8,128)(2,1)S(1)} %copy-done.4, bf16[3,4608,128]{2,1,0:T(8,128)(2,1)S(1)} %bitcast.136), kind=kOutput, calls=%fused_computation.44 | convolution fusion | flops 906166272 | bytes 10813440 | tf_op jit(solution)/shard_map/hqk,hkd->hqd/dot_general | solution.py:121
  177.2 2.6 %fusion.29 = bf16[3,256,128]{2,1,0:T(8,128)(2,1)S(1)} fusion(bf16[3,256,4608]{1,2,0:T(8,128)(2,1)S(1)} %bitcast.139, bf16[3,4608,128]{2,1,0:T(8,128)(2,1)S(1)} %bitcast.137), kind=kOutput, calls=%fused_computation.45 | convolution fusion | flops 906166272 | bytes 10813440 | tf_op jit(solution)/shard_map/hqk,hkd->hqd/dot_general | solution.py:121
  179.9 2.6 %fusion.42 = (bf16[3,3,4,8,16,128]{5,4,3,2,0,1:T(8,128)(2,1)S(1)}, f32[3,3,4,8,16,128]{5,4,3,2,0,1:T(8,128)S(1)}) fusion(bf16[3,3,4,8,16,128]{5,4,3,2,0,1:T(8,128)(2,1)} %collective-permute-done.13, bf16[3,3,4,8,16,128]{5,4,3,2,0,1:T(8,128)(2,1)S(1)} %collective-permute-done.12, f32[3,3,3,4,8,16,128]{6,5,4,3,2,1,0:T(8,128)} %bitcast.141), kind=kLoop, calls=%fused_computation.77 | loop fusion | flops 2949120 | bytes 8257536 | tf_op jit(solution)/shard_map/convert.1
  182.5 0.2 slice_bitcast_fusion.9
  182.7 6.8 %collective-permute-start.14 = (bf16[3,4,8,16,128]{4,3,2,1,0:T(8,128)(2,1)S(1)}, bf16[3,4,8,16,128]{4,3,2,1,0:T(8,128)(2,1)S(1)}, u32[]{:S(2)}, u32[]{:S(2)}) collective-permute-start(bf16[3,4,8,16,128]{4,3,2,1,0:T(8,128)(2,1)S(1)} %get-tuple-element.11), channel_id=1, source_target_pairs={{16,0},{32,16},{48,32},{64,48},{80,64},{96,80},{112,96},{17,1},{33... | collective-permute-start | bytes 1179656 | tf_op jit(solution)/shard_map/ppermute | solution.py:12
  189.5 1.9 collective-permute-start.15
  191.4 0.6 collective-permute-done.8
  192.0 4.2 %collective-permute-done.9 = bf16[3,3,4,8,16,128]{5,4,3,2,0,1:T(8,128)(2,1)} collective-permute-done((bf16[3,3,4,8,16,128]{5,4,3,2,0,1:T(8,128)(2,1)S(1)}, bf16[3,3,4,8,16,128]{5,4,3,2,0,1:T(8,128)(2,1)}, u32[]{:S(2)}, u32[]{:S(2)}) %collective-permute-start.9) | collective-permute-done | bytes 1179680 | tf_op jit(solution)/shard_map/ppermute | solution.py:12
  196.2 2.6 %fusion.44 = (bf16[3,3,4,8,16,128]{5,4,3,2,0,1:T(8,128)(2,1)S(1)}, f32[3,3,4,8,16,128]{5,4,3,2,0,1:T(8,128)S(1)}) fusion(bf16[3,3,4,8,16,128]{5,4,3,2,0,1:T(8,128)(2,1)} %collective-permute-done.9, bf16[3,3,4,8,16,128]{5,4,3,2,0,1:T(8,128)(2,1)S(1)} %collective-permute-done.8, f32[3,3,3,4,8,16,128]{6,5,4,3,2,1,0:T(8,128)} %bitcast.143), kind=kLoop, calls=%fused_computation.78 | loop fusion | flops 2949120 | bytes 8257536 | tf_op jit(solution)/shard_map/convert.5
  198.8 0.1 slice_bitcast_fusion.11
  198.9 6.6 %collective-permute-start.10 = (bf16[3,4,8,16,128]{4,3,2,1,0:T(8,128)(2,1)S(1)}, bf16[3,4,8,16,128]{4,3,2,1,0:T(8,128)(2,1)S(1)}, u32[]{:S(2)}, u32[]{:S(2)}) collective-permute-start(bf16[3,4,8,16,128]{4,3,2,1,0:T(8,128)(2,1)S(1)} %get-tuple-element.13), channel_id=1, source_target_pairs={{16,0},{32,16},{48,32},{64,48},{80,64},{96,80},{112,96},{17,1},{33... | collective-permute-start | bytes 1179656 | tf_op jit(solution)/shard_map/ppermute | solution.py:12
  205.5 1.9 collective-permute-start.11
  207.5 0.8 pad_maximum_fusion.4
  208.3 0.9 fusion.38
  209.2 1.6 collective-permute-done.10
  210.8 8.0 %collective-permute-done.11 = bf16[3,4,8,16,128]{4,3,2,1,0:T(8,128)(2,1)S(1)} collective-permute-done((bf16[3,4,8,16,128]{4,3,2,1,0:T(8,128)(2,1)S(1)}, bf16[3,4,8,16,128]{4,3,2,1,0:T(8,128)(2,1)S(1)}, u32[]{:S(2)}, u32[]{:S(2)}) %collective-permute-start.11) | collective-permute-done | bytes 393248 | tf_op jit(solution)/shard_map/ppermute | solution.py:12
  218.8 0.9 fusion.41
  (42 shorter events, 0.1 us)
Async XLA Ops:
  0.6 55.8 %copy-start.9 = (bf16[3,4,8,16,128]{4,3,2,1,0:T(8,128)(2,1)S(1)}, bf16[3,4,8,16,128]{4,3,2,1,0:T(8,128)(2,1)}, u32[]{:S(2)}) copy-start(bf16[3,4,8,16,128]{4,3,2,1,0:T(8,128)(2,1)} %param.5) | copy-start | bytes 1179652
  0.6 30.5 %copy-start.10 = (bf16[3,4,8,16,128]{4,3,2,1,0:T(8,128)(2,1)S(1)}, bf16[3,4,8,16,128]{4,3,2,1,0:T(8,128)(2,1)}, u32[]{:S(2)}) copy-start(bf16[3,4,8,16,128]{4,3,2,1,0:T(8,128)(2,1)} %param.6) | copy-start | bytes 1179652
  0.7 30.3 %copy-start.13 = (bf16[3,4,8,16,128]{4,3,2,1,0:T(8,128)(2,1)S(1)}, bf16[3,4,8,16,128]{4,3,2,1,0:T(8,128)(2,1)}, u32[]{:S(2)}) copy-start(bf16[3,4,8,16,128]{4,3,2,1,0:T(8,128)(2,1)} %param.7) | copy-start | bytes 1179652
  0.7 19.1 %collective-permute-start = (bf16[3,1,1,4,8,16,128]{6,5,4,3,0,2,1:T(8,128)(2,1)}, bf16[3,1,1,4,8,16,128]{6,5,4,3,0,2,1:T(8,128)(2,1)S(1)}, u32[]{:S(2)}, u32[]{:S(2)}) collective-permute-start(bf16[3,1,1,4,8,16,128]{6,5,4,3,0,2,1:T(8,128)(2,1)} %bitcast.154), channel_id=1, source_target_pairs={{0,16},{16,32},{32,48},{48,64},{64,80},{80,96},{96,112},{1,17},{17... | collective-permute-start | bytes 1179656 | tf_op jit(solution)/shard_map/ppermute | solution.py:26
  4.6 15.2 %collective-permute-start.1 = (bf16[3,1,1,4,8,16,128]{6,5,4,3,0,2,1:T(8,128)(2,1)}, bf16[3,1,1,4,8,16,128]{6,5,4,3,0,2,1:T(8,128)(2,1)S(1)}, u32[]{:S(2)}, u32[]{:S(2)}) collective-permute-start(bf16[3,1,1,4,8,16,128]{6,5,4,3,0,2,1:T(8,128)(2,1)} %bitcast.155), channel_id=1, source_target_pairs={{16,0},{32,16},{48,32},{64,48},{80,64},{96,80},{112,96},{17,1},{33... | collective-permute-start | bytes 1179656 | tf_op jit(solution)/shard_map/ppermute | solution.py:27
  10.3 20.8 %collective-permute-start.4 = (bf16[3,1,1,4,8,16,128]{6,5,4,3,0,2,1:T(8,128)(2,1)}, bf16[3,1,1,4,8,16,128]{6,5,4,3,0,2,1:T(8,128)(2,1)S(1)}, u32[]{:S(2)}, u32[]{:S(2)}) collective-permute-start(bf16[3,1,1,4,8,16,128]{6,5,4,3,0,2,1:T(8,128)(2,1)} %bitcast.158), channel_id=1, source_target_pairs={{0,16},{16,32},{32,48},{48,64},{64,80},{80,96},{96,112},{1,17},{17... | collective-permute-start | bytes 1179656 | tf_op jit(solution)/shard_map/ppermute | solution.py:26
  12.2 18.9 %collective-permute-start.5 = (bf16[3,1,1,4,8,16,128]{6,5,4,3,0,2,1:T(8,128)(2,1)}, bf16[3,1,1,4,8,16,128]{6,5,4,3,0,2,1:T(8,128)(2,1)S(1)}, u32[]{:S(2)}, u32[]{:S(2)}) collective-permute-start(bf16[3,1,1,4,8,16,128]{6,5,4,3,0,2,1:T(8,128)(2,1)} %bitcast.159), channel_id=1, source_target_pairs={{16,0},{32,16},{48,32},{64,48},{80,64},{96,80},{112,96},{17,1},{33... | collective-permute-start | bytes 1179656 | tf_op jit(solution)/shard_map/ppermute | solution.py:27
  21.9 31.1 %collective-permute-start.2 = (bf16[3,3,1,4,8,16,128]{6,5,4,3,0,2,1:T(8,128)(2,1)}, bf16[3,3,1,4,8,16,128]{6,5,4,3,0,2,1:T(8,128)(2,1)}, u32[]{:S(2)}, u32[]{:S(2)}) collective-permute-start(bf16[3,3,1,4,8,16,128]{6,5,4,3,0,2,1:T(8,128)(2,1)} %pad_maximum_fusion.2), channel_id=1, source_target_pairs={{0,4},{4,8},{8,12},{1,5},{5,9},{9,13},{2,6},{6,10},{10,14},{3,7},{... | collective-permute-start | bytes 3538952 | tf_op jit(solution)/shard_map/ppermute | solution.py:26
  25.3 31.1 %collective-permute-start.3 = (bf16[3,3,1,4,8,16,128]{6,5,4,3,0,2,1:T(8,128)(2,1)}, bf16[3,3,1,4,8,16,128]{6,5,4,3,0,2,1:T(8,128)(2,1)}, u32[]{:S(2)}, u32[]{:S(2)}) collective-permute-start(bf16[3,3,1,4,8,16,128]{6,5,4,3,0,2,1:T(8,128)(2,1)} %pad_maximum_fusion.2), channel_id=1, source_target_pairs={{4,0},{8,4},{12,8},{5,1},{9,5},{13,9},{6,2},{10,6},{14,10},{7,3},{... | collective-permute-start | bytes 3538952 | tf_op jit(solution)/shard_map/ppermute | solution.py:27
  31.0 28.6 %copy-start.7 = (bf16[3,4,8,8,128]{4,3,2,1,0:T(8,128)(2,1)}, bf16[3,4,8,8,128]{4,3,2,1,0:T(8,128)(2,1)S(1)}, u32[]{:S(2)}) copy-start(bf16[3,4,8,8,128]{4,3,2,1,0:T(8,128)(2,1)S(1)} %get-tuple-element.17) | copy-start | bytes 589828
  31.1 27.2 %copy-start.11 = (bf16[3,1,1,4,8,16,128]{6,5,4,3,0,2,1:T(8,128)(2,1)}, bf16[3,1,1,4,8,16,128]{6,5,4,3,0,2,1:T(8,128)(2,1)S(1)}, u32[]{:S(2)}) copy-start(bf16[3,1,1,4,8,16,128]{6,5,4,3,0,2,1:T(8,128)(2,1)S(1)} %collective-permute-done.4) | copy-start | bytes 1179652
  31.1 27.2 %copy-start.12 = (bf16[3,1,1,4,8,16,128]{6,5,4,3,0,2,1:T(8,128)(2,1)}, bf16[3,1,1,4,8,16,128]{6,5,4,3,0,2,1:T(8,128)(2,1)S(1)}, u32[]{:S(2)}) copy-start(bf16[3,1,1,4,8,16,128]{6,5,4,3,0,2,1:T(8,128)(2,1)S(1)} %collective-permute-done.5) | copy-start | bytes 1179652
  32.4 49.9 %collective-permute-start.6 = (bf16[3,3,1,4,8,16,128]{6,5,4,3,0,2,1:T(8,128)(2,1)}, bf16[3,3,1,4,8,16,128]{6,5,4,3,0,2,1:T(8,128)(2,1)}, u32[]{:S(2)}, u32[]{:S(2)}) collective-permute-start(bf16[3,3,1,4,8,16,128]{6,5,4,3,0,2,1:T(8,128)(2,1)} %pad_maximum_fusion.3), channel_id=1, source_target_pairs={{0,4},{4,8},{8,12},{1,5},{5,9},{9,13},{2,6},{6,10},{10,14},{3,7},{... | collective-permute-start | bytes 3538952 | tf_op jit(solution)/shard_map/ppermute | solution.py:26
  34.8 47.5 %collective-permute-start.7 = (bf16[3,3,1,4,8,16,128]{6,5,4,3,0,2,1:T(8,128)(2,1)}, bf16[3,3,1,4,8,16,128]{6,5,4,3,0,2,1:T(8,128)(2,1)}, u32[]{:S(2)}, u32[]{:S(2)}) collective-permute-start(bf16[3,3,1,4,8,16,128]{6,5,4,3,0,2,1:T(8,128)(2,1)} %pad_maximum_fusion.3), channel_id=1, source_target_pairs={{4,0},{8,4},{12,8},{5,1},{9,5},{13,9},{6,2},{10,6},{14,10},{7,3},{... | collective-permute-start | bytes 3538952 | tf_op jit(solution)/shard_map/ppermute | solution.py:27
  59.5 4.3 %copy-start.2 = (bf16[3,3,3,4,8,16,128]{6,5,4,3,2,1,0:T(8,128)(2,1)}, bf16[3,3,3,4,8,16,128]{6,5,4,3,2,1,0:T(8,128)(2,1)S(1)}, u32[]{:S(2)}) copy-start(bf16[3,3,3,4,8,16,128]{6,5,4,3,2,1,0:T(8,128)(2,1)S(1)} %copy.7) | copy-start | bytes 10616836
  63.9 23.6 %copy-start = (f32[3,4608,256]{2,1,0:T(8,128)}, f32[3,4608,256]{2,1,0:T(8,128)S(1)}, u32[]{:S(2)}) copy-start(f32[3,4608,256]{2,1,0:T(8,128)S(1)} %get-tuple-element.24) | copy-start | bytes 42467332
  92.3 9.3 %copy-start.1 = (bf16[3,3,3,4,8,16,128]{6,5,4,3,2,1,0:T(8,128)(2,1)S(1)}, bf16[3,3,3,4,8,16,128]{6,5,4,3,2,1,0:T(8,128)(2,1)}, u32[]{:S(2)}) copy-start(bf16[3,3,3,4,8,16,128]{6,5,4,3,2,1,0:T(8,128)(2,1)} %copy.8) | copy-start | bytes 10616836
  125.7 54.2 %collective-permute-start.12 = (bf16[3,3,4,8,16,128]{5,4,3,2,0,1:T(8,128)(2,1)}, bf16[3,3,4,8,16,128]{5,4,3,2,0,1:T(8,128)(2,1)S(1)}, u32[]{:S(2)}, u32[]{:S(2)}) collective-permute-start(bf16[3,3,4,8,16,128]{5,4,3,2,0,1:T(8,128)(2,1)} %get-tuple-element.7), channel_id=1, source_target_pairs={{4,0},{8,4},{12,8},{5,1},{9,5},{13,9},{6,2},{10,6},{14,10},{7,3},{... | collective-permute-start | bytes 3538952 | tf_op jit(solution)/shard_map/ppermute | solution.py:12
  129.1 11.1 %copy-start.8 = (bf16[3,4,8,8,128]{4,3,2,1,0:T(8,128)(2,1)S(1)}, bf16[3,4,8,8,128]{4,3,2,1,0:T(8,128)(2,1)}, u32[]{:S(2)}) copy-start(bf16[3,4,8,8,128]{4,3,2,1,0:T(8,128)(2,1)} %copy-done.7) | copy-start | bytes 589828
  129.1 50.8 %collective-permute-start.13 = (bf16[3,3,4,8,16,128]{5,4,3,2,0,1:T(8,128)(2,1)S(1)}, bf16[3,3,4,8,16,128]{5,4,3,2,0,1:T(8,128)(2,1)}, u32[]{:S(2)}, u32[]{:S(2)}) collective-permute-start(bf16[3,3,4,8,16,128]{5,4,3,2,0,1:T(8,128)(2,1)S(1)} %get-tuple-element.8), channel_id=1, source_target_pairs={{0,4},{4,8},{8,12},{1,5},{5,9},{9,13},{2,6},{6,10},{10,14},{3,7},{... | collective-permute-start | bytes 3538952 | tf_op jit(solution)/shard_map/ppermute | solution.py:12
  148.2 8.4 %copy-start.6 = (bf16[3,4,8,8,128]{4,3,2,1,0:T(8,128)(2,1)S(1)}, bf16[3,4,8,8,128]{4,3,2,1,0:T(8,128)(2,1)}, u32[]{:S(2)}) copy-start(bf16[3,4,8,8,128]{4,3,2,1,0:T(8,128)(2,1)} %get-tuple-element.18) | copy-start | bytes 589828
  156.5 18.0 %copy-start.4 = (bf16[3,256,4608]{1,2,0:T(8,128)(2,1)S(1)}, bf16[3,256,4608]{1,2,0:T(8,128)(2,1)}, u32[]{:S(2)}) copy-start(bf16[3,256,4608]{1,2,0:T(8,128)(2,1)} %fusion.4) | copy-start | bytes 21233668
  163.7 4.0 %copy-start.5 = (f32[3,4608,128]{2,1,0:T(8,128)}, f32[3,4608,128]{2,1,0:T(8,128)S(1)}, u32[]{:S(2)}) copy-start(f32[3,4608,128]{2,1,0:T(8,128)S(1)} %fusion.10) | copy-start | bytes 21233668
  163.7 10.8 %copy-start.3 = (bf16[3,3,3,4,8,16,128]{6,5,4,3,2,1,0:T(8,128)(2,1)S(1)}, bf16[3,3,3,4,8,16,128]{6,5,4,3,2,1,0:T(8,128)(2,1)}, u32[]{:S(2)}) copy-start(bf16[3,3,3,4,8,16,128]{6,5,4,3,2,1,0:T(8,128)(2,1)} %copy-done.2) | copy-start | bytes 10616836
  167.7 24.3 %collective-permute-start.8 = (bf16[3,3,4,8,16,128]{5,4,3,2,0,1:T(8,128)(2,1)}, bf16[3,3,4,8,16,128]{5,4,3,2,0,1:T(8,128)(2,1)S(1)}, u32[]{:S(2)}, u32[]{:S(2)}) collective-permute-start(bf16[3,3,4,8,16,128]{5,4,3,2,0,1:T(8,128)(2,1)} %get-tuple-element.9), channel_id=1, source_target_pairs={{4,0},{8,4},{12,8},{5,1},{9,5},{13,9},{6,2},{10,6},{14,10},{7,3},{... | collective-permute-start | bytes 3538952 | tf_op jit(solution)/shard_map/ppermute | solution.py:12
  171.9 5.3 %slice-start = ((s8[7077888]{0:T(1024)(128)(4,1)}), s8[4194304]{0:T(1024)(128)(4,1)S(1)}, s32[]{:S(2)}) async-start(s8[7077888]{0:T(1024)(128)(4,1)} %bitcast.138), calls=%async_computation | async-start | bytes 8388608
  171.9 5.3 %slice-start.1 = ((s8[7077888]{0:T(1024)(128)(4,1)}), s8[2883584]{0:T(1024)(128)(4,1)S(1)}, s32[]{:S(2)}) async-start(s8[7077888]{0:T(1024)(128)(4,1)} %bitcast.138), calls=%async_computation.1 | async-start | bytes 5767168
  171.9 24.2 %collective-permute-start.9 = (bf16[3,3,4,8,16,128]{5,4,3,2,0,1:T(8,128)(2,1)S(1)}, bf16[3,3,4,8,16,128]{5,4,3,2,0,1:T(8,128)(2,1)}, u32[]{:S(2)}, u32[]{:S(2)}) collective-permute-start(bf16[3,3,4,8,16,128]{5,4,3,2,0,1:T(8,128)(2,1)S(1)} %get-tuple-element.10), channel_id=1, source_target_pairs={{0,4},{4,8},{8,12},{1,5},{5,9},{9,13},{2,6},{6,10},{10,14},{3,7},{... | collective-permute-start | bytes 3538952 | tf_op jit(solution)/shard_map/ppermute | solution.py:12
  182.7 25.6 %collective-permute-start.14 = (bf16[3,4,8,16,128]{4,3,2,1,0:T(8,128)(2,1)S(1)}, bf16[3,4,8,16,128]{4,3,2,1,0:T(8,128)(2,1)S(1)}, u32[]{:S(2)}, u32[]{:S(2)}) collective-permute-start(bf16[3,4,8,16,128]{4,3,2,1,0:T(8,128)(2,1)S(1)} %get-tuple-element.11), channel_id=1, source_target_pairs={{16,0},{32,16},{48,32},{64,48},{80,64},{96,80},{112,96},{17,1},{33... | collective-permute-start | bytes 1179656 | tf_op jit(solution)/shard_map/ppermute | solution.py:12
  189.5 18.8 %collective-permute-start.15 = (bf16[3,4,8,16,128]{4,3,2,1,0:T(8,128)(2,1)S(1)}, bf16[3,4,8,16,128]{4,3,2,1,0:T(8,128)(2,1)S(1)}, u32[]{:S(2)}, u32[]{:S(2)}) collective-permute-start(bf16[3,4,8,16,128]{4,3,2,1,0:T(8,128)(2,1)S(1)} %get-tuple-element.12), channel_id=1, source_target_pairs={{0,16},{16,32},{32,48},{48,64},{64,80},{80,96},{96,112},{1,17},{17... | collective-permute-start | bytes 1179656 | tf_op jit(solution)/shard_map/ppermute | solution.py:12
  198.9 11.9 %collective-permute-start.10 = (bf16[3,4,8,16,128]{4,3,2,1,0:T(8,128)(2,1)S(1)}, bf16[3,4,8,16,128]{4,3,2,1,0:T(8,128)(2,1)S(1)}, u32[]{:S(2)}, u32[]{:S(2)}) collective-permute-start(bf16[3,4,8,16,128]{4,3,2,1,0:T(8,128)(2,1)S(1)} %get-tuple-element.13), channel_id=1, source_target_pairs={{16,0},{32,16},{48,32},{64,48},{80,64},{96,80},{112,96},{17,1},{33... | collective-permute-start | bytes 1179656 | tf_op jit(solution)/shard_map/ppermute | solution.py:12
  205.5 13.3 %collective-permute-start.11 = (bf16[3,4,8,16,128]{4,3,2,1,0:T(8,128)(2,1)S(1)}, bf16[3,4,8,16,128]{4,3,2,1,0:T(8,128)(2,1)S(1)}, u32[]{:S(2)}, u32[]{:S(2)}) collective-permute-start(bf16[3,4,8,16,128]{4,3,2,1,0:T(8,128)(2,1)S(1)} %get-tuple-element.14), channel_id=1, source_target_pairs={{0,16},{16,32},{32,48},{48,64},{64,80},{80,96},{96,112},{1,17},{17... | collective-permute-start | bytes 1179656 | tf_op jit(solution)/shard_map/ppermute | solution.py:12
where the time goes:
time: 220 us
  matrix products  85.6 us (39%)
  starting transfers between devices  62.7 us (28%)
  waiting for transfers between devices  31.6 us (14%)
  other arithmetic  24.4 us (11%)
  local copies, waits for them, and re-layouts  14.3 us (6%)
    ppermute x8, starting transfers between devices, shifted(): return lax.ppermute(block, axis, route)  30 us
    ppermute x4, starting transfers between devices, extended(): after = lax.ppermute(first, axis, down)  21 us
    dot_general x2, matrix products, query_step(): jnp.einsum('hqk,hkd->hqd', weight_bf, v_span, preferred_element_type=jnp....  17.6 us
    dot_general x2, matrix products, query_step(): jnp.einsum('hqd,hkd->hqk', g_rows, v_span, preferred_element_type=jnp.flo...  16.9 us
    dot_general x2, matrix products, query_step(): jnp.einsum('hqk,hqd->hkd', weight_bf, g_rows, preferred_element_type=jnp....  16.8 us
    dot_general x2, matrix products, query_step(): jnp.einsum('hqk,hqd->hkd', d_scores, q_rows, preferred_element_type=jnp.f...  15.1 us
    ppermute x8, waiting for transfers between devices, shifted(): return lax.ppermute(block, axis, route)  14.4 us
    dot_general x2, matrix products, scores_of(): jnp.einsum('hqd,hkd->hqk', left_rows, right_rows, preferred_element_type=...  14 us
  transfers between devices with their start and end apart: 16, of which 6 were waited for; matrix products, arithmetic and copies ran while one was open for 35% of the time, Pallas kernels for 0%

commit v1 on v0

v1 whole, which is shorter than its diff:
```python
import functools
import math

import jax
import jax.numpy as jnp
from jax import lax
from jax.experimental import pallas as pl
from jax.experimental.pallas import tpu as pltpu
from jax.sharding import PartitionSpec as P

EDGES = ((0, 1), (0, -1), (1, 0), (-1, 0))
CORNERS = ((1, 1), (-1, -1), (1, -1), (-1, 1))
AROUND = EDGES + CORNERS
KEY_CHUNK = 256


def contract(a, b, dim_a, dim_b):
    return lax.dot_general(
        a, b, (((dim_a,), (dim_b,)), ((), ())), preferred_element_type=jnp.float32
    )


def stats_kernel(count, first, factor, live, *refs):
    q_ref, g_ref = refs[:2]
    kv_refs = refs[2 : 2 + count]
    out_ref = refs[-1]
    if first:
        shape = out_ref.shape[2:]
        out_ref[0, 0] = jnp.full(shape, -jnp.inf, jnp.float32)
        out_ref[0, 1] = jnp.zeros(shape, jnp.float32)
        out_ref[0, 2] = jnp.zeros(shape, jnp.float32)
    else:
        out_ref[...] = refs[2 + count][...]

    for slot, kv_ref in enumerate(kv_refs):

        def one(kv_ref=kv_ref):
            q = q_ref[0]
            g = g_ref[0]
            top, total, dot = out_ref[0, 0], out_ref[0, 1], out_ref[0, 2]
            keys = kv_ref.shape[2]
            for start in range(0, keys, KEY_CHUNK):
                k = kv_ref[0, 0, start : start + KEY_CHUNK]
                v = kv_ref[1, 0, start : start + KEY_CHUNK]
                s = contract(k, q, 1, 1)
                dp = contract(v, g, 1, 1)
                new = jnp.maximum(top, jnp.max(s, axis=0, keepdims=True))
                keep = jnp.exp2((top - new) * factor)
                e = jnp.exp2((s - new) * factor)
                total = total * keep + jnp.sum(e, axis=0, keepdims=True)
                dot = dot * keep + jnp.sum(e * dp, axis=0, keepdims=True)
                top = new
            out_ref[0, 0] = top
            out_ref[0, 1] = total
            out_ref[0, 2] = dot

        if first:
            one()
        else:
            pl.when(live[slot] > 0)(one)


def grads_kernel(count, own, first, factor, scale, live, *refs):
    q_ref, g_ref, st_ref = refs[:3]
    kv_refs = refs[3 : 3 + count]
    rest = refs[3 + count :]
    if first:
        acc_in, outs = None, rest
    else:
        acc_in, outs = rest[0], rest[1:]
    acc_ref = outs[-1]
    if first:
        acc_ref[...] = jnp.zeros_like(acc_ref)
    else:
        acc_ref[...] = acc_in[...]

    for slot, kv_ref in enumerate(kv_refs):

        def one(kv_ref=kv_ref, out_ref=outs[slot]):
            q = q_ref[0]
            g = g_ref[0]
            top, total, dot = st_ref[0, 0], st_ref[0, 1], st_ref[0, 2]
            log_total = top * factor + jnp.log2(total)
            delta = dot / total
            keys = kv_ref.shape[2]
            acc = acc_ref[0]
            for start in range(0, keys, KEY_CHUNK):
                rows = slice(start, start + KEY_CHUNK)
                k = kv_ref[0, 0, rows]
                v = kv_ref[1, 0, rows]
                s = contract(k, q, 1, 1)
                dp = contract(v, g, 1, 1)
                p = jnp.exp2(s * factor - log_total)
                ds = (p * (dp - delta)).astype(jnp.bfloat16)
                dv = contract(p.astype(jnp.bfloat16), g, 1, 0)
                dk = contract(ds, q, 1, 0) * scale
                acc = acc + contract(k, ds, 0, 0)
                out_ref[0, 0, rows] = dk.astype(out_ref.dtype)
                out_ref[1, 0, rows] = dv.astype(out_ref.dtype)
            acc_ref[0] = acc

        if own:
            one()
        else:
            pl.when(live[slot] > 0)(one)

    if own:
        dq_ref = outs[count]
        dq_ref[0] = (acc_ref[0] * scale).T.astype(dq_ref.dtype)


def per_head(shape, head_dim=0):
    block = tuple(1 if i == head_dim else n for i, n in enumerate(shape))
    return pl.BlockSpec(
        block, lambda h, *_: tuple(h if i == head_dim else 0 for i in range(len(shape)))
    )


def run_stats(live, q, g, blocks, stats, factor):
    heads, rows, depth = q.shape
    first = stats is None
    count = len(blocks)
    stat_shape = (heads, 3, 1, rows)
    args = [q, g, *blocks] + ([] if first else [stats])
    keys = blocks[0].shape[2]
    return pl.pallas_call(
        functools.partial(stats_kernel, count, first, factor),
        out_shape=jax.ShapeDtypeStruct(stat_shape, jnp.float32),
        grid_spec=pltpu.PrefetchScalarGridSpec(
            num_scalar_prefetch=1,
            grid=(heads,),
            in_specs=[per_head(a.shape) for a in (q, g)]
            + [per_head(b.shape, 1) for b in blocks]
            + ([] if first else [per_head(stat_shape)]),
            out_specs=per_head(stat_shape),
        ),
        cost_estimate=pl.CostEstimate(
            flops=4 * count * heads * rows * keys * depth,
            bytes_accessed=(2 + 2 * count) * heads * rows * depth * 2,
            transcendentals=count * heads * rows * keys,
        ),
        name="stats",
    )(live, *args)


def run_grads(live, q, g, stats, blocks, acc, factor, scale, own=False):
    heads, rows, depth = q.shape
    first = acc is None
    count = len(blocks)
    acc_shape = (heads, depth, rows)
    args = [q, g, stats, *blocks] + ([] if first else [acc])
    part = jnp.float32 if own else jnp.bfloat16
    keys = blocks[0].shape[2]
    out_shape = [jax.ShapeDtypeStruct(b.shape, part) for b in blocks]
    out_specs = [per_head(b.shape, 1) for b in blocks]
    if own:
        out_shape.append(jax.ShapeDtypeStruct(q.shape, jnp.bfloat16))
        out_specs.append(per_head(q.shape))
    out_shape.append(jax.ShapeDtypeStruct(acc_shape, jnp.float32))
    out_specs.append(per_head(acc_shape))
    return pl.pallas_call(
        functools.partial(grads_kernel, count, own, first, factor, scale),
        out_shape=out_shape,
        grid_spec=pltpu.PrefetchScalarGridSpec(
            num_scalar_prefetch=1,
            grid=(heads,),
            in_specs=[per_head(a.shape) for a in (q, g, stats)]
            + [per_head(b.shape, 1) for b in blocks]
            + ([] if first else [per_head(acc_shape)]),
            out_specs=out_specs,
        ),
        cost_estimate=pl.CostEstimate(
            flops=10 * count * heads * rows * keys * depth,
            bytes_accessed=(2 + 4 * count) * heads * rows * depth * 2,
            transcendentals=count * heads * rows * keys,
        ),
        name="grads",
    )(live, *args)


def moved(x, step, sizes):
    frames, rows = sizes
    route = []
    for f in range(frames):
        for r in range(rows):
            to_f, to_r = f + step[0], r + step[1]
            if 0 <= to_f < frames and 0 <= to_r < rows:
                route.append((f * rows + r, to_f * rows + to_r))
    return lax.ppermute(x, ("tm", "height"), route)


def local(query_in, key_in, value_in, out_grad):
    shape = query_in.shape
    heads, depth = shape[0], shape[-1]
    flat = (heads, math.prod(shape[1:4]), depth)
    scale = depth**-0.5
    factor = scale * math.log2(math.e)
    q, g = query_in.reshape(flat), out_grad.reshape(flat)
    kv = jnp.stack([key_in.reshape(flat), value_in.reshape(flat)])
    sizes = (lax.axis_size("tm"), lax.axis_size("height"))
    at = (lax.axis_index("tm"), lax.axis_index("height"))

    def lives(steps):
        flags = [
            (at[0] + f >= 0) & (at[0] + f < sizes[0]) & (at[1] + r >= 0) & (at[1] + r < sizes[1])
            for f, r in steps
        ]
        return jnp.stack(flags).astype(jnp.int32)

    near = {step: moved(kv, (-step[0], -step[1]), sizes) for step in AROUND}
    one = jnp.ones((1,), jnp.int32)
    stats = run_stats(one, q, g, [kv], None, factor)
    stats = run_stats(lives(EDGES), q, g, [near[s] for s in EDGES], stats, factor)
    stats = run_stats(lives(CORNERS), q, g, [near[s] for s in CORNERS], stats, factor)

    acc = None
    back = []
    for steps in (CORNERS[:2], CORNERS[2:], EDGES[:2], EDGES[2:]):
        *parts, acc = run_grads(
            lives(steps), q, g, stats, [near[s] for s in steps], acc, factor, scale
        )
        back += [moved(part, step, sizes) for part, step in zip(parts, steps)]
    total, dq, _ = run_grads(one, q, g, stats, [kv], acc, factor, scale, own=True)
    for part in back:
        total = total + part.astype(jnp.float32)
    total = total.astype(jnp.bfloat16)
    return dq.reshape(shape), total[0].reshape(shape), total[1].reshape(shape)


def solution(mesh):
    spec = P("head", "tm", "height", None, None)
    return jax.shard_map(
        local, mesh=mesh, in_specs=(spec,) * 4, out_specs=(spec,) * 3, check_vma=False
    )
```

time: 220 us -> 181 us (0.82)
  the two profiles are of different devices: /device:TPU:18 before, /device:TPU:98 now
where the time goes in v1:
time: 181 us; the launch traced here: 180 us
  waiting for transfers between devices  58 us (32%)
  Pallas kernels  57.4 us (32%)
  starting transfers between devices  54.3 us (30%)
  other arithmetic  7.96 us (4%)
    ppermute x16, waiting for transfers between devices, moved(): return lax.ppermute(x, ('tm', 'height'), route)  58 us
    ppermute x16, starting transfers between devices, moved(): return lax.ppermute(x, ('tm', 'height'), route)  54.3 us
    pallas_call x5, Pallas kernels, run_grads(): pl.pallas_call(functools.partial(grads_kernel, count, own, first, factor,...  36 us
    pallas_call x3, Pallas kernels, run_stats(): pl.pallas_call(functools.partial(stats_kernel, count, first, factor), out...  21.5 us
  transfers between devices with their start and end apart: 16, of which 9 were waited for; matrix products, arithmetic and copies ran while one was open for 2% of the time, Pallas kernels for 10%

profile of v1, /device:TPU:98, one launch (start us, length us, event | category | flops | bytes accessed | tf_op | source)
XLA Modules:
  0.0 179.5 jit_solution(13057335867049711094)
XLA Ops:
  0.6 1.2 pad_maximum_fusion.refs_2_.refs_3_
  1.8 0.0 copy-start
  1.8 3.7 %collective-permute-start.7 = (bf16[2,3,512,128]{3,2,1,0:T(8,128)(2,1)S(1)}, bf16[2,3,512,128]{3,2,1,0:T(8,128)(2,1)S(1)}, u32[]{:S(2)}, u32[]{:S(2)}) collective-permute-start(bf16[2,3,512,128]{3,2,1,0:T(8,128)(2,1)S(1)} %pad_maximum_fusion.refs_2_.refs_3_), channel_id=1, source_target_pairs={{0,16},{4,20},{8,24},{12,28},{16,32},{20,36},{24,40},{28,44},{32,4... | collective-permute-start | bytes 2359304 | tf_op jit(solution)/shard_map/ppermute | solution.py:189
  5.6 2.1 %collective-permute-start.6 = (bf16[2,3,512,128]{3,2,1,0:T(8,128)(2,1)S(1)}, bf16[2,3,512,128]{3,2,1,0:T(8,128)(2,1)S(1)}, u32[]{:S(2)}, u32[]{:S(2)}) collective-permute-start(bf16[2,3,512,128]{3,2,1,0:T(8,128)(2,1)S(1)} %pad_maximum_fusion.refs_2_.refs_3_), channel_id=1, source_target_pairs={{16,0},{20,4},{24,8},{28,12},{32,16},{36,20},{40,24},{44,28},{48,3... | collective-permute-start | bytes 2359304 | tf_op jit(solution)/shard_map/ppermute | solution.py:189
  7.7 3.4 %collective-permute-start.5 = (bf16[2,3,512,128]{3,2,1,0:T(8,128)(2,1)S(1)}, bf16[2,3,512,128]{3,2,1,0:T(8,128)(2,1)S(1)}, u32[]{:S(2)}, u32[]{:S(2)}) collective-permute-start(bf16[2,3,512,128]{3,2,1,0:T(8,128)(2,1)S(1)} %pad_maximum_fusion.refs_2_.refs_3_), channel_id=1, source_target_pairs={{0,4},{4,8},{8,12},{16,20},{20,24},{24,28},{32,36},{36,40},{40,44}... | collective-permute-start | bytes 2359304 | tf_op jit(solution)/shard_map/ppermute | solution.py:189
  11.1 2.5 %collective-permute-start.4 = (bf16[2,3,512,128]{3,2,1,0:T(8,128)(2,1)S(1)}, bf16[2,3,512,128]{3,2,1,0:T(8,128)(2,1)}, u32[]{:S(2)}, u32[]{:S(2)}) collective-permute-start(bf16[2,3,512,128]{3,2,1,0:T(8,128)(2,1)S(1)} %pad_maximum_fusion.refs_2_.refs_3_), channel_id=1, source_target_pairs={{4,0},{8,4},{12,8},{20,16},{24,20},{28,24},{36,32},{40,36},{44,40}... | collective-permute-start | bytes 2359304 | tf_op jit(solution)/shard_map/ppermute | solution.py:189
  13.6 6.2 %collective-permute-start.3 = (bf16[2,3,512,128]{3,2,1,0:T(8,128)(2,1)S(1)}, bf16[2,3,512,128]{3,2,1,0:T(8,128)(2,1)}, u32[]{:S(2)}, u32[]{:S(2)}) collective-permute-start(bf16[2,3,512,128]{3,2,1,0:T(8,128)(2,1)S(1)} %pad_maximum_fusion.refs_2_.refs_3_), channel_id=1, source_target_pairs={{4,16},{8,20},{12,24},{20,32},{24,36},{28,40},{36,48},{40,52},{44,... | collective-permute-start | bytes 2359304 | tf_op jit(solution)/shard_map/ppermute | solution.py:189
  19.8 3.2 %collective-permute-done.7.refs_5_.refs_4_ = bf16[2,3,512,128]{3,2,1,0:T(8,128)(2,1)S(1)} collective-permute-done((bf16[2,3,512,128]{3,2,1,0:T(8,128)(2,1)S(1)}, bf16[2,3,512,128]{3,2,1,0:T(8,128)(2,1)S(1)}, u32[]{:S(2)}, u32[]{:S(2)}) %collective-permute-start.7) | collective-permute-done | bytes 786464 | tf_op jit(solution)/shard_map/ppermute | solution.py:189
  23.0 0.0 copy-start.1
  23.0 3.2 %collective-permute-start.2 = (bf16[2,3,512,128]{3,2,1,0:T(8,128)(2,1)S(1)}, bf16[2,3,512,128]{3,2,1,0:T(8,128)(2,1)}, u32[]{:S(2)}, u32[]{:S(2)}) collective-permute-start(bf16[2,3,512,128]{3,2,1,0:T(8,128)(2,1)S(1)} %pad_maximum_fusion.refs_2_.refs_3_), channel_id=1, source_target_pairs={{16,4},{20,8},{24,12},{32,20},{36,24},{40,28},{48,36},{52,40},{56,... | collective-permute-start | bytes 2359304 | tf_op jit(solution)/shard_map/ppermute | solution.py:189
  26.2 3.8 %collective-permute-done.6.refs_4_.refs_3_ = bf16[2,3,512,128]{3,2,1,0:T(8,128)(2,1)S(1)} collective-permute-done((bf16[2,3,512,128]{3,2,1,0:T(8,128)(2,1)S(1)}, bf16[2,3,512,128]{3,2,1,0:T(8,128)(2,1)S(1)}, u32[]{:S(2)}, u32[]{:S(2)}) %collective-permute-start.6) | collective-permute-done | bytes 786464 | tf_op jit(solution)/shard_map/ppermute | solution.py:189
  30.1 0.0 copy-start.2
  30.1 4.0 %collective-permute-start.1 = (bf16[2,3,512,128]{3,2,1,0:T(8,128)(2,1)S(1)}, bf16[2,3,512,128]{3,2,1,0:T(8,128)(2,1)}, u32[]{:S(2)}, u32[]{:S(2)}) collective-permute-start(bf16[2,3,512,128]{3,2,1,0:T(8,128)(2,1)S(1)} %pad_maximum_fusion.refs_2_.refs_3_), channel_id=1, source_target_pairs={{0,20},{4,24},{8,28},{16,36},{20,40},{24,44},{32,52},{36,56},{40,6... | collective-permute-start | bytes 2359304 | tf_op jit(solution)/shard_map/ppermute | solution.py:189
  34.1 0.0 collective-permute-done.5.refs_3_.refs_4_
  34.1 0.0 copy-start.3
  34.1 3.6 %collective-permute-start = (bf16[2,3,512,128]{3,2,1,0:T(8,128)(2,1)S(1)}, bf16[2,3,512,128]{3,2,1,0:T(8,128)(2,1)}, u32[]{:S(2)}, u32[]{:S(2)}) collective-permute-start(bf16[2,3,512,128]{3,2,1,0:T(8,128)(2,1)S(1)} %pad_maximum_fusion.refs_2_.refs_3_), channel_id=1, source_target_pairs={{20,0},{24,4},{28,8},{36,16},{40,20},{44,24},{52,32},{56,36},{60,4... | collective-permute-start | bytes 2359304 | tf_op jit(solution)/shard_map/ppermute | solution.py:189
  37.7 0.6 add_convert_fusion.6.live
  38.3 0.0 copy-done
  38.3 4.0 %stats.3.refs_6_ = f32[3,3,1,512]{3,2,1,0:T(1,128)} custom-call(s32[1]{0:T(128)} %constant.4.clone.1.live, bf16[3,512,128]{2,1,0:T(8,128)(2,1)} %bitcast.17, bf16[3,512,128]{2,1,0:T(8,128)(2,1)} %bitcast.25, bf16[2,3,512,128]{3,2,1,0:T(8,128)(2,1)} %copy-done), custom_call_target="tpu_custom_call" | custom-call | flops 402653184 | bytes 1572864 | tf_op jit(solution)/shard_map/stats/pallas_call | solution.py:126
  42.3 0.6 add_convert_fusion.1.live
  42.9 0.6 add_convert_fusion.5.live
  43.4 0.7 add_convert_fusion.3.live
  44.1 0.6 add_convert_fusion.2.live
  44.7 0.6 add_convert_fusion.4.live
  45.2 0.0 collective-permute-done.4.refs_2_.refs_3_
  45.2 0.0 copy-done.1
  45.2 0.0 copy-done.2
  45.2 0.0 copy-done.3
  45.3 8.8 %stats.4.refs_6_ = f32[3,3,1,512]{3,2,1,0:T(1,128)} custom-call(s32[4]{0:T(128)} %add_convert_fusion.2.live, bf16[3,512,128]{2,1,0:T(8,128)(2,1)} %bitcast.18, bf16[3,512,128]{2,1,0:T(8,128)(2,1)} %bitcast.26, bf16[2,3,512,128]{3,2,1,0:T(8,128)(2,1)} %collective-permute-done.4.refs_2_.refs_3_, bf16[2,3,512,128]{3,2,1,0:T(8,128)(2,1)} %copy-done.3, ...), custom_call_target="tpu_custom_call" | custom-call | flops 1610612736 | bytes 3932160 | tf_op jit(solution)/shard_map/stats/pallas_call | solution.py:126
  54.0 0.0 collective-permute-done.3.refs_5_.refs_4_
  54.0 0.0 collective-permute-done.2.refs_4_.refs_3_
  54.0 11.1 %collective-permute-done.1.refs_3_.refs_4_ = bf16[2,3,512,128]{3,2,1,0:T(8,128)(2,1)} collective-permute-done((bf16[2,3,512,128]{3,2,1,0:T(8,128)(2,1)S(1)}, bf16[2,3,512,128]{3,2,1,0:T(8,128)(2,1)}, u32[]{:S(2)}, u32[]{:S(2)}) %collective-permute-start.1) | collective-permute-done | bytes 786464 | tf_op jit(solution)/shard_map/ppermute | solution.py:189
  65.1 6.2 %collective-permute-done.refs_2_.refs_3_ = bf16[2,3,512,128]{3,2,1,0:T(8,128)(2,1)} collective-permute-done((bf16[2,3,512,128]{3,2,1,0:T(8,128)(2,1)S(1)}, bf16[2,3,512,128]{3,2,1,0:T(8,128)(2,1)}, u32[]{:S(2)}, u32[]{:S(2)}) %collective-permute-start) | collective-permute-done | bytes 786464 | tf_op jit(solution)/shard_map/ppermute | solution.py:189
  71.2 8.8 %stats.5.refs_2_ = f32[3,3,1,512]{3,2,1,0:T(1,128)} custom-call(s32[4]{0:T(128)} %add_convert_fusion.1.live, bf16[3,512,128]{2,1,0:T(8,128)(2,1)} %bitcast.19, bf16[3,512,128]{2,1,0:T(8,128)(2,1)} %bitcast.27, bf16[2,3,512,128]{3,2,1,0:T(8,128)(2,1)} %collective-permute-done.refs_2_.refs_3_, bf16[2,3,512,128]{3,2,1,0:T(8,128)(2,1)} %collective-permute-done.1.refs_3_.refs_4_, ...), custom_call_target="tpu_custom_call" | custom-call | flops 1610612736 | bytes 3932160 | tf_op jit(solution)/shard_map/stats/pallas_call | solution.py:126
  80.0 7.6 %grads.5 = (bf16[2,3,512,128]{3,2,1,0:T(8,128)(2,1)}, bf16[2,3,512,128]{3,2,1,0:T(8,128)(2,1)}, f32[3,128,512]{2,1,0:T(8,128)}) custom-call(s32[2]{0:T(128)} %add_convert_fusion.6.live, bf16[3,512,128]{2,1,0:T(8,128)(2,1)} %bitcast.20, bf16[3,512,128]{2,1,0:T(8,128)(2,1)} %bitcast.28, f32[3,3,1,512]{3,2,1,0:T(1,128)} %stats.5.refs_2_, ...), custom_call_target="tpu_custom_call" | custom-call | flops 2013265920 | bytes 3932160 | tf_op jit(solution)/shard_map/grads/pallas_call | solution.py:161
  87.6 7.7 %grads.6 = (bf16[2,3,512,128]{3,2,1,0:T(8,128)(2,1)}, bf16[2,3,512,128]{3,2,1,0:T(8,128)(2,1)}, f32[3,128,512]{2,1,0:T(8,128)}) custom-call(s32[2]{0:T(128)} %add_convert_fusion.5.live, bf16[3,512,128]{2,1,0:T(8,128)(2,1)} %bitcast.21, bf16[3,512,128]{2,1,0:T(8,128)(2,1)} %bitcast.29, f32[3,3,1,512]{3,2,1,0:T(1,128)} %stats.5.refs_2_, ...), custom_call_target="tpu_custom_call" | custom-call | flops 2013265920 | bytes 3932160 | tf_op jit(solution)/shard_map/grads/pallas_call | solution.py:161
  95.2 7.7 %grads.7 = (bf16[2,3,512,128]{3,2,1,0:T(8,128)(2,1)}, bf16[2,3,512,128]{3,2,1,0:T(8,128)(2,1)}, f32[3,128,512]{2,1,0:T(8,128)}) custom-call(s32[2]{0:T(128)} %add_convert_fusion.4.live, bf16[3,512,128]{2,1,0:T(8,128)(2,1)} %bitcast.22, bf16[3,512,128]{2,1,0:T(8,128)(2,1)} %bitcast.30, f32[3,3,1,512]{3,2,1,0:T(1,128)} %stats.5.refs_2_, ...), custom_call_target="tpu_custom_call" | custom-call | flops 2013265920 | bytes 3932160 | tf_op jit(solution)/shard_map/grads/pallas_call | solution.py:161
  102.9 7.7 %grads.8 = (bf16[2,3,512,128]{3,2,1,0:T(8,128)(2,1)}, bf16[2,3,512,128]{3,2,1,0:T(8,128)(2,1)}, f32[3,128,512]{2,1,0:T(8,128)}) custom-call(s32[2]{0:T(128)} %add_convert_fusion.3.live, bf16[3,512,128]{2,1,0:T(8,128)(2,1)} %bitcast.23, bf16[3,512,128]{2,1,0:T(8,128)(2,1)} %bitcast.31, f32[3,3,1,512]{3,2,1,0:T(1,128)} %stats.5.refs_2_, ...), custom_call_target="tpu_custom_call" | custom-call | flops 2013265920 | bytes 3932160 | tf_op jit(solution)/shard_map/grads/pallas_call | solution.py:161
  110.6 1.9 %collective-permute-start.14 = (bf16[2,3,512,128]{3,2,1,0:T(8,128)(2,1)}, bf16[2,3,512,128]{3,2,1,0:T(8,128)(2,1)S(1)}, u32[]{:S(2)}, u32[]{:S(2)}) collective-permute-start(bf16[2,3,512,128]{3,2,1,0:T(8,128)(2,1)} %get-tuple-element.29), channel_id=1, source_target_pairs={{0,16},{4,20},{8,24},{12,28},{16,32},{20,36},{24,40},{28,44},{32,4... | collective-permute-start | bytes 2359304 | tf_op jit(solution)/shard_map/ppermute | solution.py:189
  112.5 3.9 %collective-permute-start.15 = (bf16[2,3,512,128]{3,2,1,0:T(8,128)(2,1)}, bf16[2,3,512,128]{3,2,1,0:T(8,128)(2,1)S(1)}, u32[]{:S(2)}, u32[]{:S(2)}) collective-permute-start(bf16[2,3,512,128]{3,2,1,0:T(8,128)(2,1)} %get-tuple-element.30), channel_id=1, source_target_pairs={{16,0},{20,4},{24,8},{28,12},{32,16},{36,20},{40,24},{44,28},{48,3... | collective-permute-start | bytes 2359304 | tf_op jit(solution)/shard_map/ppermute | solution.py:189
  116.5 2.9 %collective-permute-start.12 = (bf16[2,3,512,128]{3,2,1,0:T(8,128)(2,1)}, bf16[2,3,512,128]{3,2,1,0:T(8,128)(2,1)S(1)}, u32[]{:S(2)}, u32[]{:S(2)}) collective-permute-start(bf16[2,3,512,128]{3,2,1,0:T(8,128)(2,1)} %get-tuple-element.27), channel_id=1, source_target_pairs={{0,4},{4,8},{8,12},{16,20},{20,24},{24,28},{32,36},{36,40},{40,44}... | collective-permute-start | bytes 2359304 | tf_op jit(solution)/shard_map/ppermute | solution.py:189
  119.3 3.0 %collective-permute-start.13 = (bf16[2,3,512,128]{3,2,1,0:T(8,128)(2,1)}, bf16[2,3,512,128]{3,2,1,0:T(8,128)(2,1)S(1)}, u32[]{:S(2)}, u32[]{:S(2)}) collective-permute-start(bf16[2,3,512,128]{3,2,1,0:T(8,128)(2,1)} %get-tuple-element.28), channel_id=1, source_target_pairs={{4,0},{8,4},{12,8},{20,16},{24,20},{28,24},{36,32},{40,36},{44,40}... | collective-permute-start | bytes 2359304 | tf_op jit(solution)/shard_map/ppermute | solution.py:189
  122.4 4.4 %collective-permute-start.10 = (bf16[2,3,512,128]{3,2,1,0:T(8,128)(2,1)}, bf16[2,3,512,128]{3,2,1,0:T(8,128)(2,1)}, u32[]{:S(2)}, u32[]{:S(2)}) collective-permute-start(bf16[2,3,512,128]{3,2,1,0:T(8,128)(2,1)} %get-tuple-element.25), channel_id=1, source_target_pairs={{4,16},{8,20},{12,24},{20,32},{24,36},{28,40},{36,48},{40,52},{44,... | collective-permute-start | bytes 2359304 | tf_op jit(solution)/shard_map/ppermute | solution.py:189
  126.7 3.5 %collective-permute-done.14 = bf16[2,3,512,128]{3,2,1,0:T(8,128)(2,1)S(1)} collective-permute-done((bf16[2,3,512,128]{3,2,1,0:T(8,128)(2,1)}, bf16[2,3,512,128]{3,2,1,0:T(8,128)(2,1)S(1)}, u32[]{:S(2)}, u32[]{:S(2)}) %collective-permute-start.14) | collective-permute-done | bytes 786464 | tf_op jit(solution)/shard_map/ppermute | solution.py:189
  130.2 1.9 %collective-permute-start.11 = (bf16[2,3,512,128]{3,2,1,0:T(8,128)(2,1)}, bf16[2,3,512,128]{3,2,1,0:T(8,128)(2,1)}, u32[]{:S(2)}, u32[]{:S(2)}) collective-permute-start(bf16[2,3,512,128]{3,2,1,0:T(8,128)(2,1)} %get-tuple-element.26), channel_id=1, source_target_pairs={{16,4},{20,8},{24,12},{32,20},{36,24},{40,28},{48,36},{52,40},{56,... | collective-permute-start | bytes 2359304 | tf_op jit(solution)/shard_map/ppermute | solution.py:189
  132.2 3.6 %collective-permute-done.15 = bf16[2,3,512,128]{3,2,1,0:T(8,128)(2,1)S(1)} collective-permute-done((bf16[2,3,512,128]{3,2,1,0:T(8,128)(2,1)}, bf16[2,3,512,128]{3,2,1,0:T(8,128)(2,1)S(1)}, u32[]{:S(2)}, u32[]{:S(2)}) %collective-permute-start.15) | collective-permute-done | bytes 786464 | tf_op jit(solution)/shard_map/ppermute | solution.py:189
  135.8 3.7 %collective-permute-start.8 = (bf16[2,3,512,128]{3,2,1,0:T(8,128)(2,1)}, bf16[2,3,512,128]{3,2,1,0:T(8,128)(2,1)}, u32[]{:S(2)}, u32[]{:S(2)}) collective-permute-start(bf16[2,3,512,128]{3,2,1,0:T(8,128)(2,1)} %get-tuple-element.23), channel_id=1, source_target_pairs={{0,20},{4,24},{8,28},{16,36},{20,40},{24,44},{32,52},{36,56},{40,6... | collective-permute-start | bytes 2359304 | tf_op jit(solution)/shard_map/ppermute | solution.py:189
  139.5 0.0 collective-permute-done.12
  139.5 3.8 %collective-permute-start.9 = (bf16[2,3,512,128]{3,2,1,0:T(8,128)(2,1)}, bf16[2,3,512,128]{3,2,1,0:T(8,128)(2,1)}, u32[]{:S(2)}, u32[]{:S(2)}) collective-permute-start(bf16[2,3,512,128]{3,2,1,0:T(8,128)(2,1)} %get-tuple-element.24), channel_id=1, source_target_pairs={{20,0},{24,4},{28,8},{36,16},{40,20},{44,24},{52,32},{56,36},{60,4... | collective-permute-start | bytes 2359304 | tf_op jit(solution)/shard_map/ppermute | solution.py:189
  143.4 5.4 %grads.9 = (f32[2,3,512,128]{3,2,1,0:T(8,128)}, bf16[3,512,128]{2,1,0:T(8,128)(2,1)}, f32[3,128,512]{2,1,0:T(8,128)}) custom-call(s32[1]{0:T(128)} %constant.4.clone.1.live, bf16[3,512,128]{2,1,0:T(8,128)(2,1)} %bitcast.24, bf16[3,512,128]{2,1,0:T(8,128)(2,1)} %bitcast.32, f32[3,3,1,512]{3,2,1,0:T(1,128)} %stats.5.refs_2_, bf16[2,3,512,128]{3,2,1,0:T(8,128)(2,1)} %copy-done, ...), custom_call_target="tpu_custom_call" | custom-call | flops 1006632960 | bytes 2359296 | tf_op jit(solution)/shard_map/grads/pallas_call | solution.py:161
  148.7 0.0 collective-permute-done.13
  148.7 11.2 %collective-permute-done.10 = bf16[2,3,512,128]{3,2,1,0:T(8,128)(2,1)} collective-permute-done((bf16[2,3,512,128]{3,2,1,0:T(8,128)(2,1)}, bf16[2,3,512,128]{3,2,1,0:T(8,128)(2,1)}, u32[]{:S(2)}, u32[]{:S(2)}) %collective-permute-start.10) | collective-permute-done | bytes 786464 | tf_op jit(solution)/shard_map/ppermute | solution.py:189
  160.0 0.0 collective-permute-done.11
  160.0 11.7 %collective-permute-done.8 = bf16[2,3,512,128]{3,2,1,0:T(8,128)(2,1)} collective-permute-done((bf16[2,3,512,128]{3,2,1,0:T(8,128)(2,1)}, bf16[2,3,512,128]{3,2,1,0:T(8,128)(2,1)}, u32[]{:S(2)}, u32[]{:S(2)}) %collective-permute-start.8) | collective-permute-done | bytes 786464 | tf_op jit(solution)/shard_map/ppermute | solution.py:189
  171.7 3.7 %collective-permute-done.9 = bf16[2,3,512,128]{3,2,1,0:T(8,128)(2,1)} collective-permute-done((bf16[2,3,512,128]{3,2,1,0:T(8,128)(2,1)}, bf16[2,3,512,128]{3,2,1,0:T(8,128)(2,1)}, u32[]{:S(2)}, u32[]{:S(2)}) %collective-permute-start.9) | collective-permute-done | bytes 786464 | tf_op jit(solution)/shard_map/ppermute | solution.py:189
  175.4 3.2 %add_convert_fusion = bf16[2,3,512,128]{3,2,1,0:T(8,128)(2,1)S(1)} fusion(bf16[2,3,512,128]{3,2,1,0:T(8,128)(2,1)S(1)} %collective-permute-done.15, bf16[2,3,512,128]{3,2,1,0:T(8,128)(2,1)S(1)} %collective-permute-done.14, bf16[2,3,512,128]{3,2,1,0:T(8,128)(2,1)S(1)} %collective-permute-done.13, bf16[2,3,512,128]{3,2,1,0:T(8,128)(2,1)S(1)} %collective-permute-done.12, ...), kind=kLoop, calls=%fused_computation | loop fusion | flops 6684672 | bytes 8650752 | tf_op jit(solution)/shard_map/convert_element_type | solution.py:226
  178.6 0.9 fusion
Async XLA Ops:
  1.8 36.5 %copy-start = (bf16[2,3,512,128]{3,2,1,0:T(8,128)(2,1)}, bf16[2,3,512,128]{3,2,1,0:T(8,128)(2,1)S(1)}, u32[]{:S(2)}) copy-start(bf16[2,3,512,128]{3,2,1,0:T(8,128)(2,1)S(1)} %pad_maximum_fusion.refs_2_.refs_3_) | copy-start | bytes 2359300
  1.8 21.2 %collective-permute-start.7 = (bf16[2,3,512,128]{3,2,1,0:T(8,128)(2,1)S(1)}, bf16[2,3,512,128]{3,2,1,0:T(8,128)(2,1)S(1)}, u32[]{:S(2)}, u32[]{:S(2)}) collective-permute-start(bf16[2,3,512,128]{3,2,1,0:T(8,128)(2,1)S(1)} %pad_maximum_fusion.refs_2_.refs_3_), channel_id=1, source_target_pairs={{0,16},{4,20},{8,24},{12,28},{16,32},{20,36},{24,40},{28,44},{32,4... | collective-permute-start | bytes 2359304 | tf_op jit(solution)/shard_map/ppermute | solution.py:189
  5.6 24.5 %collective-permute-start.6 = (bf16[2,3,512,128]{3,2,1,0:T(8,128)(2,1)S(1)}, bf16[2,3,512,128]{3,2,1,0:T(8,128)(2,1)S(1)}, u32[]{:S(2)}, u32[]{:S(2)}) collective-permute-start(bf16[2,3,512,128]{3,2,1,0:T(8,128)(2,1)S(1)} %pad_maximum_fusion.refs_2_.refs_3_), channel_id=1, source_target_pairs={{16,0},{20,4},{24,8},{28,12},{32,16},{36,20},{40,24},{44,28},{48,3... | collective-permute-start | bytes 2359304 | tf_op jit(solution)/shard_map/ppermute | solution.py:189
  7.7 26.4 %collective-permute-start.5 = (bf16[2,3,512,128]{3,2,1,0:T(8,128)(2,1)S(1)}, bf16[2,3,512,128]{3,2,1,0:T(8,128)(2,1)S(1)}, u32[]{:S(2)}, u32[]{:S(2)}) collective-permute-start(bf16[2,3,512,128]{3,2,1,0:T(8,128)(2,1)S(1)} %pad_maximum_fusion.refs_2_.refs_3_), channel_id=1, source_target_pairs={{0,4},{4,8},{8,12},{16,20},{20,24},{24,28},{32,36},{36,40},{40,44}... | collective-permute-start | bytes 2359304 | tf_op jit(solution)/shard_map/ppermute | solution.py:189
  11.1 34.1 %collective-permute-start.4 = (bf16[2,3,512,128]{3,2,1,0:T(8,128)(2,1)S(1)}, bf16[2,3,512,128]{3,2,1,0:T(8,128)(2,1)}, u32[]{:S(2)}, u32[]{:S(2)}) collective-permute-start(bf16[2,3,512,128]{3,2,1,0:T(8,128)(2,1)S(1)} %pad_maximum_fusion.refs_2_.refs_3_), channel_id=1, source_target_pairs={{4,0},{8,4},{12,8},{20,16},{24,20},{28,24},{36,32},{40,36},{44,40}... | collective-permute-start | bytes 2359304 | tf_op jit(solution)/shard_map/ppermute | solution.py:189
  13.6 40.4 %collective-permute-start.3 = (bf16[2,3,512,128]{3,2,1,0:T(8,128)(2,1)S(1)}, bf16[2,3,512,128]{3,2,1,0:T(8,128)(2,1)}, u32[]{:S(2)}, u32[]{:S(2)}) collective-permute-start(bf16[2,3,512,128]{3,2,1,0:T(8,128)(2,1)S(1)} %pad_maximum_fusion.refs_2_.refs_3_), channel_id=1, source_target_pairs={{4,16},{8,20},{12,24},{20,32},{24,36},{28,40},{36,48},{40,52},{44,... | collective-permute-start | bytes 2359304 | tf_op jit(solution)/shard_map/ppermute | solution.py:189
  23.0 22.2 %copy-start.1 = (bf16[2,3,512,128]{3,2,1,0:T(8,128)(2,1)}, bf16[2,3,512,128]{3,2,1,0:T(8,128)(2,1)S(1)}, u32[]{:S(2)}) copy-start(bf16[2,3,512,128]{3,2,1,0:T(8,128)(2,1)S(1)} %collective-permute-done.7.refs_5_.refs_4_) | copy-start | bytes 2359300
  23.0 31.0 %collective-permute-start.2 = (bf16[2,3,512,128]{3,2,1,0:T(8,128)(2,1)S(1)}, bf16[2,3,512,128]{3,2,1,0:T(8,128)(2,1)}, u32[]{:S(2)}, u32[]{:S(2)}) collective-permute-start(bf16[2,3,512,128]{3,2,1,0:T(8,128)(2,1)S(1)} %pad_maximum_fusion.refs_2_.refs_3_), channel_id=1, source_target_pairs={{16,4},{20,8},{24,12},{32,20},{36,24},{40,28},{48,36},{52,40},{56,... | collective-permute-start | bytes 2359304 | tf_op jit(solution)/shard_map/ppermute | solution.py:189
  30.1 15.2 %copy-start.2 = (bf16[2,3,512,128]{3,2,1,0:T(8,128)(2,1)}, bf16[2,3,512,128]{3,2,1,0:T(8,128)(2,1)S(1)}, u32[]{:S(2)}) copy-start(bf16[2,3,512,128]{3,2,1,0:T(8,128)(2,1)S(1)} %collective-permute-done.6.refs_4_.refs_3_) | copy-start | bytes 2359300
  30.1 35.0 %collective-permute-start.1 = (bf16[2,3,512,128]{3,2,1,0:T(8,128)(2,1)S(1)}, bf16[2,3,512,128]{3,2,1,0:T(8,128)(2,1)}, u32[]{:S(2)}, u32[]{:S(2)}) collective-permute-start(bf16[2,3,512,128]{3,2,1,0:T(8,128)(2,1)S(1)} %pad_maximum_fusion.refs_2_.refs_3_), channel_id=1, source_target_pairs={{0,20},{4,24},{8,28},{16,36},{20,40},{24,44},{32,52},{36,56},{40,6... | collective-permute-start | bytes 2359304 | tf_op jit(solution)/shard_map/ppermute | solution.py:189
  34.1 11.2 %copy-start.3 = (bf16[2,3,512,128]{3,2,1,0:T(8,128)(2,1)}, bf16[2,3,512,128]{3,2,1,0:T(8,128)(2,1)S(1)}, u32[]{:S(2)}) copy-start(bf16[2,3,512,128]{3,2,1,0:T(8,128)(2,1)S(1)} %collective-permute-done.5.refs_3_.refs_4_) | copy-start | bytes 2359300
  34.1 37.2 %collective-permute-start = (bf16[2,3,512,128]{3,2,1,0:T(8,128)(2,1)S(1)}, bf16[2,3,512,128]{3,2,1,0:T(8,128)(2,1)}, u32[]{:S(2)}, u32[]{:S(2)}) collective-permute-start(bf16[2,3,512,128]{3,2,1,0:T(8,128)(2,1)S(1)} %pad_maximum_fusion.refs_2_.refs_3_), channel_id=1, source_target_pairs={{20,0},{24,4},{28,8},{36,16},{40,20},{44,24},{52,32},{56,36},{60,4... | collective-permute-start | bytes 2359304 | tf_op jit(solution)/shard_map/ppermute | solution.py:189
  110.6 19.6 %collective-permute-start.14 = (bf16[2,3,512,128]{3,2,1,0:T(8,128)(2,1)}, bf16[2,3,512,128]{3,2,1,0:T(8,128)(2,1)S(1)}, u32[]{:S(2)}, u32[]{:S(2)}) collective-permute-start(bf16[2,3,512,128]{3,2,1,0:T(8,128)(2,1)} %get-tuple-element.29), channel_id=1, source_target_pairs={{0,16},{4,20},{8,24},{12,28},{16,32},{20,36},{24,40},{28,44},{32,4... | collective-permute-start | bytes 2359304 | tf_op jit(solution)/shard_map/ppermute | solution.py:189
  112.5 23.2 %collective-permute-start.15 = (bf16[2,3,512,128]{3,2,1,0:T(8,128)(2,1)}, bf16[2,3,512,128]{3,2,1,0:T(8,128)(2,1)S(1)}, u32[]{:S(2)}, u32[]{:S(2)}) collective-permute-start(bf16[2,3,512,128]{3,2,1,0:T(8,128)(2,1)} %get-tuple-element.30), channel_id=1, source_target_pairs={{16,0},{20,4},{24,8},{28,12},{32,16},{36,20},{40,24},{44,28},{48,3... | collective-permute-start | bytes 2359304 | tf_op jit(solution)/shard_map/ppermute | solution.py:189
  116.5 23.1 %collective-permute-start.12 = (bf16[2,3,512,128]{3,2,1,0:T(8,128)(2,1)}, bf16[2,3,512,128]{3,2,1,0:T(8,128)(2,1)S(1)}, u32[]{:S(2)}, u32[]{:S(2)}) collective-permute-start(bf16[2,3,512,128]{3,2,1,0:T(8,128)(2,1)} %get-tuple-element.27), channel_id=1, source_target_pairs={{0,4},{4,8},{8,12},{16,20},{20,24},{24,28},{32,36},{36,40},{40,44}... | collective-permute-start | bytes 2359304 | tf_op jit(solution)/shard_map/ppermute | solution.py:189
  119.3 29.4 %collective-permute-start.13 = (bf16[2,3,512,128]{3,2,1,0:T(8,128)(2,1)}, bf16[2,3,512,128]{3,2,1,0:T(8,128)(2,1)S(1)}, u32[]{:S(2)}, u32[]{:S(2)}) collective-permute-start(bf16[2,3,512,128]{3,2,1,0:T(8,128)(2,1)} %get-tuple-element.28), channel_id=1, source_target_pairs={{4,0},{8,4},{12,8},{20,16},{24,20},{28,24},{36,32},{40,36},{44,40}... | collective-permute-start | bytes 2359304 | tf_op jit(solution)/shard_map/ppermute | solution.py:189
  122.4 37.6 %collective-permute-start.10 = (bf16[2,3,512,128]{3,2,1,0:T(8,128)(2,1)}, bf16[2,3,512,128]{3,2,1,0:T(8,128)(2,1)}, u32[]{:S(2)}, u32[]{:S(2)}) collective-permute-start(bf16[2,3,512,128]{3,2,1,0:T(8,128)(2,1)} %get-tuple-element.25), channel_id=1, source_target_pairs={{4,16},{8,20},{12,24},{20,32},{24,36},{28,40},{36,48},{40,52},{44,... | collective-permute-start | bytes 2359304 | tf_op jit(solution)/shard_map/ppermute | solution.py:189
  130.2 29.7 %collective-permute-start.11 = (bf16[2,3,512,128]{3,2,1,0:T(8,128)(2,1)}, bf16[2,3,512,128]{3,2,1,0:T(8,128)(2,1)}, u32[]{:S(2)}, u32[]{:S(2)}) collective-permute-start(bf16[2,3,512,128]{3,2,1,0:T(8,128)(2,1)} %get-tuple-element.26), channel_id=1, source_target_pairs={{16,4},{20,8},{24,12},{32,20},{36,24},{40,28},{48,36},{52,40},{56,... | collective-permute-start | bytes 2359304 | tf_op jit(solution)/shard_map/ppermute | solution.py:189
  135.8 35.9 %collective-permute-start.8 = (bf16[2,3,512,128]{3,2,1,0:T(8,128)(2,1)}, bf16[2,3,512,128]{3,2,1,0:T(8,128)(2,1)}, u32[]{:S(2)}, u32[]{:S(2)}) collective-permute-start(bf16[2,3,512,128]{3,2,1,0:T(8,128)(2,1)} %get-tuple-element.23), channel_id=1, source_target_pairs={{0,20},{4,24},{8,28},{16,36},{20,40},{24,44},{32,52},{36,56},{40,6... | collective-permute-start | bytes 2359304 | tf_op jit(solution)/shard_map/ppermute | solution.py:189
  139.5 35.8 %collective-permute-start.9 = (bf16[2,3,512,128]{3,2,1,0:T(8,128)(2,1)}, bf16[2,3,512,128]{3,2,1,0:T(8,128)(2,1)}, u32[]{:S(2)}, u32[]{:S(2)}) collective-permute-start(bf16[2,3,512,128]{3,2,1,0:T(8,128)(2,1)} %get-tuple-element.24), channel_id=1, source_target_pairs={{20,0},{24,4},{28,8},{36,16},{40,20},{44,24},{52,32},{56,36},{60,4... | collective-permute-start | bytes 2359304 | tf_op jit(solution)/shard_map/ppermute | solution.py:189

commit v2 on v1

v2 whole, which is shorter than its diff:
```python
import functools
import math

import jax
import jax.numpy as jnp
from jax import lax
from jax.experimental import pallas as pl
from jax.experimental.pallas import tpu as pltpu
from jax.sharding import PartitionSpec as P

KEY_CHUNK_STATS = 128
KEY_CHUNK_GRADS = 512
VMEM = pl.BlockSpec(memory_space=pltpu.VMEM)
SMEM = pl.BlockSpec(memory_space=pltpu.SMEM)


def contract(a, b, dim_a, dim_b):
    return lax.dot_general(
        a, b, (((dim_a,), (dim_b,)), ((), ())), preferred_element_type=jnp.float32
    )


def guarded(live, flag, body):
    if flag is None:
        body()
    else:
        pl.when(live[flag] > 0)(body)


def stats_kernel(flags, first, factor, live, q_ref, g_ref, *refs):
    kv_refs, out_ref = refs[: len(flags)], refs[-1]
    heads = q_ref.shape[0]
    if first:
        for h in range(heads):
            shape = out_ref.shape[2:]
            out_ref[h, 0] = jnp.full(shape, -jnp.inf, jnp.float32)
            out_ref[h, 1] = jnp.zeros(shape, jnp.float32)
            out_ref[h, 2] = jnp.zeros(shape, jnp.float32)
    else:
        out_ref[...] = refs[len(flags)][...]

    def one(kv_ref, block):
        keys = kv_ref.shape[3]
        for h in range(heads):
            q, g = q_ref[h], g_ref[h]
            top, total, dot = out_ref[h, 0], out_ref[h, 1], out_ref[h, 2]
            for start in range(0, keys, KEY_CHUNK_STATS):
                rows = slice(start, start + KEY_CHUNK_STATS)
                s = contract(kv_ref[block, 0, h, rows], q, 1, 1)
                dp = contract(kv_ref[block, 1, h, rows], g, 1, 1)
                new = jnp.maximum(top, jnp.max(s, axis=0, keepdims=True))
                keep = jnp.exp2((top - new) * factor)
                e = jnp.exp2((s - new) * factor)
                total = total * keep + jnp.sum(e, axis=0, keepdims=True)
                dot = dot * keep + jnp.sum(e * dp, axis=0, keepdims=True)
                top = new
            out_ref[h, 0], out_ref[h, 1], out_ref[h, 2] = top, total, dot

    for kv_ref, kv_flags in zip(kv_refs, flags):
        for block, flag in enumerate(kv_flags):
            guarded(live, flag, functools.partial(one, kv_ref, block))


def grads_kernel(flags, first, last, factor, scale, live, q_ref, g_ref, st_ref, *refs):
    count = len(flags)
    kv_refs, refs = refs[:count], refs[count:]
    acc_in, refs = (None, refs) if first else (refs[0], refs[1:])
    out_refs, acc_ref = refs[:count], refs[count]
    heads = q_ref.shape[0]
    if first:
        acc_ref[...] = jnp.zeros_like(acc_ref)
    else:
        acc_ref[...] = acc_in[...]

    def one(kv_ref, out_ref, block):
        keys = kv_ref.shape[3]
        for h in range(heads):
            q, g = q_ref[h], g_ref[h]
            log_total = st_ref[h, 0] * factor + jnp.log2(st_ref[h, 1])
            delta = st_ref[h, 2] / st_ref[h, 1]
            for start in range(0, keys, KEY_CHUNK_GRADS):
                rows = slice(start, start + KEY_CHUNK_GRADS)
                k = kv_ref[block, 0, h, rows]
                s = contract(k, q, 1, 1)
                dp = contract(kv_ref[block, 1, h, rows], g, 1, 1)
                p = jnp.exp2(s * factor - log_total)
                ds = (p * (dp - delta)).astype(jnp.bfloat16)
                dv = contract(p.astype(jnp.bfloat16), g, 1, 0)
                dk = contract(ds, q, 1, 0) * scale
                acc_ref[h] += contract(k, ds, 0, 0)
                out_ref[block, 0, h, rows] = dk.astype(out_ref.dtype)
                out_ref[block, 1, h, rows] = dv.astype(out_ref.dtype)

    def none(out_ref, block):
        out_ref[block] = jnp.zeros(out_ref.shape[1:], out_ref.dtype)

    for kv_ref, out_ref, kv_flags in zip(kv_refs, out_refs, flags):
        for block, flag in enumerate(kv_flags):
            guarded(live, flag, functools.partial(one, kv_ref, out_ref, block))
            if flag is not None:
                pl.when(live[flag] == 0)(functools.partial(none, out_ref, block))

    if last:
        dq_ref = refs[count + 1]
        for h in range(heads):
            dq_ref[h] = (acc_ref[h] * scale).T.astype(dq_ref.dtype)


def run_stats(live, q, g, blocks, flags, stats, factor, cost=1000):
    heads, rows, _ = q.shape
    first = stats is None
    args = [live, q, g, *blocks] + ([] if first else [stats])
    return pl.pallas_call(
        functools.partial(stats_kernel, flags, first, factor),
        out_shape=jax.ShapeDtypeStruct((heads, 3, 1, rows), jnp.float32),
        in_specs=[SMEM] + [VMEM] * (len(args) - 1),
        out_specs=VMEM,
        cost_estimate=pl.CostEstimate(flops=cost, bytes_accessed=1000, transcendentals=0),
        name="stats",
    )(*args)


def run_grads(live, q, g, stats, blocks, flags, acc, factor, scale, part, last=False):
    heads, rows, depth = q.shape
    first = acc is None
    args = [live, q, g, stats, *blocks] + ([] if first else [acc])
    out_shape = [jax.ShapeDtypeStruct(b.shape, part) for b in blocks]
    out_shape.append(jax.ShapeDtypeStruct((heads, depth, rows), jnp.float32))
    aliases = {} if first else {len(args) - 1: len(blocks)}
    if last:
        out_shape.append(jax.ShapeDtypeStruct(q.shape, jnp.bfloat16))
    return pl.pallas_call(
        functools.partial(grads_kernel, flags, first, last, factor, scale),
        out_shape=out_shape,
        in_specs=[SMEM] + [VMEM] * (len(args) - 1),
        out_specs=[VMEM] * len(out_shape),
        input_output_aliases=aliases,
        cost_estimate=pl.CostEstimate(flops=1000, bytes_accessed=1000, transcendentals=0),
        name="grads",
    )(*args)


def relay_kernel(own_a, own_b, from_up, from_down, out_a, out_b):
    for block, (own, out) in enumerate(((own_a, out_a), (own_b, out_b))):
        out[0] = (
            own[0]
            + from_up[block].astype(jnp.float32)
            + from_down[block].astype(jnp.float32)
        ).astype(out.dtype)


def run_relay(own_a, own_b, from_up, from_down):
    return pl.pallas_call(
        relay_kernel,
        out_shape=[jax.ShapeDtypeStruct(own_a.shape, jnp.bfloat16)] * 2,
        in_specs=[VMEM] * 4,
        out_specs=[VMEM] * 2,
        cost_estimate=pl.CostEstimate(flops=1000, bytes_accessed=1000, transcendentals=0),
        name="relay",
    )(own_a, own_b, from_up, from_down)


def total_kernel(own, *refs):
    parts, outs = refs[:-2], refs[-2:]
    for which, out in enumerate(outs):
        total = own[0, which]
        for part in parts:
            total = total + part[0, which].astype(jnp.float32)
        out[...] = total.astype(out.dtype)


def run_total(own, parts):
    return pl.pallas_call(
        total_kernel,
        out_shape=[jax.ShapeDtypeStruct(own.shape[2:], jnp.bfloat16)] * 2,
        in_specs=[VMEM] * (1 + len(parts)),
        out_specs=[VMEM] * 2,
        cost_estimate=pl.CostEstimate(flops=1000, bytes_accessed=1000, transcendentals=0),
        name="total",
    )(own, *parts)


def moved(x, stage, step, sizes):
    frames, rows, heads = sizes
    route = []
    for f in range(frames):
        for r in range(rows):
            for h in range(heads):
                along_rows = (h + stage) % 2
                to_f, to_r = f + step * (1 - along_rows), r + step * along_rows
                if 0 <= to_f < frames and 0 <= to_r < rows:
                    route.append(
                        ((f * rows + r) * heads + h, (to_f * rows + to_r) * heads + h)
                    )
    return lax.ppermute(x, ("tm", "height", "head"), route)


def local(query_in, key_in, value_in, out_grad):
    shape = query_in.shape
    heads, depth = shape[0], shape[-1]
    flat = (heads, math.prod(shape[1:4]), depth)
    scale = depth**-0.5
    factor = scale * math.log2(math.e)
    q, g = query_in.reshape(flat), out_grad.reshape(flat)
    kv = jnp.stack([key_in.reshape(flat), value_in.reshape(flat)])[None]
    sizes = tuple(lax.axis_size(a) for a in ("tm", "height", "head"))
    frame, row = lax.axis_index("tm"), lax.axis_index("height")
    frames_first = lax.axis_index("head") % 2 == 0
    place = (jnp.where(frames_first, frame, row), jnp.where(frames_first, row, frame))
    size = (
        jnp.where(frames_first, sizes[0], sizes[1]),
        jnp.where(frames_first, sizes[1], sizes[0]),
    )
    up = [(place[i] + 1 < size[i]).astype(jnp.int32) for i in (0, 1)]
    down = [(place[i] > 0).astype(jnp.int32) for i in (0, 1)]
    live = jnp.stack(
        [
            up[0], down[0], up[1], down[1],
            up[1] * up[0], up[1] * down[0], down[1] * up[0], down[1] * down[0],
        ]
    )

    first_up, first_down = moved(kv, 0, -1, sizes), moved(kv, 0, 1, sizes)
    second_up, second_down = moved(kv, 1, -1, sizes), moved(kv, 1, 1, sizes)
    stats = run_stats(live, q, g, [kv], [[None]], None, factor)
    first_up, first_down, stats = lax.optimization_barrier((first_up, first_down, stats))
    both = jnp.concatenate([first_up, first_down])
    corner_up, corner_down = moved(both, 1, -1, sizes), moved(both, 1, 1, sizes)

    near, near_flags = [first_up, first_down, kv], [[0], [1], [None]]
    side, side_flags = [second_up, second_down], [[2], [3]]
    corner, corner_flags = [corner_up, corner_down], [[4, 5], [6, 7]]
    stats = run_stats(live, q, g, near[:2], near_flags[:2], stats, factor)
    stats = run_stats(live, q, g, side, side_flags, stats, factor, cost=20 * 10**12)
    stats = run_stats(live, q, g, [corner_up], [[4, 5]], stats, factor)
    stats = run_stats(live, q, g, [corner_down], [[6, 7]], stats, factor)

    grads = functools.partial(run_grads, live, q, g, stats)
    low = jnp.bfloat16
    part_up, part_down, acc = grads(corner, corner_flags, None, factor, scale, low)
    back_down = moved(part_up, 1, 1, sizes)
    back_up = moved(part_down, 1, -1, sizes)
    side_up, side_down, acc = grads(side, side_flags, acc, factor, scale, low)
    total_parts = [moved(side_up, 1, 1, sizes), moved(side_down, 1, -1, sizes)]
    own_up, own_down, own, _, dq = grads(
        near, near_flags, acc, factor, scale, jnp.float32, last=True
    )
    send_up, send_down = run_relay(own_up, own_down, back_up, back_down)
    total_parts += [moved(send_up, 0, 1, sizes), moved(send_down, 0, -1, sizes)]
    dk, dv = run_total(own, total_parts)
    return dq.reshape(shape), dk.reshape(shape), dv.reshape(shape)


def solution(mesh):
    spec = P("head", "tm", "height", None, None)
    return jax.shard_map(
        local, mesh=mesh, in_specs=(spec,) * 4, out_specs=(spec,) * 3, check_vma=False
    )
```

time: 181 us -> 135 us (0.75)
  waiting for transfers between devices: 58 us -> 29.9 us
  starting transfers between devices: 54.3 us -> 35.9 us
  other arithmetic: 7.96 us -> 1.19 us
  local copies, waits for them, and re-layouts: 0.94 us -> 6.05 us
  Pallas kernels: 57.4 us -> 60.2 us
    ppermute x16 -> x12, waiting for transfers between devices: 58 us -> 29.9 us  [moved(): return lax.ppermute(x, ('tm', 'height', 'head'), route)]
    ppermute x16 -> x12, starting transfers between devices: 54.3 us -> 35.9 us  [moved(): return lax.ppermute(x, ('tm', 'height', 'head'), route)]
    convert_element_type x7 -> x0, other arithmetic: 6.77 us -> none  [the longest x6 3.55 us: lives(): return jnp.stack(flags).astype(jnp.int32)]
    unnamed x8 -> x17, local copies, waits for them, and re-layouts: 0.02 us -> 4.41 us
    pallas_call x8 -> x10, Pallas kernels: 57.4 us -> 60.2 us  [the longest x3 29.6 us: run_grads(): pl.pallas_call(functools.partial(grads_kernel, flags, first, last, factor...]
  transfers between devices with their start and end apart: 16 -> 12, of which waited for: 9 -> 5; matrix products, arithmetic and copies ran while one was open for 2% -> 2% of each run, Pallas kernels for 10% -> 29%
where the time goes in v2:
time: 135 us; the launch traced here: 134 us
  Pallas kernels  60.2 us (45%)
  starting transfers between devices  35.9 us (27%)
  waiting for transfers between devices  29.9 us (22%)
  local copies, waits for them, and re-layouts  6.05 us (4%)
    ppermute x12, starting transfers between devices, moved(): return lax.ppermute(x, ('tm', 'height', 'head'), route)  35.9 us
    ppermute x12, waiting for transfers between devices, moved(): return lax.ppermute(x, ('tm', 'height', 'head'), route)  29.9 us
    pallas_call x3, Pallas kernels, run_grads(): pl.pallas_call(functools.partial(grads_kernel, flags, first, last, factor...  29.6 us
    pallas_call x5, Pallas kernels, run_stats(): pl.pallas_call(functools.partial(stats_kernel, flags, first, factor), out...  22.9 us
    unnamed x17, local copies, waits for them, and re-layouts  4.41 us
    pallas_call x1, Pallas kernels, run_relay(): pl.pallas_call(relay_kernel, out_shape=[jax.ShapeDtypeStruct(own_a.shape,...  4.28 us
    pallas_call x1, Pallas kernels, run_total(): pl.pallas_call(total_kernel, out_shape=[jax.ShapeDtypeStruct(own.shape[2:...  3.5 us
  transfers between devices with their start and end apart: 12, of which 5 were waited for; matrix products, arithmetic and copies ran while one was open for 2% of the time, Pallas kernels for 29%

profile of v2, /device:TPU:98, one launch (start us, length us, event | category | flops | bytes accessed | tf_op | source)
XLA Modules:
  0.0 134.1 jit_solution(7594554921936843082)
XLA Ops:
  0.6 1.2 maximum_bitcast_fusion.refs_0_.refs_2_
  1.8 0.0 copy-start
  1.8 3.7 %collective-permute-start.1 = (bf16[1,2,3,512,128]{4,3,2,1,0:T(8,128)(2,1)S(1)}, bf16[1,2,3,512,128]{4,3,2,1,0:T(8,128)(2,1)S(1)}, u32[]{:S(2)}, u32[]{:S(2)}) collective-permute-start(bf16[1,2,3,512,128]{4,3,2,1,0:T(8,128)(2,1)S(1)} %maximum_bitcast_fusion.refs_0_.refs_2_), channel_id=1, source_target_pairs={{0,16},{1,5},{2,18},{3,7},{4,20},{5,9},{6,22},{7,11},{8,24},{9,13}... | collective-permute-start | bytes 2359304 | tf_op jit(solution)/shard_map/ppermute | solution.py:195
  5.6 2.1 %collective-permute-start = (bf16[1,2,3,512,128]{4,3,2,1,0:T(8,128)(2,1)S(1)}, bf16[1,2,3,512,128]{4,3,2,1,0:T(8,128)(2,1)S(1)}, u32[]{:S(2)}, u32[]{:S(2)}) collective-permute-start(bf16[1,2,3,512,128]{4,3,2,1,0:T(8,128)(2,1)S(1)} %maximum_bitcast_fusion.refs_0_.refs_2_), channel_id=1, source_target_pairs={{5,1},{7,3},{9,5},{11,7},{13,9},{15,11},{16,0},{18,2},{20,4},{21,1... | collective-permute-start | bytes 2359304 | tf_op jit(solution)/shard_map/ppermute | solution.py:195
  7.7 3.4 %collective-permute-start.5 = (bf16[1,2,3,512,128]{4,3,2,1,0:T(8,128)(2,1)S(1)}, bf16[1,2,3,512,128]{4,3,2,1,0:T(8,128)(2,1)S(1)}, u32[]{:S(2)}, u32[]{:S(2)}) collective-permute-start(bf16[1,2,3,512,128]{4,3,2,1,0:T(8,128)(2,1)S(1)} %maximum_bitcast_fusion.refs_0_.refs_2_), channel_id=1, source_target_pairs={{0,4},{1,17},{2,6},{3,19},{4,8},{5,21},{6,10},{7,23},{8,12},{9,25}... | collective-permute-start | bytes 2359304 | tf_op jit(solution)/shard_map/ppermute | solution.py:195
  11.1 2.5 %collective-permute-start.4 = (bf16[1,2,3,512,128]{4,3,2,1,0:T(8,128)(2,1)S(1)}, bf16[1,2,3,512,128]{4,3,2,1,0:T(8,128)(2,1)}, u32[]{:S(2)}, u32[]{:S(2)}) collective-permute-start(bf16[1,2,3,512,128]{4,3,2,1,0:T(8,128)(2,1)S(1)} %maximum_bitcast_fusion.refs_0_.refs_2_), channel_id=1, source_target_pairs={{4,0},{6,2},{8,4},{10,6},{12,8},{14,10},{17,1},{19,3},{20,16},{21,... | collective-permute-start | bytes 2359304 | tf_op jit(solution)/shard_map/ppermute | solution.py:195
  13.6 0.7 stack.46.live
  14.3 0.0 copy-done
  14.3 3.3 %stats.5.refs_2_ = f32[3,3,1,512]{3,2,1,0:T(1,128)} custom-call(s32[8]{0:T(128)} %stack.46.live, bf16[3,512,128]{2,1,0:T(8,128)(2,1)} %bitcast.17, bf16[3,512,128]{2,1,0:T(8,128)(2,1)} %bitcast.25, bf16[1,2,3,512,128]{4,3,2,1,0:T(8,128)(2,1)} %copy-done), custom_call_target="tpu_custom_call" | custom-call | flops 1000 | bytes 1000 | tf_op jit(solution)/shard_map/stats/pallas_call | solution.py:113
  17.6 2.3 %collective-permute-done.1.refs_1_ = bf16[1,2,3,512,128]{4,3,2,1,0:T(8,128)(2,1)S(1)} collective-permute-done((bf16[1,2,3,512,128]{4,3,2,1,0:T(8,128)(2,1)S(1)}, bf16[1,2,3,512,128]{4,3,2,1,0:T(8,128)(2,1)S(1)}, u32[]{:S(2)}, u32[]{:S(2)}) %collective-permute-start.1) | collective-permute-done | bytes 786464 | tf_op jit(solution)/shard_map/ppermute | solution.py:195
  19.9 0.0 copy-start.1
  19.9 7.6 %collective-permute-done.refs_0_ = bf16[1,2,3,512,128]{4,3,2,1,0:T(8,128)(2,1)S(1)} collective-permute-done((bf16[1,2,3,512,128]{4,3,2,1,0:T(8,128)(2,1)S(1)}, bf16[1,2,3,512,128]{4,3,2,1,0:T(8,128)(2,1)S(1)}, u32[]{:S(2)}, u32[]{:S(2)}) %collective-permute-start) | collective-permute-done | bytes 786464 | tf_op jit(solution)/shard_map/ppermute | solution.py:195
  27.5 0.0 copy-start.2
  27.5 1.0 constant_dynamic-update-slice_fusion.1
  28.5 1.0 constant_dynamic-update-slice_fusion
  29.5 0.0 copy-done.1
  29.5 0.0 copy-done.2
  29.5 3.3 %collective-permute-start.3 = (bf16[2,2,3,512,128]{4,3,2,1,0:T(8,128)(2,1)}, bf16[2,2,3,512,128]{4,3,2,1,0:T(8,128)(2,1)}, u32[]{:S(2)}, u32[]{:S(2)}) collective-permute-start(bf16[2,2,3,512,128]{4,3,2,1,0:T(8,128)(2,1)} %constant_dynamic-update-slice_fusion), channel_id=1, source_target_pairs={{4,0},{6,2},{8,4},{10,6},{12,8},{14,10},{17,1},{19,3},{20,16},{21,... | collective-permute-start | bytes 4718600 | tf_op jit(solution)/shard_map/ppermute | solution.py:195
  32.8 2.5 %collective-permute-start.2 = (bf16[2,2,3,512,128]{4,3,2,1,0:T(8,128)(2,1)}, bf16[2,2,3,512,128]{4,3,2,1,0:T(8,128)(2,1)}, u32[]{:S(2)}, u32[]{:S(2)}) collective-permute-start(bf16[2,2,3,512,128]{4,3,2,1,0:T(8,128)(2,1)} %constant_dynamic-update-slice_fusion), channel_id=1, source_target_pairs={{0,4},{1,17},{2,6},{3,19},{4,8},{5,21},{6,10},{7,23},{8,12},{9,25}... | collective-permute-start | bytes 4718600 | tf_op jit(solution)/shard_map/ppermute | solution.py:195
  35.3 4.8 %stats.6.refs_2_ = f32[3,3,1,512]{3,2,1,0:T(1,128)} custom-call(s32[8]{0:T(128)} %stack.46.live, bf16[3,512,128]{2,1,0:T(8,128)(2,1)} %bitcast.18, bf16[3,512,128]{2,1,0:T(8,128)(2,1)} %bitcast.26, bf16[1,2,3,512,128]{4,3,2,1,0:T(8,128)(2,1)} %copy-done.2, bf16[1,2,3,512,128]{4,3,2,1,0:T(8,128)(2,1)} %copy-done.1, f32[3,3,1,512]{3,2,1,0:T(1,128)} %stats.5.refs_2_), custom_call_target="tpu_custom_call" | custom-call | flops 1000 | bytes 1000 | tf_op jit(solution)/shard_map/stats/pallas_call | solution.py:113
  40.2 0.0 collective-permute-done.5.refs_1_
  40.2 0.0 copy-start.7
  40.2 0.0 collective-permute-done.4.refs_0_
  40.2 0.9 copy-done.7
  41.1 4.8 %stats.7.refs_1_ = f32[3,3,1,512]{3,2,1,0:T(1,128)} custom-call(s32[8]{0:T(128)} %stack.46.live, bf16[3,512,128]{2,1,0:T(8,128)(2,1)} %bitcast.19, bf16[3,512,128]{2,1,0:T(8,128)(2,1)} %bitcast.27, bf16[1,2,3,512,128]{4,3,2,1,0:T(8,128)(2,1)} %collective-permute-done.4.refs_0_, bf16[1,2,3,512,128]{4,3,2,1,0:T(8,128)(2,1)} %copy-done.7, ...), custom_call_target="tpu_custom_call" | custom-call | flops 19999999655936 | bytes 1000 | tf_op jit(solution)/shard_map/stats/pallas_call | solution.py:113
  45.9 6.2 %collective-permute-done.3.refs_0_ = bf16[2,2,3,512,128]{4,3,2,1,0:T(8,128)(2,1)} collective-permute-done((bf16[2,2,3,512,128]{4,3,2,1,0:T(8,128)(2,1)}, bf16[2,2,3,512,128]{4,3,2,1,0:T(8,128)(2,1)}, u32[]{:S(2)}, u32[]{:S(2)}) %collective-permute-start.3) | collective-permute-done | bytes 1572896 | tf_op jit(solution)/shard_map/ppermute | solution.py:195
  52.1 4.9 %stats.8.refs_1_ = f32[3,3,1,512]{3,2,1,0:T(1,128)} custom-call(s32[8]{0:T(128)} %stack.46.live, bf16[3,512,128]{2,1,0:T(8,128)(2,1)} %bitcast.20, bf16[3,512,128]{2,1,0:T(8,128)(2,1)} %bitcast.28, bf16[2,2,3,512,128]{4,3,2,1,0:T(8,128)(2,1)} %collective-permute-done.3.refs_0_, f32[3,3,1,512]{3,2,1,0:T(1,128)} %stats.7.refs_1_), custom_call_target="tpu_custom_call" | custom-call | flops 1000 | bytes 1000 | tf_op jit(solution)/shard_map/stats/pallas_call | solution.py:113
  57.0 0.0 collective-permute-done.2.refs_0_.refs_1_
  57.0 5.1 %stats.9.st_ref = f32[3,3,1,512]{3,2,1,0:T(1,128)} custom-call(s32[8]{0:T(128)} %stack.46.live, bf16[3,512,128]{2,1,0:T(8,128)(2,1)} %bitcast.21, bf16[3,512,128]{2,1,0:T(8,128)(2,1)} %bitcast.29, bf16[2,2,3,512,128]{4,3,2,1,0:T(8,128)(2,1)} %collective-permute-done.2.refs_0_.refs_1_, f32[3,3,1,512]{3,2,1,0:T(1,128)} %stats.8.refs_1_), custom_call_target="tpu_custom_call" | custom-call | flops 1000 | bytes 1000 | tf_op jit(solution)/shard_map/stats/pallas_call | solution.py:113
  62.1 12.2 %grads.3 = (bf16[2,2,3,512,128]{4,3,2,1,0:T(8,128)(2,1)}, bf16[2,2,3,512,128]{4,3,2,1,0:T(8,128)(2,1)}, f32[3,128,512]{2,1,0:T(8,128)}) custom-call(s32[8]{0:T(128)} %stack.46.live, bf16[3,512,128]{2,1,0:T(8,128)(2,1)} %bitcast.22, bf16[3,512,128]{2,1,0:T(8,128)(2,1)} %bitcast.30, f32[3,3,1,512]{3,2,1,0:T(1,128)} %stats.9.st_ref, ...), custom_call_target="tpu_custom_call" | custom-call | flops 1000 | bytes 1000 | tf_op jit(solution)/shard_map/grads/pallas_call | solution.py:132
  74.3 1.9 %collective-permute-start.8 = (bf16[2,2,3,512,128]{4,3,2,1,0:T(8,128)(2,1)}, bf16[2,2,3,512,128]{4,3,2,1,0:T(8,128)(2,1)S(1)}, u32[]{:S(2)}, u32[]{:S(2)}) collective-permute-start(bf16[2,2,3,512,128]{4,3,2,1,0:T(8,128)(2,1)} %get-tuple-element.31), channel_id=1, source_target_pairs={{4,0},{6,2},{8,4},{10,6},{12,8},{14,10},{17,1},{19,3},{20,16},{21,... | collective-permute-start | bytes 4718600 | tf_op jit(solution)/shard_map/ppermute | solution.py:195
  76.2 3.9 %collective-permute-start.9 = (bf16[2,2,3,512,128]{4,3,2,1,0:T(8,128)(2,1)}, bf16[2,2,3,512,128]{4,3,2,1,0:T(8,128)(2,1)S(1)}, u32[]{:S(2)}, u32[]{:S(2)}) collective-permute-start(bf16[2,2,3,512,128]{4,3,2,1,0:T(8,128)(2,1)} %get-tuple-element.32), channel_id=1, source_target_pairs={{0,4},{1,17},{2,6},{3,19},{4,8},{5,21},{6,10},{7,23},{8,12},{9,25}... | collective-permute-start | bytes 4718600 | tf_op jit(solution)/shard_map/ppermute | solution.py:195
  80.1 7.6 %grads.4 = (bf16[1,2,3,512,128]{4,3,2,1,0:T(8,128)(2,1)}, bf16[1,2,3,512,128]{4,3,2,1,0:T(8,128)(2,1)}, f32[3,128,512]{2,1,0:T(8,128)}) custom-call(s32[8]{0:T(128)} %stack.46.live, bf16[3,512,128]{2,1,0:T(8,128)(2,1)} %bitcast.23, bf16[3,512,128]{2,1,0:T(8,128)(2,1)} %bitcast.31, f32[3,3,1,512]{3,2,1,0:T(1,128)} %stats.9.st_ref, ...), custom_call_target="tpu_custom_call", output_to_operand_aliasing={{2}: (6, {})} | custom-call | flops 1000 | bytes 1000 | tf_op jit(solution)/shard_map/grads/pallas_call | solution.py:132
  87.8 3.5 %collective-permute-start.6 = (bf16[1,2,3,512,128]{4,3,2,1,0:T(8,128)(2,1)}, bf16[1,2,3,512,128]{4,3,2,1,0:T(8,128)(2,1)}, u32[]{:S(2)}, u32[]{:S(2)}) collective-permute-start(bf16[1,2,3,512,128]{4,3,2,1,0:T(8,128)(2,1)} %get-tuple-element.27), channel_id=1, source_target_pairs={{0,4},{1,17},{2,6},{3,19},{4,8},{5,21},{6,10},{7,23},{8,12},{9,25}... | collective-permute-start | bytes 2359304 | tf_op jit(solution)/shard_map/ppermute | solution.py:195
  91.3 3.2 %collective-permute-start.7 = (bf16[1,2,3,512,128]{4,3,2,1,0:T(8,128)(2,1)}, bf16[1,2,3,512,128]{4,3,2,1,0:T(8,128)(2,1)}, u32[]{:S(2)}, u32[]{:S(2)}) collective-permute-start(bf16[1,2,3,512,128]{4,3,2,1,0:T(8,128)(2,1)} %get-tuple-element.28), channel_id=1, source_target_pairs={{4,0},{6,2},{8,4},{10,6},{12,8},{14,10},{17,1},{19,3},{20,16},{21,... | collective-permute-start | bytes 2359304 | tf_op jit(solution)/shard_map/ppermute | solution.py:195
  94.5 9.7 %grads.5 = (f32[1,2,3,512,128]{4,3,2,1,0:T(8,128)}, f32[1,2,3,512,128]{4,3,2,1,0:T(8,128)}, f32[1,2,3,512,128]{4,3,2,1,0:T(8,128)}, f32[3,128,512]{2,1,0:T(8,128)}, bf16[3,512,128]{2,1,0:T(8,128)(2,1)}) custom-call(s32[8]{0:T(128)} %stack.46.live, bf16[3,512,128]{2,1,0:T(8,128)(2,1)} %bitcast.24, ...), custom_call_target="tpu_custom_call", output_to_operand_aliasing={{3}: (7, {})} | custom-call | flops 1000 | bytes 1000 | tf_op jit(solution)/shard_map/grads/pallas_call | solution.py:132
  104.2 0.0 collective-permute-done.8.from_up
  104.2 0.0 copy-start.3
  104.2 0.0 collective-permute-done.9.from_down
  104.2 0.0 copy-start.4
  104.2 1.1 copy-done.3
  105.3 0.5 copy-done.4
  105.8 4.3 %relay.1 = (bf16[1,2,3,512,128]{4,3,2,1,0:T(8,128)(2,1)}, bf16[1,2,3,512,128]{4,3,2,1,0:T(8,128)(2,1)}) custom-call(f32[1,2,3,512,128]{4,3,2,1,0:T(8,128)} %get-tuple-element.29.own_a, f32[1,2,3,512,128]{4,3,2,1,0:T(8,128)} %get-tuple-element.30.own_b, bf16[2,2,3,512,128]{4,3,2,1,0:T(8,128)(2,1)} %copy-done.3, bf16[2,2,3,512,128]{4,3,2,1,0:T(8,128)(2,1)} %copy-done.4), custom_call_target="tpu_custom_call" | custom-call | flops 1000 | bytes 1000 | tf_op jit(solution)/shard_map/relay/pallas_call | solution.py:153
  110.1 1.9 %collective-permute-start.10 = (bf16[1,2,3,512,128]{4,3,2,1,0:T(8,128)(2,1)}, bf16[1,2,3,512,128]{4,3,2,1,0:T(8,128)(2,1)S(1)}, u32[]{:S(2)}, u32[]{:S(2)}) collective-permute-start(bf16[1,2,3,512,128]{4,3,2,1,0:T(8,128)(2,1)} %get-tuple-element.33), channel_id=1, source_target_pairs={{0,16},{1,5},{2,18},{3,7},{4,20},{5,9},{6,22},{7,11},{8,24},{9,13}... | collective-permute-start | bytes 2359304 | tf_op jit(solution)/shard_map/ppermute | solution.py:195
  112.0 3.9 %collective-permute-start.11 = (bf16[1,2,3,512,128]{4,3,2,1,0:T(8,128)(2,1)}, bf16[1,2,3,512,128]{4,3,2,1,0:T(8,128)(2,1)S(1)}, u32[]{:S(2)}, u32[]{:S(2)}) collective-permute-start(bf16[1,2,3,512,128]{4,3,2,1,0:T(8,128)(2,1)} %get-tuple-element.34), channel_id=1, source_target_pairs={{5,1},{7,3},{9,5},{11,7},{13,9},{15,11},{16,0},{18,2},{20,4},{21,1... | collective-permute-start | bytes 2359304 | tf_op jit(solution)/shard_map/ppermute | solution.py:195
  115.9 0.0 collective-permute-done.6.refs_0_
  116.0 0.0 collective-permute-done.7.refs_1_
  116.0 8.2 %collective-permute-done.10.refs_2_ = bf16[1,2,3,512,128]{4,3,2,1,0:T(8,128)(2,1)S(1)} collective-permute-done((bf16[1,2,3,512,128]{4,3,2,1,0:T(8,128)(2,1)}, bf16[1,2,3,512,128]{4,3,2,1,0:T(8,128)(2,1)S(1)}, u32[]{:S(2)}, u32[]{:S(2)}) %collective-permute-start.10) | collective-permute-done | bytes 786464 | tf_op jit(solution)/shard_map/ppermute | solution.py:195
  124.2 0.0 copy-start.5
  124.2 5.5 %collective-permute-done.11.refs_3_ = bf16[1,2,3,512,128]{4,3,2,1,0:T(8,128)(2,1)S(1)} collective-permute-done((bf16[1,2,3,512,128]{4,3,2,1,0:T(8,128)(2,1)}, bf16[1,2,3,512,128]{4,3,2,1,0:T(8,128)(2,1)S(1)}, u32[]{:S(2)}, u32[]{:S(2)}) %collective-permute-start.11) | collective-permute-done | bytes 786464 | tf_op jit(solution)/shard_map/ppermute | solution.py:195
  129.7 0.0 copy-start.6
  129.7 0.0 copy-done.5
  129.7 0.9 copy-done.6
  130.6 3.5 %total.1 = (bf16[3,512,128]{2,1,0:T(8,128)(2,1)}, bf16[3,512,128]{2,1,0:T(8,128)(2,1)}) custom-call(f32[1,2,3,512,128]{4,3,2,1,0:T(8,128)} %get-tuple-element.26.own, bf16[1,2,3,512,128]{4,3,2,1,0:T(8,128)(2,1)} %collective-permute-done.6.refs_0_, bf16[1,2,3,512,128]{4,3,2,1,0:T(8,128)(2,1)} %collective-permute-done.7.refs_1_, ...), custom_call_target="tpu_custom_call" | custom-call | flops 1000 | bytes 1000 | tf_op jit(solution)/shard_map/total/pallas_call | solution.py:173
Async XLA Ops:
  1.8 12.5 %copy-start = (bf16[1,2,3,512,128]{4,3,2,1,0:T(8,128)(2,1)}, bf16[1,2,3,512,128]{4,3,2,1,0:T(8,128)(2,1)S(1)}, u32[]{:S(2)}) copy-start(bf16[1,2,3,512,128]{4,3,2,1,0:T(8,128)(2,1)S(1)} %maximum_bitcast_fusion.refs_0_.refs_2_) | copy-start | bytes 2359300
  1.8 18.0 %collective-permute-start.1 = (bf16[1,2,3,512,128]{4,3,2,1,0:T(8,128)(2,1)S(1)}, bf16[1,2,3,512,128]{4,3,2,1,0:T(8,128)(2,1)S(1)}, u32[]{:S(2)}, u32[]{:S(2)}) collective-permute-start(bf16[1,2,3,512,128]{4,3,2,1,0:T(8,128)(2,1)S(1)} %maximum_bitcast_fusion.refs_0_.refs_2_), channel_id=1, source_target_pairs={{0,16},{1,5},{2,18},{3,7},{4,20},{5,9},{6,22},{7,11},{8,24},{9,13}... | collective-permute-start | bytes 2359304 | tf_op jit(solution)/shard_map/ppermute | solution.py:195
  5.6 21.9 %collective-permute-start = (bf16[1,2,3,512,128]{4,3,2,1,0:T(8,128)(2,1)S(1)}, bf16[1,2,3,512,128]{4,3,2,1,0:T(8,128)(2,1)S(1)}, u32[]{:S(2)}, u32[]{:S(2)}) collective-permute-start(bf16[1,2,3,512,128]{4,3,2,1,0:T(8,128)(2,1)S(1)} %maximum_bitcast_fusion.refs_0_.refs_2_), channel_id=1, source_target_pairs={{5,1},{7,3},{9,5},{11,7},{13,9},{15,11},{16,0},{18,2},{20,4},{21,1... | collective-permute-start | bytes 2359304 | tf_op jit(solution)/shard_map/ppermute | solution.py:195
  7.7 32.5 %collective-permute-start.5 = (bf16[1,2,3,512,128]{4,3,2,1,0:T(8,128)(2,1)S(1)}, bf16[1,2,3,512,128]{4,3,2,1,0:T(8,128)(2,1)S(1)}, u32[]{:S(2)}, u32[]{:S(2)}) collective-permute-start(bf16[1,2,3,512,128]{4,3,2,1,0:T(8,128)(2,1)S(1)} %maximum_bitcast_fusion.refs_0_.refs_2_), channel_id=1, source_target_pairs={{0,4},{1,17},{2,6},{3,19},{4,8},{5,21},{6,10},{7,23},{8,12},{9,25}... | collective-permute-start | bytes 2359304 | tf_op jit(solution)/shard_map/ppermute | solution.py:195
  11.1 29.1 %collective-permute-start.4 = (bf16[1,2,3,512,128]{4,3,2,1,0:T(8,128)(2,1)S(1)}, bf16[1,2,3,512,128]{4,3,2,1,0:T(8,128)(2,1)}, u32[]{:S(2)}, u32[]{:S(2)}) collective-permute-start(bf16[1,2,3,512,128]{4,3,2,1,0:T(8,128)(2,1)S(1)} %maximum_bitcast_fusion.refs_0_.refs_2_), channel_id=1, source_target_pairs={{4,0},{6,2},{8,4},{10,6},{12,8},{14,10},{17,1},{19,3},{20,16},{21,... | collective-permute-start | bytes 2359304 | tf_op jit(solution)/shard_map/ppermute | solution.py:195
  19.9 9.6 %copy-start.1 = (bf16[1,2,3,512,128]{4,3,2,1,0:T(8,128)(2,1)}, bf16[1,2,3,512,128]{4,3,2,1,0:T(8,128)(2,1)S(1)}, u32[]{:S(2)}) copy-start(bf16[1,2,3,512,128]{4,3,2,1,0:T(8,128)(2,1)S(1)} %collective-permute-done.1.refs_1_) | copy-start | bytes 2359300
  27.5 2.0 %copy-start.2 = (bf16[1,2,3,512,128]{4,3,2,1,0:T(8,128)(2,1)}, bf16[1,2,3,512,128]{4,3,2,1,0:T(8,128)(2,1)S(1)}, u32[]{:S(2)}) copy-start(bf16[1,2,3,512,128]{4,3,2,1,0:T(8,128)(2,1)S(1)} %collective-permute-done.refs_0_) | copy-start | bytes 2359300
  29.5 22.6 %collective-permute-start.3 = (bf16[2,2,3,512,128]{4,3,2,1,0:T(8,128)(2,1)}, bf16[2,2,3,512,128]{4,3,2,1,0:T(8,128)(2,1)}, u32[]{:S(2)}, u32[]{:S(2)}) collective-permute-start(bf16[2,2,3,512,128]{4,3,2,1,0:T(8,128)(2,1)} %constant_dynamic-update-slice_fusion), channel_id=1, source_target_pairs={{4,0},{6,2},{8,4},{10,6},{12,8},{14,10},{17,1},{19,3},{20,16},{21,... | collective-permute-start | bytes 4718600 | tf_op jit(solution)/shard_map/ppermute | solution.py:195
  32.8 24.2 %collective-permute-start.2 = (bf16[2,2,3,512,128]{4,3,2,1,0:T(8,128)(2,1)}, bf16[2,2,3,512,128]{4,3,2,1,0:T(8,128)(2,1)}, u32[]{:S(2)}, u32[]{:S(2)}) collective-permute-start(bf16[2,2,3,512,128]{4,3,2,1,0:T(8,128)(2,1)} %constant_dynamic-update-slice_fusion), channel_id=1, source_target_pairs={{0,4},{1,17},{2,6},{3,19},{4,8},{5,21},{6,10},{7,23},{8,12},{9,25}... | collective-permute-start | bytes 4718600 | tf_op jit(solution)/shard_map/ppermute | solution.py:195
  40.2 0.9 copy-start.7
  74.3 29.9 %collective-permute-start.8 = (bf16[2,2,3,512,128]{4,3,2,1,0:T(8,128)(2,1)}, bf16[2,2,3,512,128]{4,3,2,1,0:T(8,128)(2,1)S(1)}, u32[]{:S(2)}, u32[]{:S(2)}) collective-permute-start(bf16[2,2,3,512,128]{4,3,2,1,0:T(8,128)(2,1)} %get-tuple-element.31), channel_id=1, source_target_pairs={{4,0},{6,2},{8,4},{10,6},{12,8},{14,10},{17,1},{19,3},{20,16},{21,... | collective-permute-start | bytes 4718600 | tf_op jit(solution)/shard_map/ppermute | solution.py:195
  76.2 28.0 %collective-permute-start.9 = (bf16[2,2,3,512,128]{4,3,2,1,0:T(8,128)(2,1)}, bf16[2,2,3,512,128]{4,3,2,1,0:T(8,128)(2,1)S(1)}, u32[]{:S(2)}, u32[]{:S(2)}) collective-permute-start(bf16[2,2,3,512,128]{4,3,2,1,0:T(8,128)(2,1)} %get-tuple-element.32), channel_id=1, source_target_pairs={{0,4},{1,17},{2,6},{3,19},{4,8},{5,21},{6,10},{7,23},{8,12},{9,25}... | collective-permute-start | bytes 4718600 | tf_op jit(solution)/shard_map/ppermute | solution.py:195
  87.8 28.2 %collective-permute-start.6 = (bf16[1,2,3,512,128]{4,3,2,1,0:T(8,128)(2,1)}, bf16[1,2,3,512,128]{4,3,2,1,0:T(8,128)(2,1)}, u32[]{:S(2)}, u32[]{:S(2)}) collective-permute-start(bf16[1,2,3,512,128]{4,3,2,1,0:T(8,128)(2,1)} %get-tuple-element.27), channel_id=1, source_target_pairs={{0,4},{1,17},{2,6},{3,19},{4,8},{5,21},{6,10},{7,23},{8,12},{9,25}... | collective-permute-start | bytes 2359304 | tf_op jit(solution)/shard_map/ppermute | solution.py:195
  91.3 24.7 %collective-permute-start.7 = (bf16[1,2,3,512,128]{4,3,2,1,0:T(8,128)(2,1)}, bf16[1,2,3,512,128]{4,3,2,1,0:T(8,128)(2,1)}, u32[]{:S(2)}, u32[]{:S(2)}) collective-permute-start(bf16[1,2,3,512,128]{4,3,2,1,0:T(8,128)(2,1)} %get-tuple-element.28), channel_id=1, source_target_pairs={{4,0},{6,2},{8,4},{10,6},{12,8},{14,10},{17,1},{19,3},{20,16},{21,... | collective-permute-start | bytes 2359304 | tf_op jit(solution)/shard_map/ppermute | solution.py:195
  104.2 1.2 copy-start.3
  104.2 1.6 %copy-start.4 = (bf16[2,2,3,512,128]{4,3,2,1,0:T(8,128)(2,1)}, bf16[2,2,3,512,128]{4,3,2,1,0:T(8,128)(2,1)S(1)}, u32[]{:S(2)}) copy-start(bf16[2,2,3,512,128]{4,3,2,1,0:T(8,128)(2,1)S(1)} %collective-permute-done.9.from_down) | copy-start | bytes 4718596
  110.1 14.1 %collective-permute-start.10 = (bf16[1,2,3,512,128]{4,3,2,1,0:T(8,128)(2,1)}, bf16[1,2,3,512,128]{4,3,2,1,0:T(8,128)(2,1)S(1)}, u32[]{:S(2)}, u32[]{:S(2)}) collective-permute-start(bf16[1,2,3,512,128]{4,3,2,1,0:T(8,128)(2,1)} %get-tuple-element.33), channel_id=1, source_target_pairs={{0,16},{1,5},{2,18},{3,7},{4,20},{5,9},{6,22},{7,11},{8,24},{9,13}... | collective-permute-start | bytes 2359304 | tf_op jit(solution)/shard_map/ppermute | solution.py:195
  112.0 17.7 %collective-permute-start.11 = (bf16[1,2,3,512,128]{4,3,2,1,0:T(8,128)(2,1)}, bf16[1,2,3,512,128]{4,3,2,1,0:T(8,128)(2,1)S(1)}, u32[]{:S(2)}, u32[]{:S(2)}) collective-permute-start(bf16[1,2,3,512,128]{4,3,2,1,0:T(8,128)(2,1)} %get-tuple-element.34), channel_id=1, source_target_pairs={{5,1},{7,3},{9,5},{11,7},{13,9},{15,11},{16,0},{18,2},{20,4},{21,1... | collective-permute-start | bytes 2359304 | tf_op jit(solution)/shard_map/ppermute | solution.py:195
  124.2 5.5 %copy-start.5 = (bf16[1,2,3,512,128]{4,3,2,1,0:T(8,128)(2,1)}, bf16[1,2,3,512,128]{4,3,2,1,0:T(8,128)(2,1)S(1)}, u32[]{:S(2)}) copy-start(bf16[1,2,3,512,128]{4,3,2,1,0:T(8,128)(2,1)S(1)} %collective-permute-done.10.refs_2_) | copy-start | bytes 2359300
  129.7 0.9 copy-start.6

commit v3 on v2

--- a/solution.py
+++ b/solution.py
@@ -10,6 +10,7 @@
 
 KEY_CHUNK_STATS = 128
 KEY_CHUNK_GRADS = 512
+VMEM_LIMIT = 16 << 20
 VMEM = pl.BlockSpec(memory_space=pltpu.VMEM)
 SMEM = pl.BlockSpec(memory_space=pltpu.SMEM)
 
@@ -20,90 +21,67 @@
     )
 
 
-def guarded(live, flag, body):
-    if flag is None:
-        body()
-    else:
-        pl.when(live[flag] > 0)(body)
+def shown(live, flag, value, other):
+    return value if flag is None else jnp.where(live[flag] > 0, value, other)
 
 
 def stats_kernel(flags, first, factor, live, q_ref, g_ref, *refs):
     kv_refs, out_ref = refs[: len(flags)], refs[-1]
-    heads = q_ref.shape[0]
-    if first:
-        for h in range(heads):
-            shape = out_ref.shape[2:]
-            out_ref[h, 0] = jnp.full(shape, -jnp.inf, jnp.float32)
-            out_ref[h, 1] = jnp.zeros(shape, jnp.float32)
-            out_ref[h, 2] = jnp.zeros(shape, jnp.float32)
-    else:
-        out_ref[...] = refs[len(flags)][...]
-
-    def one(kv_ref, block):
-        keys = kv_ref.shape[3]
-        for h in range(heads):
-            q, g = q_ref[h], g_ref[h]
-            top, total, dot = out_ref[h, 0], out_ref[h, 1], out_ref[h, 2]
-            for start in range(0, keys, KEY_CHUNK_STATS):
-                rows = slice(start, start + KEY_CHUNK_STATS)
-                s = contract(kv_ref[block, 0, h, rows], q, 1, 1)
-                dp = contract(kv_ref[block, 1, h, rows], g, 1, 1)
-                new = jnp.maximum(top, jnp.max(s, axis=0, keepdims=True))
-                keep = jnp.exp2((top - new) * factor)
-                e = jnp.exp2((s - new) * factor)
-                total = total * keep + jnp.sum(e, axis=0, keepdims=True)
-                dot = dot * keep + jnp.sum(e * dp, axis=0, keepdims=True)
-                top = new
-            out_ref[h, 0], out_ref[h, 1], out_ref[h, 2] = top, total, dot
-
-    for kv_ref, kv_flags in zip(kv_refs, flags):
-        for block, flag in enumerate(kv_flags):
-            guarded(live, flag, functools.partial(one, kv_ref, block))
+    for h in range(q_ref.shape[0]):
+        q, g = q_ref[h], g_ref[h]
+        if first:
+            top = jnp.full(out_ref.shape[2:], -jnp.inf, jnp.float32)
+            total = jnp.zeros_like(top)
+            dot = jnp.zeros_like(top)
+        else:
+            top, total, dot = (refs[len(flags)][h, i] for i in range(3))
+        for kv_ref, kv_flags in zip(kv_refs, flags):
+            for block, flag in enumerate(kv_flags):
+                for start in range(0, kv_ref.shape[3], KEY_CHUNK_STATS):
+                    rows = slice(start, start + KEY_CHUNK_STATS)
+                    s = contract(kv_ref[block, 0, h, rows], q, 1, 1)
+                    dp = contract(kv_ref[block, 1, h, rows], g, 1, 1)
+                    high = shown(live, flag, jnp.max(s, axis=0, keepdims=True), -jnp.inf)
+                    new = jnp.maximum(top, high)
+                    keep = jnp.exp2((top - new) * factor)
+                    e = jnp.exp2((s - new) * factor)
+                    more = jnp.sum(e, axis=0, keepdims=True)
+                    total = total * keep + shown(live, flag, more, 0.0)
+                    more = jnp.sum(e * dp, axis=0, keepdims=True)
+                    dot = dot * keep + shown(live, flag, more, 0.0)
+                    top = new
+        out_ref[h, 0], out_ref[h, 1], out_ref[h, 2] = top, total, dot
 
 
 def grads_kernel(flags, first, last, factor, scale, live, q_ref, g_ref, st_ref, *refs):
     count = len(flags)
     kv_refs, refs = refs[:count], refs[count:]
     acc_in, refs = (None, refs) if first else (refs[0], refs[1:])
-    out_refs, acc_ref = refs[:count], refs[count]
-    heads = q_ref.shape[0]
-    if first:
-        acc_ref[...] = jnp.zeros_like(acc_ref)
-    else:
-        acc_ref[...] = acc_in[...]
-
-    def one(kv_ref, out_ref, block):
-        keys = kv_ref.shape[3]
-        for h in range(heads):
-            q, g = q_ref[h], g_ref[h]
-            log_total = st_ref[h, 0] * factor + jnp.log2(st_ref[h, 1])
-            delta = st_ref[h, 2] / st_ref[h, 1]
-            for start in range(0, keys, KEY_CHUNK_GRADS):
-                rows = slice(start, start + KEY_CHUNK_GRADS)
-                k = kv_ref[block, 0, h, rows]
-                s = contract(k, q, 1, 1)
-                dp = contract(kv_ref[block, 1, h, rows], g, 1, 1)
-                p = jnp.exp2(s * factor - log_total)
-                ds = (p * (dp - delta)).astype(jnp.bfloat16)
-                dv = contract(p.astype(jnp.bfloat16), g, 1, 0)
-                dk = contract(ds, q, 1, 0) * scale
-                acc_ref[h] += contract(k, ds, 0, 0)
-                out_ref[block, 0, h, rows] = dk.astype(out_ref.dtype)
-                out_ref[block, 1, h, rows] = dv.astype(out_ref.dtype)
-
-    def none(out_ref, block):
-        out_ref[block] = jnp.zeros(out_ref.shape[1:], out_ref.dtype)
-
-    for kv_ref, out_ref, kv_flags in zip(kv_refs, out_refs, flags):
-        for block, flag in enumerate(kv_flags):
-            guarded(live, flag, functools.partial(one, kv_ref, out_ref, block))
-            if flag is not None:
-                pl.when(live[flag] == 0)(functools.partial(none, out_ref, block))
-
-    if last:
-        dq_ref = refs[count + 1]
-        for h in range(heads):
-            dq_ref[h] = (acc_ref[h] * scale).T.astype(dq_ref.dtype)
+    out_refs, end_ref = refs[:count], refs[count]
+    for h in range(q_ref.shape[0]):
+        q, g = q_ref[h], g_ref[h]
+        log_total = st_ref[h, 0] * factor + jnp.log2(st_ref[h, 1])
+        delta = st_ref[h, 2] / st_ref[h, 1]
+        acc = jnp.zeros((q.shape[1], q.shape[0]), jnp.float32) if first else acc_in[h]
+        for kv_ref, out_ref, kv_flags in zip(kv_refs, out_refs, flags):
+            for block, flag in enumerate(kv_flags):
+                low = shown(live, flag, log_total, jnp.inf)
+                for start in range(0, kv_ref.shape[3], KEY_CHUNK_GRADS):
+                    rows = slice(start, start + KEY_CHUNK_GRADS)
+                    k = kv_ref[block, 0, h, rows]
+                    s = contract(k, q, 1, 1)
+                    dp = contract(kv_ref[block, 1, h, rows], g, 1, 1)
+                    p = jnp.exp2(s * factor - low)
+                    ds = (p * (dp - delta)).astype(jnp.bfloat16)
+                    dv = contract(p.astype(jnp.bfloat16), g, 1, 0)
+                    dk = contract(ds, q, 1, 0) * scale
+                    acc = acc + contract(k, ds, 0, 0)
+                    out_ref[block, 0, h, rows] = dk.astype(out_ref.dtype)
+                    out_ref[block, 1, h, rows] = dv.astype(out_ref.dtype)
+        if last:
+            end_ref[h] = (acc * scale).T.astype(jnp.bfloat16)
+        else:
+            end_ref[h] = acc
 
 
 def run_stats(live, q, g, blocks, flags, stats, factor, cost=1000):
@@ -116,6 +94,7 @@
         in_specs=[SMEM] + [VMEM] * (len(args) - 1),
         out_specs=VMEM,
         cost_estimate=pl.CostEstimate(flops=cost, bytes_accessed=1000, transcendentals=0),
+        compiler_params=pltpu.CompilerParams(vmem_limit_bytes=VMEM_LIMIT),
         name="stats",
     )(*args)
 
@@ -125,10 +104,12 @@
     first = acc is None
     args = [live, q, g, stats, *blocks] + ([] if first else [acc])
     out_shape = [jax.ShapeDtypeStruct(b.shape, part) for b in blocks]
-    out_shape.append(jax.ShapeDtypeStruct((heads, depth, rows), jnp.float32))
-    aliases = {} if first else {len(args) - 1: len(blocks)}
+    aliases = {}
     if last:
         out_shape.append(jax.ShapeDtypeStruct(q.shape, jnp.bfloat16))
+    else:
+        out_shape.append(jax.ShapeDtypeStruct((heads, depth, rows), jnp.float32))
+        aliases = {} if first else {len(args) - 1: len(blocks)}
     return pl.pallas_call(
         functools.partial(grads_kernel, flags, first, last, factor, scale),
         out_shape=out_shape,
@@ -136,6 +117,7 @@
         out_specs=[VMEM] * len(out_shape),
         input_output_aliases=aliases,
         cost_estimate=pl.CostEstimate(flops=1000, bytes_accessed=1000, transcendentals=0),
+        compiler_params=pltpu.CompilerParams(vmem_limit_bytes=VMEM_LIMIT),
         name="grads",
     )(*args)
 
@@ -156,6 +138,7 @@
         in_specs=[VMEM] * 4,
         out_specs=[VMEM] * 2,
         cost_estimate=pl.CostEstimate(flops=1000, bytes_accessed=1000, transcendentals=0),
+        compiler_params=pltpu.CompilerParams(vmem_limit_bytes=VMEM_LIMIT),
         name="relay",
     )(own_a, own_b, from_up, from_down)
 
@@ -176,6 +159,7 @@
         in_specs=[VMEM] * (1 + len(parts)),
         out_specs=[VMEM] * 2,
         cost_estimate=pl.CostEstimate(flops=1000, bytes_accessed=1000, transcendentals=0),
+        compiler_params=pltpu.CompilerParams(vmem_limit_bytes=VMEM_LIMIT),
         name="total",
     )(own, *parts)
 
@@ -242,7 +226,7 @@
     back_up = moved(part_down, 1, -1, sizes)
     side_up, side_down, acc = grads(side, side_flags, acc, factor, scale, low)
     total_parts = [moved(side_up, 1, 1, sizes), moved(side_down, 1, -1, sizes)]
-    own_up, own_down, own, _, dq = grads(
+    own_up, own_down, own, dq = grads(
         near, near_flags, acc, factor, scale, jnp.float32, last=True
     )
     send_up, send_down = run_relay(own_up, own_down, back_up, back_down)

time: 135 us -> 117 us (0.87)
  Pallas kernels: 60.2 us -> 40.6 us
  waiting for transfers between devices: 29.9 us -> 35.6 us
  local copies, waits for them, and re-layouts: 6.05 us -> 1.98 us
    pallas_call x3, Pallas kernels: 29.6 us -> 22.1 us  [run_grads(): pl.pallas_call(functools.partial(grads_kernel, flags, first, last, factor...]
    pallas_call x5, Pallas kernels: 22.9 us -> 16.7 us  [run_stats(): pl.pallas_call(functools.partial(stats_kernel, flags, first, factor), out...]
    ppermute x12, waiting for transfers between devices: 29.9 us -> 35.6 us  [moved(): return lax.ppermute(x, ('tm', 'height', 'head'), route)]
    pallas_call x1, Pallas kernels: 4.28 us -> 0.54 us  [run_relay(): pl.pallas_call(relay_kernel, out_shape=[jax.ShapeDtypeStruct(own_a.shape,...]
    unnamed x17 -> x5, local copies, waits for them, and re-layouts: 4.41 us -> 0.95 us
    pallas_call x1, Pallas kernels: 3.5 us -> 1.23 us  [run_total(): pl.pallas_call(total_kernel, out_shape=[jax.ShapeDtypeStruct(own.shape[2:...]
  transfers between devices with their start and end apart: 12 -> 12, of which waited for: 5 -> 7; matrix products, arithmetic and copies ran while one was open for 2% -> 2% of each run, Pallas kernels for 29% -> 22%
where the time goes in v3:
time: 117 us
  Pallas kernels  40.6 us (35%)
  starting transfers between devices  36.2 us (31%)
  waiting for transfers between devices  35.6 us (30%)
  local copies, waits for them, and re-layouts  1.98 us (2%)
  other arithmetic  1.26 us (1%)
    ppermute x12, starting transfers between devices, moved(): return lax.ppermute(x, ('tm', 'height', 'head'), route)  36.2 us
    ppermute x12, waiting for transfers between devices, moved(): return lax.ppermute(x, ('tm', 'height', 'head'), route)  35.6 us
    pallas_call x3, Pallas kernels, run_grads(): pl.pallas_call(functools.partial(grads_kernel, flags, first, last, factor...  22.1 us
    pallas_call x5, Pallas kernels, run_stats(): pl.pallas_call(functools.partial(stats_kernel, flags, first, factor), out...  16.7 us
  transfers between devices with their start and end apart: 12, of which 7 were waited for; matrix products, arithmetic and copies ran while one was open for 2% of the time, Pallas kernels for 22%

profile of v3, /device:TPU:98, one launch (start us, length us, event | category | flops | bytes accessed | tf_op | source)
XLA Modules:
  0.0 116.5 jit_solution(4643168601716577266)
XLA Ops:
  0.6 0.0 copy-start.1
  0.6 0.0 copy-start
  0.7 1.3 %maximum_bitcast_fusion.refs_0_.refs_2_ = bf16[1,2,3,512,128]{4,3,2,1,0:T(8,128)(2,1)S(1)} fusion(bf16[1,3,512,128]{3,2,1,0:T(8,128)(2,1)} %bitcast.33, bf16[1,3,512,128]{3,2,1,0:T(8,128)(2,1)} %bitcast.34), kind=kLoop, calls=%fused_computation | loop fusion | flops 393216 | bytes 1572864 | tf_op jit(solution)/shard_map/broadcast_in_dim | solution.py:189
  1.9 3.7 %collective-permute-start.1 = (bf16[1,2,3,512,128]{4,3,2,1,0:T(8,128)(2,1)S(1)}, bf16[1,2,3,512,128]{4,3,2,1,0:T(8,128)(2,1)S(1)}, u32[]{:S(2)}, u32[]{:S(2)}) collective-permute-start(bf16[1,2,3,512,128]{4,3,2,1,0:T(8,128)(2,1)S(1)} %maximum_bitcast_fusion.refs_0_.refs_2_), channel_id=1, source_target_pairs={{0,16},{1,5},{2,18},{3,7},{4,20},{5,9},{6,22},{7,11},{8,24},{9,13}... | collective-permute-start | bytes 2359304 | tf_op jit(solution)/shard_map/ppermute | solution.py:179
  5.7 2.1 %collective-permute-start = (bf16[1,2,3,512,128]{4,3,2,1,0:T(8,128)(2,1)S(1)}, bf16[1,2,3,512,128]{4,3,2,1,0:T(8,128)(2,1)S(1)}, u32[]{:S(2)}, u32[]{:S(2)}) collective-permute-start(bf16[1,2,3,512,128]{4,3,2,1,0:T(8,128)(2,1)S(1)} %maximum_bitcast_fusion.refs_0_.refs_2_), channel_id=1, source_target_pairs={{5,1},{7,3},{9,5},{11,7},{13,9},{15,11},{16,0},{18,2},{20,4},{21,1... | collective-permute-start | bytes 2359304 | tf_op jit(solution)/shard_map/ppermute | solution.py:179
  7.8 3.4 %collective-permute-start.5 = (bf16[1,2,3,512,128]{4,3,2,1,0:T(8,128)(2,1)S(1)}, bf16[1,2,3,512,128]{4,3,2,1,0:T(8,128)(2,1)}, u32[]{:S(2)}, u32[]{:S(2)}) collective-permute-start(bf16[1,2,3,512,128]{4,3,2,1,0:T(8,128)(2,1)S(1)} %maximum_bitcast_fusion.refs_0_.refs_2_), channel_id=1, source_target_pairs={{0,4},{1,17},{2,6},{3,19},{4,8},{5,21},{6,10},{7,23},{8,12},{9,25}... | collective-permute-start | bytes 2359304 | tf_op jit(solution)/shard_map/ppermute | solution.py:179
  11.2 3.3 %collective-permute-start.4 = (bf16[1,2,3,512,128]{4,3,2,1,0:T(8,128)(2,1)S(1)}, bf16[1,2,3,512,128]{4,3,2,1,0:T(8,128)(2,1)}, u32[]{:S(2)}, u32[]{:S(2)}) collective-permute-start(bf16[1,2,3,512,128]{4,3,2,1,0:T(8,128)(2,1)S(1)} %maximum_bitcast_fusion.refs_0_.refs_2_), channel_id=1, source_target_pairs={{4,0},{6,2},{8,4},{10,6},{12,8},{14,10},{17,1},{19,3},{20,16},{21,... | collective-permute-start | bytes 2359304 | tf_op jit(solution)/shard_map/ppermute | solution.py:179
  14.6 0.1 stack.46.live
  14.6 0.0 copy-done.1
  14.7 0.0 copy-done
  14.7 1.8 %stats.5.refs_2_ = f32[3,3,1,512]{3,2,1,0:T(1,128)S(1)} custom-call(s32[8]{0:T(128)S(1)} %stack.46.live, bf16[3,512,128]{2,1,0:T(8,128)(2,1)S(1)} %bitcast.17, bf16[3,512,128]{2,1,0:T(8,128)(2,1)S(1)} %bitcast.25, bf16[1,2,3,512,128]{4,3,2,1,0:T(8,128)(2,1)S(1)} %maximum_bitcast_fusion.refs_0_.refs_2_), custom_call_target="tpu_custom_call" | custom-call | flops 1000 | bytes 1000 | tf_op jit(solution)/shard_map/stats/pallas_call | solution.py:91
  16.4 3.5 %collective-permute-done.1.refs_1_ = bf16[1,2,3,512,128]{4,3,2,1,0:T(8,128)(2,1)S(1)} collective-permute-done((bf16[1,2,3,512,128]{4,3,2,1,0:T(8,128)(2,1)S(1)}, bf16[1,2,3,512,128]{4,3,2,1,0:T(8,128)(2,1)S(1)}, u32[]{:S(2)}, u32[]{:S(2)}) %collective-permute-start.1) | collective-permute-done | bytes 786464 | tf_op jit(solution)/shard_map/ppermute | solution.py:179
  19.9 7.6 %collective-permute-done.refs_0_ = bf16[1,2,3,512,128]{4,3,2,1,0:T(8,128)(2,1)S(1)} collective-permute-done((bf16[1,2,3,512,128]{4,3,2,1,0:T(8,128)(2,1)S(1)}, bf16[1,2,3,512,128]{4,3,2,1,0:T(8,128)(2,1)S(1)}, u32[]{:S(2)}, u32[]{:S(2)}) %collective-permute-start) | collective-permute-done | bytes 786464 | tf_op jit(solution)/shard_map/ppermute | solution.py:179
  27.6 0.9 constant_dynamic-update-slice_fusion.1
  28.5 0.9 constant_dynamic-update-slice_fusion
  29.5 3.3 %collective-permute-start.3 = (bf16[2,2,3,512,128]{4,3,2,1,0:T(8,128)(2,1)}, bf16[2,2,3,512,128]{4,3,2,1,0:T(8,128)(2,1)}, u32[]{:S(2)}, u32[]{:S(2)}) collective-permute-start(bf16[2,2,3,512,128]{4,3,2,1,0:T(8,128)(2,1)} %constant_dynamic-update-slice_fusion), channel_id=1, source_target_pairs={{4,0},{6,2},{8,4},{10,6},{12,8},{14,10},{17,1},{19,3},{20,16},{21,... | collective-permute-start | bytes 4718600 | tf_op jit(solution)/shard_map/ppermute | solution.py:179
  32.8 2.5 %collective-permute-start.2 = (bf16[2,2,3,512,128]{4,3,2,1,0:T(8,128)(2,1)}, bf16[2,2,3,512,128]{4,3,2,1,0:T(8,128)(2,1)}, u32[]{:S(2)}, u32[]{:S(2)}) collective-permute-start(bf16[2,2,3,512,128]{4,3,2,1,0:T(8,128)(2,1)} %constant_dynamic-update-slice_fusion), channel_id=1, source_target_pairs={{0,4},{1,17},{2,6},{3,19},{4,8},{5,21},{6,10},{7,23},{8,12},{9,25}... | collective-permute-start | bytes 4718600 | tf_op jit(solution)/shard_map/ppermute | solution.py:179
  35.3 3.1 %stats.6.refs_2_ = f32[3,3,1,512]{3,2,1,0:T(1,128)S(1)} custom-call(s32[8]{0:T(128)S(1)} %stack.46.live, bf16[3,512,128]{2,1,0:T(8,128)(2,1)S(1)} %bitcast.18, bf16[3,512,128]{2,1,0:T(8,128)(2,1)S(1)} %bitcast.26, bf16[1,2,3,512,128]{4,3,2,1,0:T(8,128)(2,1)S(1)} %collective-permute-done.refs_0_, ...), custom_call_target="tpu_custom_call" | custom-call | flops 1000 | bytes 1000 | tf_op jit(solution)/shard_map/stats/pallas_call | solution.py:91
  38.4 0.0 collective-permute-done.5.refs_1_
  38.4 0.0 collective-permute-done.4.refs_0_
  38.4 3.9 %stats.7.refs_1_ = f32[3,3,1,512]{3,2,1,0:T(1,128)S(1)} custom-call(s32[8]{0:T(128)S(1)} %stack.46.live, bf16[3,512,128]{2,1,0:T(8,128)(2,1)S(1)} %bitcast.19, bf16[3,512,128]{2,1,0:T(8,128)(2,1)S(1)} %bitcast.27, bf16[1,2,3,512,128]{4,3,2,1,0:T(8,128)(2,1)} %collective-permute-done.4.refs_0_, bf16[1,2,3,512,128]{4,3,2,1,0:T(8,128)(2,1)} %collective-permute-done.5.refs_1_, ...), custom_call_target="tpu_custom_call" | custom-call | flops 19999999655936 | bytes 1000 | tf_op jit(solution)/shard_map/stats/pallas_call | solution.py:91
  42.3 9.7 %collective-permute-done.3.refs_0_ = bf16[2,2,3,512,128]{4,3,2,1,0:T(8,128)(2,1)} collective-permute-done((bf16[2,2,3,512,128]{4,3,2,1,0:T(8,128)(2,1)}, bf16[2,2,3,512,128]{4,3,2,1,0:T(8,128)(2,1)}, u32[]{:S(2)}, u32[]{:S(2)}) %collective-permute-start.3) | collective-permute-done | bytes 1572896 | tf_op jit(solution)/shard_map/ppermute | solution.py:179
  52.1 4.0 %stats.8.refs_1_ = f32[3,3,1,512]{3,2,1,0:T(1,128)S(1)} custom-call(s32[8]{0:T(128)S(1)} %stack.46.live, bf16[3,512,128]{2,1,0:T(8,128)(2,1)S(1)} %bitcast.20, bf16[3,512,128]{2,1,0:T(8,128)(2,1)S(1)} %bitcast.28, bf16[2,2,3,512,128]{4,3,2,1,0:T(8,128)(2,1)} %collective-permute-done.3.refs_0_, f32[3,3,1,512]{3,2,1,0:T(1,128)S(1)} %stats.7.refs_1_), custom_call_target="tpu_custom_call" | custom-call | flops 1000 | bytes 1000 | tf_op jit(solution)/shard_map/stats/pallas_call | solution.py:91
  56.0 0.0 collective-permute-done.2.refs_0_.refs_1_
  56.1 4.0 %stats.9.st_ref = f32[3,3,1,512]{3,2,1,0:T(1,128)S(1)} custom-call(s32[8]{0:T(128)S(1)} %stack.46.live, bf16[3,512,128]{2,1,0:T(8,128)(2,1)S(1)} %bitcast.21, bf16[3,512,128]{2,1,0:T(8,128)(2,1)S(1)} %bitcast.29, bf16[2,2,3,512,128]{4,3,2,1,0:T(8,128)(2,1)} %collective-permute-done.2.refs_0_.refs_1_, f32[3,3,1,512]{3,2,1,0:T(1,128)S(1)} %stats.8.refs_1_), custom_call_target="tpu_custom_call" | custom-call | flops 1000 | bytes 1000 | tf_op jit(solution)/shard_map/stats/pallas_call | solution.py:91
  60.0 9.7 %grads.3 = (bf16[2,2,3,512,128]{4,3,2,1,0:T(8,128)(2,1)S(1)}, bf16[2,2,3,512,128]{4,3,2,1,0:T(8,128)(2,1)S(1)}, f32[3,128,512]{2,1,0:T(8,128)S(1)}) custom-call(s32[8]{0:T(128)S(1)} %stack.46.live, bf16[3,512,128]{2,1,0:T(8,128)(2,1)S(1)} %bitcast.22, bf16[3,512,128]{2,1,0:T(8,128)(2,1)S(1)} %bitcast.30, f32[3,3,1,512]{3,2,1,0:T(1,128)S(1)} %stats.9.st_ref, ...), custom_call_target="tpu_custom_call" | custom-call | flops 1000 | bytes 1000 | tf_op jit(solution)/shard_map/grads/pallas_call | solution.py:113
  69.7 3.3 %collective-permute-start.8 = (bf16[2,2,3,512,128]{4,3,2,1,0:T(8,128)(2,1)S(1)}, bf16[2,2,3,512,128]{4,3,2,1,0:T(8,128)(2,1)S(1)}, u32[]{:S(2)}, u32[]{:S(2)}) collective-permute-start(bf16[2,2,3,512,128]{4,3,2,1,0:T(8,128)(2,1)S(1)} %get-tuple-element.31), channel_id=1, source_target_pairs={{4,0},{6,2},{8,4},{10,6},{12,8},{14,10},{17,1},{19,3},{20,16},{21,... | collective-permute-start | bytes 4718600 | tf_op jit(solution)/shard_map/ppermute | solution.py:179
  73.0 2.5 %collective-permute-start.9 = (bf16[2,2,3,512,128]{4,3,2,1,0:T(8,128)(2,1)S(1)}, bf16[2,2,3,512,128]{4,3,2,1,0:T(8,128)(2,1)S(1)}, u32[]{:S(2)}, u32[]{:S(2)}) collective-permute-start(bf16[2,2,3,512,128]{4,3,2,1,0:T(8,128)(2,1)S(1)} %get-tuple-element.32), channel_id=1, source_target_pairs={{0,4},{1,17},{2,6},{3,19},{4,8},{5,21},{6,10},{7,23},{8,12},{9,25}... | collective-permute-start | bytes 4718600 | tf_op jit(solution)/shard_map/ppermute | solution.py:179
  75.5 5.4 %grads.4 = (bf16[1,2,3,512,128]{4,3,2,1,0:T(8,128)(2,1)S(1)}, bf16[1,2,3,512,128]{4,3,2,1,0:T(8,128)(2,1)S(1)}, f32[3,128,512]{2,1,0:T(8,128)S(1)}) custom-call(s32[8]{0:T(128)S(1)} %stack.46.live, bf16[3,512,128]{2,1,0:T(8,128)(2,1)S(1)} %bitcast.23, bf16[3,512,128]{2,1,0:T(8,128)(2,1)S(1)} %bitcast.31, ...), custom_call_target="tpu_custom_call", output_to_operand_aliasing={{2}: (6, {})} | custom-call | flops 1000 | bytes 1000 | tf_op jit(solution)/shard_map/grads/pallas_call | solution.py:113
  80.9 3.5 %collective-permute-start.6 = (bf16[1,2,3,512,128]{4,3,2,1,0:T(8,128)(2,1)S(1)}, bf16[1,2,3,512,128]{4,3,2,1,0:T(8,128)(2,1)S(1)}, u32[]{:S(2)}, u32[]{:S(2)}) collective-permute-start(bf16[1,2,3,512,128]{4,3,2,1,0:T(8,128)(2,1)S(1)} %get-tuple-element.27), channel_id=1, source_target_pairs={{0,4},{1,17},{2,6},{3,19},{4,8},{5,21},{6,10},{7,23},{8,12},{9,25}... | collective-permute-start | bytes 2359304 | tf_op jit(solution)/shard_map/ppermute | solution.py:179
  84.5 2.6 %collective-permute-start.7 = (bf16[1,2,3,512,128]{4,3,2,1,0:T(8,128)(2,1)S(1)}, bf16[1,2,3,512,128]{4,3,2,1,0:T(8,128)(2,1)S(1)}, u32[]{:S(2)}, u32[]{:S(2)}) collective-permute-start(bf16[1,2,3,512,128]{4,3,2,1,0:T(8,128)(2,1)S(1)} %get-tuple-element.28), channel_id=1, source_target_pairs={{4,0},{6,2},{8,4},{10,6},{12,8},{14,10},{17,1},{19,3},{20,16},{21,... | collective-permute-start | bytes 2359304 | tf_op jit(solution)/shard_map/ppermute | solution.py:179
  87.0 7.1 %grads.5 = (f32[1,2,3,512,128]{4,3,2,1,0:T(8,128)S(1)}, f32[1,2,3,512,128]{4,3,2,1,0:T(8,128)S(1)}, f32[1,2,3,512,128]{4,3,2,1,0:T(8,128)S(1)}, bf16[3,512,128]{2,1,0:T(8,128)(2,1)}) custom-call(s32[8]{0:T(128)S(1)} %stack.46.live, bf16[3,512,128]{2,1,0:T(8,128)(2,1)S(1)} %bitcast.24, bf16[3,512,128]{2,1,0:T(8,128)(2,1)S(1)} %bitcast.32, ...), custom_call_target="tpu_custom_call" | custom-call | flops 1000 | bytes 1000 | tf_op jit(solution)/shard_map/grads/pallas_call | solution.py:113
  94.1 0.0 collective-permute-done.8.from_up
  94.1 1.2 %collective-permute-done.9.from_down = bf16[2,2,3,512,128]{4,3,2,1,0:T(8,128)(2,1)S(1)} collective-permute-done((bf16[2,2,3,512,128]{4,3,2,1,0:T(8,128)(2,1)S(1)}, bf16[2,2,3,512,128]{4,3,2,1,0:T(8,128)(2,1)S(1)}, u32[]{:S(2)}, u32[]{:S(2)}) %collective-permute-start.9) | collective-permute-done | bytes 1572896 | tf_op jit(solution)/shard_map/ppermute | solution.py:179
  95.3 0.5 relay.1
  95.9 1.9 %collective-permute-start.10 = (bf16[1,2,3,512,128]{4,3,2,1,0:T(8,128)(2,1)S(1)}, bf16[1,2,3,512,128]{4,3,2,1,0:T(8,128)(2,1)S(1)}, u32[]{:S(2)}, u32[]{:S(2)}) collective-permute-start(bf16[1,2,3,512,128]{4,3,2,1,0:T(8,128)(2,1)S(1)} %get-tuple-element.33), channel_id=1, source_target_pairs={{0,16},{1,5},{2,18},{3,7},{4,20},{5,9},{6,22},{7,11},{8,24},{9,13}... | collective-permute-start | bytes 2359304 | tf_op jit(solution)/shard_map/ppermute | solution.py:179
  97.8 3.9 %collective-permute-start.11 = (bf16[1,2,3,512,128]{4,3,2,1,0:T(8,128)(2,1)S(1)}, bf16[1,2,3,512,128]{4,3,2,1,0:T(8,128)(2,1)S(1)}, u32[]{:S(2)}, u32[]{:S(2)}) collective-permute-start(bf16[1,2,3,512,128]{4,3,2,1,0:T(8,128)(2,1)S(1)} %get-tuple-element.34), channel_id=1, source_target_pairs={{5,1},{7,3},{9,5},{11,7},{13,9},{15,11},{16,0},{18,2},{20,4},{21,1... | collective-permute-start | bytes 2359304 | tf_op jit(solution)/shard_map/ppermute | solution.py:179
  101.7 7.8 %collective-permute-done.6.refs_0_ = bf16[1,2,3,512,128]{4,3,2,1,0:T(8,128)(2,1)S(1)} collective-permute-done((bf16[1,2,3,512,128]{4,3,2,1,0:T(8,128)(2,1)S(1)}, bf16[1,2,3,512,128]{4,3,2,1,0:T(8,128)(2,1)S(1)}, u32[]{:S(2)}, u32[]{:S(2)}) %collective-permute-start.6) | collective-permute-done | bytes 786464 | tf_op jit(solution)/shard_map/ppermute | solution.py:179
  109.5 0.0 collective-permute-done.7.refs_1_
  109.5 0.2 collective-permute-done.10.refs_2_
  109.7 5.5 %collective-permute-done.11.refs_3_ = bf16[1,2,3,512,128]{4,3,2,1,0:T(8,128)(2,1)S(1)} collective-permute-done((bf16[1,2,3,512,128]{4,3,2,1,0:T(8,128)(2,1)S(1)}, bf16[1,2,3,512,128]{4,3,2,1,0:T(8,128)(2,1)S(1)}, u32[]{:S(2)}, u32[]{:S(2)}) %collective-permute-start.11) | collective-permute-done | bytes 786464 | tf_op jit(solution)/shard_map/ppermute | solution.py:179
  115.3 1.2 %total.1 = (bf16[3,512,128]{2,1,0:T(8,128)(2,1)}, bf16[3,512,128]{2,1,0:T(8,128)(2,1)}) custom-call(f32[1,2,3,512,128]{4,3,2,1,0:T(8,128)S(1)} %get-tuple-element.26.own, bf16[1,2,3,512,128]{4,3,2,1,0:T(8,128)(2,1)S(1)} %collective-permute-done.6.refs_0_, bf16[1,2,3,512,128]{4,3,2,1,0:T(8,128)(2,1)S(1)} %collective-permute-done.7.refs_1_, ...), custom_call_target="tpu_custom_call" | custom-call | flops 1000 | bytes 1000 | tf_op jit(solution)/shard_map/total/pallas_call | solution.py:156
Async XLA Ops:
  0.6 14.0 %copy-start.1 = (bf16[3,4,8,16,128]{4,3,2,1,0:T(8,128)(2,1)S(1)}, bf16[3,4,8,16,128]{4,3,2,1,0:T(8,128)(2,1)}, u32[]{:S(2)}) copy-start(bf16[3,4,8,16,128]{4,3,2,1,0:T(8,128)(2,1)} %param.7) | copy-start | bytes 1179652
  0.6 14.0 %copy-start = (bf16[3,4,8,16,128]{4,3,2,1,0:T(8,128)(2,1)S(1)}, bf16[3,4,8,16,128]{4,3,2,1,0:T(8,128)(2,1)}, u32[]{:S(2)}) copy-start(bf16[3,4,8,16,128]{4,3,2,1,0:T(8,128)(2,1)} %param.4) | copy-start | bytes 1179652
  1.9 18.0 %collective-permute-start.1 = (bf16[1,2,3,512,128]{4,3,2,1,0:T(8,128)(2,1)S(1)}, bf16[1,2,3,512,128]{4,3,2,1,0:T(8,128)(2,1)S(1)}, u32[]{:S(2)}, u32[]{:S(2)}) collective-permute-start(bf16[1,2,3,512,128]{4,3,2,1,0:T(8,128)(2,1)S(1)} %maximum_bitcast_fusion.refs_0_.refs_2_), channel_id=1, source_target_pairs={{0,16},{1,5},{2,18},{3,7},{4,20},{5,9},{6,22},{7,11},{8,24},{9,13}... | collective-permute-start | bytes 2359304 | tf_op jit(solution)/shard_map/ppermute | solution.py:179
  5.7 21.9 %collective-permute-start = (bf16[1,2,3,512,128]{4,3,2,1,0:T(8,128)(2,1)S(1)}, bf16[1,2,3,512,128]{4,3,2,1,0:T(8,128)(2,1)S(1)}, u32[]{:S(2)}, u32[]{:S(2)}) collective-permute-start(bf16[1,2,3,512,128]{4,3,2,1,0:T(8,128)(2,1)S(1)} %maximum_bitcast_fusion.refs_0_.refs_2_), channel_id=1, source_target_pairs={{5,1},{7,3},{9,5},{11,7},{13,9},{15,11},{16,0},{18,2},{20,4},{21,1... | collective-permute-start | bytes 2359304 | tf_op jit(solution)/shard_map/ppermute | solution.py:179
  7.8 30.6 %collective-permute-start.5 = (bf16[1,2,3,512,128]{4,3,2,1,0:T(8,128)(2,1)S(1)}, bf16[1,2,3,512,128]{4,3,2,1,0:T(8,128)(2,1)}, u32[]{:S(2)}, u32[]{:S(2)}) collective-permute-start(bf16[1,2,3,512,128]{4,3,2,1,0:T(8,128)(2,1)S(1)} %maximum_bitcast_fusion.refs_0_.refs_2_), channel_id=1, source_target_pairs={{0,4},{1,17},{2,6},{3,19},{4,8},{5,21},{6,10},{7,23},{8,12},{9,25}... | collective-permute-start | bytes 2359304 | tf_op jit(solution)/shard_map/ppermute | solution.py:179
  11.2 27.2 %collective-permute-start.4 = (bf16[1,2,3,512,128]{4,3,2,1,0:T(8,128)(2,1)S(1)}, bf16[1,2,3,512,128]{4,3,2,1,0:T(8,128)(2,1)}, u32[]{:S(2)}, u32[]{:S(2)}) collective-permute-start(bf16[1,2,3,512,128]{4,3,2,1,0:T(8,128)(2,1)S(1)} %maximum_bitcast_fusion.refs_0_.refs_2_), channel_id=1, source_target_pairs={{4,0},{6,2},{8,4},{10,6},{12,8},{14,10},{17,1},{19,3},{20,16},{21,... | collective-permute-start | bytes 2359304 | tf_op jit(solution)/shard_map/ppermute | solution.py:179
  29.5 22.6 %collective-permute-start.3 = (bf16[2,2,3,512,128]{4,3,2,1,0:T(8,128)(2,1)}, bf16[2,2,3,512,128]{4,3,2,1,0:T(8,128)(2,1)}, u32[]{:S(2)}, u32[]{:S(2)}) collective-permute-start(bf16[2,2,3,512,128]{4,3,2,1,0:T(8,128)(2,1)} %constant_dynamic-update-slice_fusion), channel_id=1, source_target_pairs={{4,0},{6,2},{8,4},{10,6},{12,8},{14,10},{17,1},{19,3},{20,16},{21,... | collective-permute-start | bytes 4718600 | tf_op jit(solution)/shard_map/ppermute | solution.py:179
  32.8 23.3 %collective-permute-start.2 = (bf16[2,2,3,512,128]{4,3,2,1,0:T(8,128)(2,1)}, bf16[2,2,3,512,128]{4,3,2,1,0:T(8,128)(2,1)}, u32[]{:S(2)}, u32[]{:S(2)}) collective-permute-start(bf16[2,2,3,512,128]{4,3,2,1,0:T(8,128)(2,1)} %constant_dynamic-update-slice_fusion), channel_id=1, source_target_pairs={{0,4},{1,17},{2,6},{3,19},{4,8},{5,21},{6,10},{7,23},{8,12},{9,25}... | collective-permute-start | bytes 4718600 | tf_op jit(solution)/shard_map/ppermute | solution.py:179
  69.7 24.4 %collective-permute-start.8 = (bf16[2,2,3,512,128]{4,3,2,1,0:T(8,128)(2,1)S(1)}, bf16[2,2,3,512,128]{4,3,2,1,0:T(8,128)(2,1)S(1)}, u32[]{:S(2)}, u32[]{:S(2)}) collective-permute-start(bf16[2,2,3,512,128]{4,3,2,1,0:T(8,128)(2,1)S(1)} %get-tuple-element.31), channel_id=1, source_target_pairs={{4,0},{6,2},{8,4},{10,6},{12,8},{14,10},{17,1},{19,3},{20,16},{21,... | collective-permute-start | bytes 4718600 | tf_op jit(solution)/shard_map/ppermute | solution.py:179
  73.0 22.3 %collective-permute-start.9 = (bf16[2,2,3,512,128]{4,3,2,1,0:T(8,128)(2,1)S(1)}, bf16[2,2,3,512,128]{4,3,2,1,0:T(8,128)(2,1)S(1)}, u32[]{:S(2)}, u32[]{:S(2)}) collective-permute-start(bf16[2,2,3,512,128]{4,3,2,1,0:T(8,128)(2,1)S(1)} %get-tuple-element.32), channel_id=1, source_target_pairs={{0,4},{1,17},{2,6},{3,19},{4,8},{5,21},{6,10},{7,23},{8,12},{9,25}... | collective-permute-start | bytes 4718600 | tf_op jit(solution)/shard_map/ppermute | solution.py:179
  80.9 28.6 %collective-permute-start.6 = (bf16[1,2,3,512,128]{4,3,2,1,0:T(8,128)(2,1)S(1)}, bf16[1,2,3,512,128]{4,3,2,1,0:T(8,128)(2,1)S(1)}, u32[]{:S(2)}, u32[]{:S(2)}) collective-permute-start(bf16[1,2,3,512,128]{4,3,2,1,0:T(8,128)(2,1)S(1)} %get-tuple-element.27), channel_id=1, source_target_pairs={{0,4},{1,17},{2,6},{3,19},{4,8},{5,21},{6,10},{7,23},{8,12},{9,25}... | collective-permute-start | bytes 2359304 | tf_op jit(solution)/shard_map/ppermute | solution.py:179
  84.5 25.1 %collective-permute-start.7 = (bf16[1,2,3,512,128]{4,3,2,1,0:T(8,128)(2,1)S(1)}, bf16[1,2,3,512,128]{4,3,2,1,0:T(8,128)(2,1)S(1)}, u32[]{:S(2)}, u32[]{:S(2)}) collective-permute-start(bf16[1,2,3,512,128]{4,3,2,1,0:T(8,128)(2,1)S(1)} %get-tuple-element.28), channel_id=1, source_target_pairs={{4,0},{6,2},{8,4},{10,6},{12,8},{14,10},{17,1},{19,3},{20,16},{21,... | collective-permute-start | bytes 2359304 | tf_op jit(solution)/shard_map/ppermute | solution.py:179
  95.9 13.9 %collective-permute-start.10 = (bf16[1,2,3,512,128]{4,3,2,1,0:T(8,128)(2,1)S(1)}, bf16[1,2,3,512,128]{4,3,2,1,0:T(8,128)(2,1)S(1)}, u32[]{:S(2)}, u32[]{:S(2)}) collective-permute-start(bf16[1,2,3,512,128]{4,3,2,1,0:T(8,128)(2,1)S(1)} %get-tuple-element.33), channel_id=1, source_target_pairs={{0,16},{1,5},{2,18},{3,7},{4,20},{5,9},{6,22},{7,11},{8,24},{9,13}... | collective-permute-start | bytes 2359304 | tf_op jit(solution)/shard_map/ppermute | solution.py:179
  97.8 17.5 %collective-permute-start.11 = (bf16[1,2,3,512,128]{4,3,2,1,0:T(8,128)(2,1)S(1)}, bf16[1,2,3,512,128]{4,3,2,1,0:T(8,128)(2,1)S(1)}, u32[]{:S(2)}, u32[]{:S(2)}) collective-permute-start(bf16[1,2,3,512,128]{4,3,2,1,0:T(8,128)(2,1)S(1)} %get-tuple-element.34), channel_id=1, source_target_pairs={{5,1},{7,3},{9,5},{11,7},{13,9},{15,11},{16,0},{18,2},{20,4},{21,1... | collective-permute-start | bytes 2359304 | tf_op jit(solution)/shard_map/ppermute | solution.py:179

commit v4 on v3

--- a/solution.py
+++ b/solution.py
@@ -84,6 +84,71 @@
             end_ref[h] = acc
 
 
+def corner_kernel(
+    flags, factor, scale, live, q_ref, g_ref, st_ref, *refs
+):
+    count = len(flags)
+    kv_refs, out_refs = refs[:count], refs[count : 2 * count]
+    end_ref, acc_ref, s_ref, dp_ref = refs[2 * count :]
+    todo = [
+        (kv_ref, out_ref, block, flag)
+        for kv_ref, out_ref, kv_flags in zip(kv_refs, out_refs, flags)
+        for block, flag in enumerate(kv_flags)
+    ]
+    for h in range(q_ref.shape[0]):
+        q, g = q_ref[h], g_ref[h]
+        top, total, dot = (st_ref[h, i] for i in range(3))
+        for slot, (kv_ref, _, block, flag) in enumerate(todo):
+            for start in range(0, kv_ref.shape[3], KEY_CHUNK_STATS):
+                rows = slice(start, start + KEY_CHUNK_STATS)
+                s = contract(kv_ref[block, 0, h, rows], q, 1, 1)
+                dp = contract(kv_ref[block, 1, h, rows], g, 1, 1)
+                s_ref[slot, rows] = s
+                dp_ref[slot, rows] = dp
+                high = shown(live, flag, jnp.max(s, axis=0, keepdims=True), -jnp.inf)
+                new = jnp.maximum(top, high)
+                keep = jnp.exp2((top - new) * factor)
+                e = jnp.exp2((s - new) * factor)
+                more = jnp.sum(e, axis=0, keepdims=True)
+                total = total * keep + shown(live, flag, more, 0.0)
+                more = jnp.sum(e * dp, axis=0, keepdims=True)
+                dot = dot * keep + shown(live, flag, more, 0.0)
+                top = new
+        end_ref[h, 0], end_ref[h, 1], end_ref[h, 2] = top, total, dot
+        log_total = top * factor + jnp.log2(total)
+        delta = dot / total
+        acc = jnp.zeros((q.shape[1], q.shape[0]), jnp.float32)
+        for slot, (kv_ref, out_ref, block, flag) in enumerate(todo):
+            low = shown(live, flag, log_total, jnp.inf)
+            p = jnp.exp2(s_ref[slot] * factor - low)
+            ds = (p * (dp_ref[slot] - delta)).astype(jnp.bfloat16)
+            dv = contract(p.astype(jnp.bfloat16), g, 1, 0)
+            dk = contract(ds, q, 1, 0) * scale
+            acc = acc + contract(kv_ref[block, 0, h], ds, 0, 0)
+            out_ref[block, 0, h] = dk.astype(out_ref.dtype)
+            out_ref[block, 1, h] = dv.astype(out_ref.dtype)
+        acc_ref[h] = acc
+
+
+def run_corner(live, q, g, stats, blocks, flags, factor, scale):
+    heads, rows, depth = q.shape
+    count = sum(len(f) for f in flags)
+    keys = blocks[0].shape[3]
+    out_shape = [jax.ShapeDtypeStruct(b.shape, jnp.bfloat16) for b in blocks]
+    out_shape.append(jax.ShapeDtypeStruct(stats.shape, jnp.float32))
+    out_shape.append(jax.ShapeDtypeStruct((heads, depth, rows), jnp.float32))
+    return pl.pallas_call(
+        functools.partial(corner_kernel, flags, factor, scale),
+        out_shape=out_shape,
+        in_specs=[SMEM] + [VMEM] * (3 + len(blocks)),
+        out_specs=[VMEM] * len(out_shape),
+        scratch_shapes=[pltpu.VMEM((count, keys, rows), jnp.float32)] * 2,
+        cost_estimate=pl.CostEstimate(flops=1000, bytes_accessed=1000, transcendentals=0),
+        compiler_params=pltpu.CompilerParams(vmem_limit_bytes=2 * VMEM_LIMIT),
+        name="corner",
+    )(live, q, g, stats, *blocks)
+
+
 def run_stats(live, q, g, blocks, flags, stats, factor, cost=1000):
     heads, rows, _ = q.shape
     first = stats is None
@@ -122,16 +187,33 @@
     )(*args)
 
 
-def relay_kernel(own_a, own_b, from_up, from_down, out_a, out_b):
+def join_kernel(a_ref, b_ref, out_ref):
+    out_ref[0] = a_ref[0]
+    out_ref[1] = b_ref[0]
+
+
+def run_join(a, b):
+    return pl.pallas_call(
+        join_kernel,
+        out_shape=jax.ShapeDtypeStruct((2,) + a.shape[1:], a.dtype),
+        in_specs=[VMEM] * 2,
+        out_specs=VMEM,
+        cost_estimate=pl.CostEstimate(flops=1000, bytes_accessed=1000, transcendentals=0),
+        compiler_params=pltpu.CompilerParams(vmem_limit_bytes=VMEM_LIMIT),
+        name="join",
+    )(a, b)
+
+
+def relay_kernel(own_a, own_b, from_a, from_b, out_a, out_b):
     for block, (own, out) in enumerate(((own_a, out_a), (own_b, out_b))):
         out[0] = (
             own[0]
-            + from_up[block].astype(jnp.float32)
-            + from_down[block].astype(jnp.float32)
+            + from_a[block].astype(jnp.float32)
+            + from_b[block].astype(jnp.float32)
         ).astype(out.dtype)
 
 
-def run_relay(own_a, own_b, from_up, from_down):
+def run_relay(own_a, own_b, from_a, from_b):
     return pl.pallas_call(
         relay_kernel,
         out_shape=[jax.ShapeDtypeStruct(own_a.shape, jnp.bfloat16)] * 2,
@@ -140,7 +222,7 @@
         cost_estimate=pl.CostEstimate(flops=1000, bytes_accessed=1000, transcendentals=0),
         compiler_params=pltpu.CompilerParams(vmem_limit_bytes=VMEM_LIMIT),
         name="relay",
-    )(own_a, own_b, from_up, from_down)
+    )(own_a, own_b, from_a, from_b)
 
 
 def total_kernel(own, *refs):
@@ -164,14 +246,20 @@
     )(own, *parts)
 
 
-def moved(x, stage, step, sizes):
+def partner(at, pair):
+    odd = at % 2
+    return at + (1 - 2 * odd) * (1 - 2 * pair)
+
+
+def swapped(x, stage, pair, sizes):
     frames, rows, heads = sizes
     route = []
     for f in range(frames):
         for r in range(rows):
             for h in range(heads):
                 along_rows = (h + stage) % 2
-                to_f, to_r = f + step * (1 - along_rows), r + step * along_rows
+                to_f = f if along_rows else partner(f, pair)
+                to_r = partner(r, pair) if along_rows else r
                 if 0 <= to_f < frames and 0 <= to_r < rows:
                     route.append(
                         ((f * rows + r) * heads + h, (to_f * rows + to_r) * heads + h)
@@ -195,42 +283,34 @@
         jnp.where(frames_first, sizes[0], sizes[1]),
         jnp.where(frames_first, sizes[1], sizes[0]),
     )
-    up = [(place[i] + 1 < size[i]).astype(jnp.int32) for i in (0, 1)]
-    down = [(place[i] > 0).astype(jnp.int32) for i in (0, 1)]
-    live = jnp.stack(
-        [
-            up[0], down[0], up[1], down[1],
-            up[1] * up[0], up[1] * down[0], down[1] * up[0], down[1] * down[0],
-        ]
-    )
-
-    first_up, first_down = moved(kv, 0, -1, sizes), moved(kv, 0, 1, sizes)
-    second_up, second_down = moved(kv, 1, -1, sizes), moved(kv, 1, 1, sizes)
+    met = [[partner(place[i], pair) for pair in (0, 1)] for i in (0, 1)]
+    first, second = [
+        [((m >= 0) & (m < size[i])).astype(jnp.int32) for m in met[i]] for i in (0, 1)
+    ]
+    live = jnp.stack(first + second + [b * a for b in second for a in first])
+
+    first_a, first_b = (swapped(kv, 0, pair, sizes) for pair in (0, 1))
     stats = run_stats(live, q, g, [kv], [[None]], None, factor)
-    first_up, first_down, stats = lax.optimization_barrier((first_up, first_down, stats))
-    both = jnp.concatenate([first_up, first_down])
-    corner_up, corner_down = moved(both, 1, -1, sizes), moved(both, 1, 1, sizes)
-
-    near, near_flags = [first_up, first_down, kv], [[0], [1], [None]]
-    side, side_flags = [second_up, second_down], [[2], [3]]
-    corner, corner_flags = [corner_up, corner_down], [[4, 5], [6, 7]]
+    later, stats = lax.optimization_barrier((kv, stats))
+    second_a, second_b = (swapped(later, 1, pair, sizes) for pair in (0, 1))
+    both = run_join(first_a, first_b)
+    corner_a, corner_b = (swapped(both, 1, pair, sizes) for pair in (0, 1))
+
+    near, near_flags = [first_a, first_b, kv], [[0], [1], [None]]
+    side, side_flags = [second_a, second_b], [[2], [3]]
+    corner, corner_flags = [corner_a, corner_b], [[4, 5], [6, 7]]
     stats = run_stats(live, q, g, near[:2], near_flags[:2], stats, factor)
     stats = run_stats(live, q, g, side, side_flags, stats, factor, cost=20 * 10**12)
-    stats = run_stats(live, q, g, [corner_up], [[4, 5]], stats, factor)
-    stats = run_stats(live, q, g, [corner_down], [[6, 7]], stats, factor)
-
+    part_a, part_b, stats, acc = run_corner(
+        live, q, g, stats, corner, corner_flags, factor, scale
+    )
+    back_a, back_b = swapped(part_a, 1, 0, sizes), swapped(part_b, 1, 1, sizes)
     grads = functools.partial(run_grads, live, q, g, stats)
-    low = jnp.bfloat16
-    part_up, part_down, acc = grads(corner, corner_flags, None, factor, scale, low)
-    back_down = moved(part_up, 1, 1, sizes)
-    back_up = moved(part_down, 1, -1, sizes)
-    side_up, side_down, acc = grads(side, side_flags, acc, factor, scale, low)
-    total_parts = [moved(side_up, 1, 1, sizes), moved(side_down, 1, -1, sizes)]
-    own_up, own_down, own, dq = grads(
-        near, near_flags, acc, factor, scale, jnp.float32, last=True
-    )
-    send_up, send_down = run_relay(own_up, own_down, back_up, back_down)
-    total_parts += [moved(send_up, 0, 1, sizes), moved(send_down, 0, -1, sizes)]
+    side_a, side_b, acc = grads(side, side_flags, acc, factor, scale, jnp.bfloat16)
+    total_parts = [swapped(side_a, 1, 0, sizes), swapped(side_b, 1, 1, sizes)]
+    own_a, own_b, own, dq = grads(near, near_flags, acc, factor, scale, jnp.float32, last=True)
+    send_a, send_b = run_relay(own_a, own_b, back_a, back_b)
+    total_parts += [swapped(send_a, 0, 0, sizes), swapped(send_b, 0, 1, sizes)]
     dk, dv = run_total(own, total_parts)
     return dq.reshape(shape), dk.reshape(shape), dv.reshape(shape)
 

time: 117 us -> 109 us (0.932)
  starting transfers between devices: 36.2 us -> 22.6 us
  waiting for transfers between devices: 35.6 us -> 44.7 us
  Pallas kernels: 40.6 us -> 38.1 us
  local copies, waits for them, and re-layouts: 1.98 us -> 0.1 us
    pallas_call x0 -> x2, Pallas kernels: none -> 16.7 us  [the longest x1 15.4 us: run_corner(): pl.pallas_call(functools.partial(corner_kernel, flags, factor, scale), ou...]
    ppermute x12, starting transfers between devices: 36.2 us -> 22.6 us  [swapped(): return lax.ppermute(x, ('tm', 'height', 'head'), route)]
    pallas_call x3 -> x2, Pallas kernels: 22.1 us -> 11.6 us  [run_grads(): pl.pallas_call(functools.partial(grads_kernel, flags, first, last, factor...]
    ppermute x12, waiting for transfers between devices: 35.6 us -> 44.7 us  [swapped(): return lax.ppermute(x, ('tm', 'height', 'head'), route)]
    pallas_call x5 -> x3, Pallas kernels: 16.7 us -> 7.98 us  [run_stats(): pl.pallas_call(functools.partial(stats_kernel, flags, first, factor), out...]
  transfers between devices with their start and end apart: 12 -> 12, of which waited for: 7 -> 8; matrix products, arithmetic and copies ran while one was open for 2% -> 0% of each run, Pallas kernels for 22% -> 20%
where the time goes in v4:
time: 109 us; the launch traced here: 108 us
  waiting for transfers between devices  44.7 us (41%)
  Pallas kernels  38.1 us (35%)
  starting transfers between devices  22.6 us (21%)
  other arithmetic  1.26 us (1%)
    ppermute x12, waiting for transfers between devices, swapped(): return lax.ppermute(x, ('tm', 'height', 'head'), route)  44.7 us
    ppermute x12, starting transfers between devices, swapped(): return lax.ppermute(x, ('tm', 'height', 'head'), route)  22.6 us
    pallas_call x1, Pallas kernels, run_corner(): pl.pallas_call(functools.partial(corner_kernel, flags, factor, scale), ou...  15.4 us
    pallas_call x2, Pallas kernels, run_grads(): pl.pallas_call(functools.partial(grads_kernel, flags, first, last, factor...  11.6 us
    pallas_call x3, Pallas kernels, run_stats(): pl.pallas_call(functools.partial(stats_kernel, flags, first, factor), out...  7.98 us
  transfers between devices with their start and end apart: 12, of which 8 were waited for; matrix products, arithmetic and copies ran while one was open for 0% of the time, Pallas kernels for 20%

profile of v4, /device:TPU:98, one launch (start us, length us, event | category | flops | bytes accessed | tf_op | source)
XLA Modules:
  0.0 107.6 jit_solution(13353112847224573661)
XLA Ops:
  0.6 0.0 copy-start.1
  0.6 0.0 copy-start
  0.7 1.3 %maximum_bitcast_fusion.refs_0_.refs_2_ = bf16[1,2,3,512,128]{4,3,2,1,0:T(8,128)(2,1)S(1)} fusion(bf16[1,3,512,128]{3,2,1,0:T(8,128)(2,1)} %bitcast.29, bf16[1,3,512,128]{3,2,1,0:T(8,128)(2,1)} %bitcast.30), kind=kLoop, calls=%fused_computation | loop fusion | flops 393216 | bytes 1572864 | tf_op jit(solution)/shard_map/broadcast_in_dim | solution.py:277
  1.9 3.7 %collective-permute-start.3 = (bf16[1,2,3,512,128]{4,3,2,1,0:T(8,128)(2,1)S(1)}, bf16[1,2,3,512,128]{4,3,2,1,0:T(8,128)(2,1)S(1)}, u32[]{:S(2)}, u32[]{:S(2)}) collective-permute-start(bf16[1,2,3,512,128]{4,3,2,1,0:T(8,128)(2,1)S(1)} %maximum_bitcast_fusion.refs_0_.refs_2_), channel_id=1, source_target_pairs={{5,9},{7,11},{9,5},{11,7},{16,32},{18,34},{20,36},{21,25},{22,38},... | collective-permute-start | bytes 2359304 | tf_op jit(solution)/shard_map/ppermute | solution.py:267
  5.7 0.1 collective-permute-start.2
  5.8 0.1 stack.46.live
  5.9 0.0 copy-done.1
  5.9 0.0 copy-done
  5.9 1.8 %stats.3.refs_2_ = f32[3,3,1,512]{3,2,1,0:T(1,128)S(1)} custom-call(s32[8]{0:T(128)S(1)} %stack.46.live, bf16[3,512,128]{2,1,0:T(8,128)(2,1)S(1)} %bitcast.17, bf16[3,512,128]{2,1,0:T(8,128)(2,1)S(1)} %bitcast.23, bf16[1,2,3,512,128]{4,3,2,1,0:T(8,128)(2,1)S(1)} %maximum_bitcast_fusion.refs_0_.refs_2_), custom_call_target="tpu_custom_call" | custom-call | flops 1000 | bytes 1000 | tf_op jit(solution)/shard_map/stats/pallas_call | solution.py:156
  7.7 3.4 %collective-permute-start.1 = (bf16[1,2,3,512,128]{4,3,2,1,0:T(8,128)(2,1)S(1)}, bf16[1,2,3,512,128]{4,3,2,1,0:T(8,128)(2,1)S(1)}, u32[]{:S(2)}, u32[]{:S(2)}) collective-permute-start(bf16[1,2,3,512,128]{4,3,2,1,0:T(8,128)(2,1)S(1)} %maximum_bitcast_fusion.refs_0_.refs_2_), channel_id=1, source_target_pairs={{4,8},{6,10},{8,4},{10,6},{17,33},{19,35},{20,24},{21,37},{22,26},... | collective-permute-start | bytes 2359304 | tf_op jit(solution)/shard_map/ppermute | solution.py:267
  11.1 0.1 collective-permute-start
  11.2 12.5 %collective-permute-done.3.refs_1_.b_ref = bf16[1,2,3,512,128]{4,3,2,1,0:T(8,128)(2,1)S(1)} collective-permute-done((bf16[1,2,3,512,128]{4,3,2,1,0:T(8,128)(2,1)S(1)}, bf16[1,2,3,512,128]{4,3,2,1,0:T(8,128)(2,1)S(1)}, u32[]{:S(2)}, u32[]{:S(2)}) %collective-permute-start.3) | collective-permute-done | bytes 786464 | tf_op jit(solution)/shard_map/ppermute | solution.py:267
  23.7 0.0 collective-permute-done.2.refs_0_.a_ref
  23.7 1.3 %join.1 = bf16[2,2,3,512,128]{4,3,2,1,0:T(8,128)(2,1)} custom-call(bf16[1,2,3,512,128]{4,3,2,1,0:T(8,128)(2,1)S(1)} %collective-permute-done.2.refs_0_.a_ref, bf16[1,2,3,512,128]{4,3,2,1,0:T(8,128)(2,1)S(1)} %collective-permute-done.3.refs_1_.b_ref), custom_call_target="tpu_custom_call" | custom-call | flops 1000 | bytes 1000 | tf_op jit(solution)/shard_map/join/pallas_call | solution.py:196
  25.0 4.3 %collective-permute-start.5 = (bf16[2,2,3,512,128]{4,3,2,1,0:T(8,128)(2,1)}, bf16[2,2,3,512,128]{4,3,2,1,0:T(8,128)(2,1)}, u32[]{:S(2)}, u32[]{:S(2)}) collective-permute-start(bf16[2,2,3,512,128]{4,3,2,1,0:T(8,128)(2,1)} %join.1), channel_id=1, source_target_pairs={{4,8},{6,10},{8,4},{10,6},{17,33},{19,35},{20,24},{21,37},{22,26},... | collective-permute-start | bytes 4718600 | tf_op jit(solution)/shard_map/ppermute | solution.py:267
  29.4 0.3 collective-permute-start.4
  29.6 3.1 %stats.4.refs_2_ = f32[3,3,1,512]{3,2,1,0:T(1,128)S(1)} custom-call(s32[8]{0:T(128)S(1)} %stack.46.live, bf16[3,512,128]{2,1,0:T(8,128)(2,1)S(1)} %bitcast.18, bf16[3,512,128]{2,1,0:T(8,128)(2,1)S(1)} %bitcast.24, bf16[1,2,3,512,128]{4,3,2,1,0:T(8,128)(2,1)S(1)} %collective-permute-done.2.refs_0_.a_ref, ...), custom_call_target="tpu_custom_call" | custom-call | flops 1000 | bytes 1000 | tf_op jit(solution)/shard_map/stats/pallas_call | solution.py:156
  32.7 0.0 collective-permute-done.1.refs_1_
  32.7 0.0 collective-permute-done.refs_0_
  32.8 3.1 %stats.5.st_ref = f32[3,3,1,512]{3,2,1,0:T(1,128)S(1)} custom-call(s32[8]{0:T(128)S(1)} %stack.46.live, bf16[3,512,128]{2,1,0:T(8,128)(2,1)S(1)} %bitcast.19, bf16[3,512,128]{2,1,0:T(8,128)(2,1)S(1)} %bitcast.25, bf16[1,2,3,512,128]{4,3,2,1,0:T(8,128)(2,1)S(1)} %collective-permute-done.refs_0_, ...), custom_call_target="tpu_custom_call" | custom-call | flops 19999999655936 | bytes 1000 | tf_op jit(solution)/shard_map/stats/pallas_call | solution.py:156
  35.9 12.2 %collective-permute-done.5.refs_1_ = bf16[2,2,3,512,128]{4,3,2,1,0:T(8,128)(2,1)} collective-permute-done((bf16[2,2,3,512,128]{4,3,2,1,0:T(8,128)(2,1)}, bf16[2,2,3,512,128]{4,3,2,1,0:T(8,128)(2,1)}, u32[]{:S(2)}, u32[]{:S(2)}) %collective-permute-start.5) | collective-permute-done | bytes 1572896 | tf_op jit(solution)/shard_map/ppermute | solution.py:267
  48.1 2.3 %collective-permute-done.4.refs_0_ = bf16[2,2,3,512,128]{4,3,2,1,0:T(8,128)(2,1)} collective-permute-done((bf16[2,2,3,512,128]{4,3,2,1,0:T(8,128)(2,1)}, bf16[2,2,3,512,128]{4,3,2,1,0:T(8,128)(2,1)}, u32[]{:S(2)}, u32[]{:S(2)}) %collective-permute-start.4) | collective-permute-done | bytes 1572896 | tf_op jit(solution)/shard_map/ppermute | solution.py:267
  50.4 15.4 %corner.1 = (bf16[2,2,3,512,128]{4,3,2,1,0:T(8,128)(2,1)S(1)}, bf16[2,2,3,512,128]{4,3,2,1,0:T(8,128)(2,1)S(1)}, f32[3,3,1,512]{3,2,1,0:T(1,128)S(1)}, f32[3,128,512]{2,1,0:T(8,128)S(1)}) custom-call(s32[8]{0:T(128)S(1)} %stack.46.live, bf16[3,512,128]{2,1,0:T(8,128)(2,1)S(1)} %bitcast.20, bf16[3,512,128]{2,1,0:T(8,128)(2,1)S(1)} %bitcast.26, ...), custom_call_target="tpu_custom_call" | custom-call | flops 1000 | bytes 1000 | tf_op jit(solution)/shard_map/corner/pallas_call | solution.py:140
  65.8 0.1 collective-permute-start.8
  65.9 2.3 %collective-permute-start.9 = (bf16[2,2,3,512,128]{4,3,2,1,0:T(8,128)(2,1)S(1)}, bf16[2,2,3,512,128]{4,3,2,1,0:T(8,128)(2,1)S(1)}, u32[]{:S(2)}, u32[]{:S(2)}) collective-permute-start(bf16[2,2,3,512,128]{4,3,2,1,0:T(8,128)(2,1)S(1)} %get-tuple-element.32), channel_id=1, source_target_pairs={{4,8},{6,10},{8,4},{10,6},{17,33},{19,35},{20,24},{21,37},{22,26},... | collective-permute-start | bytes 4718600 | tf_op jit(solution)/shard_map/ppermute | solution.py:267
  68.2 4.5 %grads.2 = (bf16[1,2,3,512,128]{4,3,2,1,0:T(8,128)(2,1)S(1)}, bf16[1,2,3,512,128]{4,3,2,1,0:T(8,128)(2,1)S(1)}, f32[3,128,512]{2,1,0:T(8,128)S(1)}) custom-call(s32[8]{0:T(128)S(1)} %stack.46.live, bf16[3,512,128]{2,1,0:T(8,128)(2,1)S(1)} %bitcast.21, bf16[3,512,128]{2,1,0:T(8,128)(2,1)S(1)} %bitcast.27, ...), custom_call_target="tpu_custom_call", output_to_operand_aliasing={{2}: (6, {})} | custom-call | flops 1000 | bytes 1000 | tf_op jit(solution)/shard_map/grads/pallas_call | solution.py:178
  72.7 0.6 collective-permute-start.6
  73.3 3.4 %collective-permute-start.7 = (bf16[1,2,3,512,128]{4,3,2,1,0:T(8,128)(2,1)S(1)}, bf16[1,2,3,512,128]{4,3,2,1,0:T(8,128)(2,1)S(1)}, u32[]{:S(2)}, u32[]{:S(2)}) collective-permute-start(bf16[1,2,3,512,128]{4,3,2,1,0:T(8,128)(2,1)S(1)} %get-tuple-element.28), channel_id=1, source_target_pairs={{4,8},{6,10},{8,4},{10,6},{17,33},{19,35},{20,24},{21,37},{22,26},... | collective-permute-start | bytes 2359304 | tf_op jit(solution)/shard_map/ppermute | solution.py:267
  76.6 7.1 %grads.3 = (f32[1,2,3,512,128]{4,3,2,1,0:T(8,128)S(1)}, f32[1,2,3,512,128]{4,3,2,1,0:T(8,128)S(1)}, f32[1,2,3,512,128]{4,3,2,1,0:T(8,128)S(1)}, bf16[3,512,128]{2,1,0:T(8,128)(2,1)}) custom-call(s32[8]{0:T(128)S(1)} %stack.46.live, bf16[3,512,128]{2,1,0:T(8,128)(2,1)S(1)} %bitcast.22, bf16[3,512,128]{2,1,0:T(8,128)(2,1)S(1)} %bitcast.28, ...), custom_call_target="tpu_custom_call" | custom-call | flops 1000 | bytes 1000 | tf_op jit(solution)/shard_map/grads/pallas_call | solution.py:178
  83.7 2.6 %collective-permute-done.8.from_a = bf16[2,2,3,512,128]{4,3,2,1,0:T(8,128)(2,1)S(1)} collective-permute-done((bf16[2,2,3,512,128]{4,3,2,1,0:T(8,128)(2,1)S(1)}, bf16[2,2,3,512,128]{4,3,2,1,0:T(8,128)(2,1)S(1)}, u32[]{:S(2)}, u32[]{:S(2)}) %collective-permute-start.8) | collective-permute-done | bytes 1572896 | tf_op jit(solution)/shard_map/ppermute | solution.py:267
  86.3 1.9 %collective-permute-done.9.from_b = bf16[2,2,3,512,128]{4,3,2,1,0:T(8,128)(2,1)S(1)} collective-permute-done((bf16[2,2,3,512,128]{4,3,2,1,0:T(8,128)(2,1)S(1)}, bf16[2,2,3,512,128]{4,3,2,1,0:T(8,128)(2,1)S(1)}, u32[]{:S(2)}, u32[]{:S(2)}) %collective-permute-start.9) | collective-permute-done | bytes 1572896 | tf_op jit(solution)/shard_map/ppermute | solution.py:267
  88.2 0.5 relay.1
  88.7 0.1 collective-permute-start.10
  88.8 4.3 %collective-permute-start.11 = (bf16[1,2,3,512,128]{4,3,2,1,0:T(8,128)(2,1)S(1)}, bf16[1,2,3,512,128]{4,3,2,1,0:T(8,128)(2,1)S(1)}, u32[]{:S(2)}, u32[]{:S(2)}) collective-permute-start(bf16[1,2,3,512,128]{4,3,2,1,0:T(8,128)(2,1)S(1)} %get-tuple-element.34), channel_id=1, source_target_pairs={{5,9},{7,11},{9,5},{11,7},{16,32},{18,34},{20,36},{21,25},{22,38},... | collective-permute-start | bytes 2359304 | tf_op jit(solution)/shard_map/ppermute | solution.py:267
  93.2 8.1 %collective-permute-done.6.refs_0_ = bf16[1,2,3,512,128]{4,3,2,1,0:T(8,128)(2,1)S(1)} collective-permute-done((bf16[1,2,3,512,128]{4,3,2,1,0:T(8,128)(2,1)S(1)}, bf16[1,2,3,512,128]{4,3,2,1,0:T(8,128)(2,1)S(1)}, u32[]{:S(2)}, u32[]{:S(2)}) %collective-permute-start.6) | collective-permute-done | bytes 786464 | tf_op jit(solution)/shard_map/ppermute | solution.py:267
  101.2 1.3 %collective-permute-done.7.refs_1_ = bf16[1,2,3,512,128]{4,3,2,1,0:T(8,128)(2,1)S(1)} collective-permute-done((bf16[1,2,3,512,128]{4,3,2,1,0:T(8,128)(2,1)S(1)}, bf16[1,2,3,512,128]{4,3,2,1,0:T(8,128)(2,1)S(1)}, u32[]{:S(2)}, u32[]{:S(2)}) %collective-permute-start.7) | collective-permute-done | bytes 786464 | tf_op jit(solution)/shard_map/ppermute | solution.py:267
  102.5 0.0 collective-permute-done.10.refs_2_
  102.5 3.8 %collective-permute-done.11.refs_3_ = bf16[1,2,3,512,128]{4,3,2,1,0:T(8,128)(2,1)S(1)} collective-permute-done((bf16[1,2,3,512,128]{4,3,2,1,0:T(8,128)(2,1)S(1)}, bf16[1,2,3,512,128]{4,3,2,1,0:T(8,128)(2,1)S(1)}, u32[]{:S(2)}, u32[]{:S(2)}) %collective-permute-start.11) | collective-permute-done | bytes 786464 | tf_op jit(solution)/shard_map/ppermute | solution.py:267
  106.3 1.2 %total.1 = (bf16[3,512,128]{2,1,0:T(8,128)(2,1)}, bf16[3,512,128]{2,1,0:T(8,128)(2,1)}) custom-call(f32[1,2,3,512,128]{4,3,2,1,0:T(8,128)S(1)} %get-tuple-element.26.own, bf16[1,2,3,512,128]{4,3,2,1,0:T(8,128)(2,1)S(1)} %collective-permute-done.6.refs_0_, bf16[1,2,3,512,128]{4,3,2,1,0:T(8,128)(2,1)S(1)} %collective-permute-done.7.refs_1_, ...), custom_call_target="tpu_custom_call" | custom-call | flops 1000 | bytes 1000 | tf_op jit(solution)/shard_map/total/pallas_call | solution.py:238
Async XLA Ops:
  0.6 5.3 %copy-start.1 = (bf16[3,4,8,16,128]{4,3,2,1,0:T(8,128)(2,1)S(1)}, bf16[3,4,8,16,128]{4,3,2,1,0:T(8,128)(2,1)}, u32[]{:S(2)}) copy-start(bf16[3,4,8,16,128]{4,3,2,1,0:T(8,128)(2,1)} %param.7) | copy-start | bytes 1179652
  0.6 5.3 %copy-start = (bf16[3,4,8,16,128]{4,3,2,1,0:T(8,128)(2,1)S(1)}, bf16[3,4,8,16,128]{4,3,2,1,0:T(8,128)(2,1)}, u32[]{:S(2)}) copy-start(bf16[3,4,8,16,128]{4,3,2,1,0:T(8,128)(2,1)} %param.4) | copy-start | bytes 1179652
  1.9 21.8 %collective-permute-start.3 = (bf16[1,2,3,512,128]{4,3,2,1,0:T(8,128)(2,1)S(1)}, bf16[1,2,3,512,128]{4,3,2,1,0:T(8,128)(2,1)S(1)}, u32[]{:S(2)}, u32[]{:S(2)}) collective-permute-start(bf16[1,2,3,512,128]{4,3,2,1,0:T(8,128)(2,1)S(1)} %maximum_bitcast_fusion.refs_0_.refs_2_), channel_id=1, source_target_pairs={{5,9},{7,11},{9,5},{11,7},{16,32},{18,34},{20,36},{21,25},{22,38},... | collective-permute-start | bytes 2359304 | tf_op jit(solution)/shard_map/ppermute | solution.py:267
  5.7 18.1 %collective-permute-start.2 = (bf16[1,2,3,512,128]{4,3,2,1,0:T(8,128)(2,1)S(1)}, bf16[1,2,3,512,128]{4,3,2,1,0:T(8,128)(2,1)S(1)}, u32[]{:S(2)}, u32[]{:S(2)}) collective-permute-start(bf16[1,2,3,512,128]{4,3,2,1,0:T(8,128)(2,1)S(1)} %maximum_bitcast_fusion.refs_0_.refs_2_), channel_id=1, source_target_pairs={{0,16},{1,5},{2,18},{3,7},{4,20},{5,1},{6,22},{7,3},{8,24},{9,13},... | collective-permute-start | bytes 2359304 | tf_op jit(solution)/shard_map/ppermute | solution.py:267
  7.7 25.0 %collective-permute-start.1 = (bf16[1,2,3,512,128]{4,3,2,1,0:T(8,128)(2,1)S(1)}, bf16[1,2,3,512,128]{4,3,2,1,0:T(8,128)(2,1)S(1)}, u32[]{:S(2)}, u32[]{:S(2)}) collective-permute-start(bf16[1,2,3,512,128]{4,3,2,1,0:T(8,128)(2,1)S(1)} %maximum_bitcast_fusion.refs_0_.refs_2_), channel_id=1, source_target_pairs={{4,8},{6,10},{8,4},{10,6},{17,33},{19,35},{20,24},{21,37},{22,26},... | collective-permute-start | bytes 2359304 | tf_op jit(solution)/shard_map/ppermute | solution.py:267
  11.1 21.6 %collective-permute-start = (bf16[1,2,3,512,128]{4,3,2,1,0:T(8,128)(2,1)S(1)}, bf16[1,2,3,512,128]{4,3,2,1,0:T(8,128)(2,1)S(1)}, u32[]{:S(2)}, u32[]{:S(2)}) collective-permute-start(bf16[1,2,3,512,128]{4,3,2,1,0:T(8,128)(2,1)S(1)} %maximum_bitcast_fusion.refs_0_.refs_2_), channel_id=1, source_target_pairs={{0,4},{1,17},{2,6},{3,19},{4,0},{5,21},{6,2},{7,23},{8,12},{9,25},... | collective-permute-start | bytes 2359304 | tf_op jit(solution)/shard_map/ppermute | solution.py:267
  25.0 23.1 %collective-permute-start.5 = (bf16[2,2,3,512,128]{4,3,2,1,0:T(8,128)(2,1)}, bf16[2,2,3,512,128]{4,3,2,1,0:T(8,128)(2,1)}, u32[]{:S(2)}, u32[]{:S(2)}) collective-permute-start(bf16[2,2,3,512,128]{4,3,2,1,0:T(8,128)(2,1)} %join.1), channel_id=1, source_target_pairs={{4,8},{6,10},{8,4},{10,6},{17,33},{19,35},{20,24},{21,37},{22,26},... | collective-permute-start | bytes 4718600 | tf_op jit(solution)/shard_map/ppermute | solution.py:267
  29.4 21.0 %collective-permute-start.4 = (bf16[2,2,3,512,128]{4,3,2,1,0:T(8,128)(2,1)}, bf16[2,2,3,512,128]{4,3,2,1,0:T(8,128)(2,1)}, u32[]{:S(2)}, u32[]{:S(2)}) collective-permute-start(bf16[2,2,3,512,128]{4,3,2,1,0:T(8,128)(2,1)} %join.1), channel_id=1, source_target_pairs={{0,4},{1,17},{2,6},{3,19},{4,0},{5,21},{6,2},{7,23},{8,12},{9,25},... | collective-permute-start | bytes 4718600 | tf_op jit(solution)/shard_map/ppermute | solution.py:267
  65.8 20.5 %collective-permute-start.8 = (bf16[2,2,3,512,128]{4,3,2,1,0:T(8,128)(2,1)S(1)}, bf16[2,2,3,512,128]{4,3,2,1,0:T(8,128)(2,1)S(1)}, u32[]{:S(2)}, u32[]{:S(2)}) collective-permute-start(bf16[2,2,3,512,128]{4,3,2,1,0:T(8,128)(2,1)S(1)} %get-tuple-element.31), channel_id=1, source_target_pairs={{0,4},{1,17},{2,6},{3,19},{4,0},{5,21},{6,2},{7,23},{8,12},{9,25},... | collective-permute-start | bytes 4718600 | tf_op jit(solution)/shard_map/ppermute | solution.py:267
  65.9 22.3 %collective-permute-start.9 = (bf16[2,2,3,512,128]{4,3,2,1,0:T(8,128)(2,1)S(1)}, bf16[2,2,3,512,128]{4,3,2,1,0:T(8,128)(2,1)S(1)}, u32[]{:S(2)}, u32[]{:S(2)}) collective-permute-start(bf16[2,2,3,512,128]{4,3,2,1,0:T(8,128)(2,1)S(1)} %get-tuple-element.32), channel_id=1, source_target_pairs={{4,8},{6,10},{8,4},{10,6},{17,33},{19,35},{20,24},{21,37},{22,26},... | collective-permute-start | bytes 4718600 | tf_op jit(solution)/shard_map/ppermute | solution.py:267
  72.7 28.5 %collective-permute-start.6 = (bf16[1,2,3,512,128]{4,3,2,1,0:T(8,128)(2,1)S(1)}, bf16[1,2,3,512,128]{4,3,2,1,0:T(8,128)(2,1)S(1)}, u32[]{:S(2)}, u32[]{:S(2)}) collective-permute-start(bf16[1,2,3,512,128]{4,3,2,1,0:T(8,128)(2,1)S(1)} %get-tuple-element.27), channel_id=1, source_target_pairs={{0,4},{1,17},{2,6},{3,19},{4,0},{5,21},{6,2},{7,23},{8,12},{9,25},... | collective-permute-start | bytes 2359304 | tf_op jit(solution)/shard_map/ppermute | solution.py:267
  73.3 29.2 %collective-permute-start.7 = (bf16[1,2,3,512,128]{4,3,2,1,0:T(8,128)(2,1)S(1)}, bf16[1,2,3,512,128]{4,3,2,1,0:T(8,128)(2,1)S(1)}, u32[]{:S(2)}, u32[]{:S(2)}) collective-permute-start(bf16[1,2,3,512,128]{4,3,2,1,0:T(8,128)(2,1)S(1)} %get-tuple-element.28), channel_id=1, source_target_pairs={{4,8},{6,10},{8,4},{10,6},{17,33},{19,35},{20,24},{21,37},{22,26},... | collective-permute-start | bytes 2359304 | tf_op jit(solution)/shard_map/ppermute | solution.py:267
  88.7 13.7 %collective-permute-start.10 = (bf16[1,2,3,512,128]{4,3,2,1,0:T(8,128)(2,1)S(1)}, bf16[1,2,3,512,128]{4,3,2,1,0:T(8,128)(2,1)S(1)}, u32[]{:S(2)}, u32[]{:S(2)}) collective-permute-start(bf16[1,2,3,512,128]{4,3,2,1,0:T(8,128)(2,1)S(1)} %get-tuple-element.33), channel_id=1, source_target_pairs={{0,16},{1,5},{2,18},{3,7},{4,20},{5,1},{6,22},{7,3},{8,24},{9,13},... | collective-permute-start | bytes 2359304 | tf_op jit(solution)/shard_map/ppermute | solution.py:267
  88.8 17.5 %collective-permute-start.11 = (bf16[1,2,3,512,128]{4,3,2,1,0:T(8,128)(2,1)S(1)}, bf16[1,2,3,512,128]{4,3,2,1,0:T(8,128)(2,1)S(1)}, u32[]{:S(2)}, u32[]{:S(2)}) collective-permute-start(bf16[1,2,3,512,128]{4,3,2,1,0:T(8,128)(2,1)S(1)} %get-tuple-element.34), channel_id=1, source_target_pairs={{5,9},{7,11},{9,5},{11,7},{16,32},{18,34},{20,36},{21,25},{22,38},... | collective-permute-start | bytes 2359304 | tf_op jit(solution)/shard_map/ppermute | solution.py:267

commit v5 on v4

v5 whole, which is shorter than its diff:
```python
import functools
import math

import jax
import jax.numpy as jnp
from jax import lax
from jax.experimental import pallas as pl
from jax.experimental.pallas import tpu as pltpu
from jax.sharding import PartitionSpec as P

KEY_CHUNK_STATS = 128
VMEM_LIMIT = 16 << 20
VMEM = pl.BlockSpec(memory_space=pltpu.VMEM)
SMEM = pl.BlockSpec(memory_space=pltpu.SMEM)


def contract(a, b, dim_a, dim_b):
    return lax.dot_general(
        a, b, (((dim_a,), (dim_b,)), ((), ())), preferred_element_type=jnp.float32
    )


def shown(live, flag, value, other):
    return value if flag is None else jnp.where(live[flag] > 0, value, other)


def by_eight(x):
    return x.reshape(x.shape[0] // 8, 8, x.shape[1])


def stats_of(kv_refs, flags, factor, live, h, q, g, carried):
    top, total, dot = carried
    for kv_ref, kv_flags in zip(kv_refs, flags):
        for block, flag in enumerate(kv_flags):
            for start in range(0, kv_ref.shape[3], KEY_CHUNK_STATS):
                rows = slice(start, start + KEY_CHUNK_STATS)
                s = by_eight(contract(kv_ref[block, 0, h, rows], q, 1, 1))
                dp = by_eight(contract(kv_ref[block, 1, h, rows], g, 1, 1))
                new = jnp.maximum(top, shown(live, flag, jnp.max(s, axis=0), -jnp.inf))
                keep = jnp.exp2((top - new) * factor)
                e = jnp.exp2((s - new[None]) * factor)
                total = total * keep + shown(live, flag, jnp.sum(e, axis=0), 0.0)
                dot = dot * keep + shown(live, flag, jnp.sum(e * dp, axis=0), 0.0)
                top = new
    return top, total, dot


def stats_kernel(flags, first, factor, live, q_ref, g_ref, *refs):
    kv_refs, out_ref = refs[: len(flags)], refs[-1]
    for h in range(q_ref.shape[0]):
        if first:
            zero = jnp.zeros(out_ref.shape[2:], jnp.float32)
            carried = (jnp.full_like(zero, -jnp.inf), zero, zero)
        else:
            carried = tuple(refs[len(flags)][h, i] for i in range(3))
        result = stats_of(kv_refs, flags, factor, live, h, q_ref[h], g_ref[h], carried)
        out_ref[h, 0], out_ref[h, 1], out_ref[h, 2] = result


def grads_of(kv_refs, out_refs, flags, factor, scale, live, h, q, g, log_total, delta, acc):
    for kv_ref, out_ref, kv_flags in zip(kv_refs, out_refs, flags):
        for block, flag in enumerate(kv_flags):
            low = shown(live, flag, log_total, jnp.inf)
            k = kv_ref[block, 0, h]
            s = contract(k, q, 1, 1)
            dp = contract(kv_ref[block, 1, h], g, 1, 1)
            p = jnp.exp2(by_eight(s) * factor - low[None])
            ds = (p * (by_eight(dp) - delta[None])).reshape(s.shape).astype(jnp.bfloat16)
            dv = contract(p.reshape(s.shape).astype(jnp.bfloat16), g, 1, 0)
            dk = contract(ds, q, 1, 0) * scale
            acc = acc + contract(k, ds, 0, 0)
            out_ref[block, 0, h] = dk.astype(out_ref.dtype)
            out_ref[block, 1, h] = dv.astype(out_ref.dtype)
    return acc


def corner_kernel(flags, factor, scale, live, q_ref, g_ref, st_ref, *refs):
    count = len(flags)
    kv_refs, out_refs = refs[:count], refs[count : 2 * count]
    end_ref, acc_ref = refs[2 * count :]
    for h in range(q_ref.shape[0]):
        q, g = q_ref[h], g_ref[h]
        carried = tuple(st_ref[h, i] for i in range(3))
        top, total, dot = stats_of(kv_refs, flags, factor, live, h, q, g, carried)
        peak = jnp.max(top, axis=0, keepdims=True)
        share = jnp.exp2((top - peak) * factor)
        total = jnp.sum(share * total, axis=0, keepdims=True)
        dot = jnp.sum(share * dot, axis=0, keepdims=True)
        end_ref[h, 0] = jnp.broadcast_to(peak * factor + jnp.log2(total), top.shape)
        end_ref[h, 1] = jnp.broadcast_to(dot / total, top.shape)
        acc = jnp.zeros((q.shape[1], q.shape[0]), jnp.float32)
        acc_ref[h] = grads_of(
            kv_refs, out_refs, flags, factor, scale, live, h, q, g,
            end_ref[h, 0], end_ref[h, 1], acc,
        )


def grads_kernel(flags, last, factor, scale, live, q_ref, g_ref, end_ref, *refs):
    count = len(flags)
    kv_refs, acc_in = refs[:count], refs[count]
    out_refs, acc_ref = refs[count + 1 : 2 * count + 1], refs[2 * count + 1]
    for h in range(q_ref.shape[0]):
        acc = grads_of(
            kv_refs, out_refs, flags, factor, scale, live, h, q_ref[h], g_ref[h],
            end_ref[h, 0], end_ref[h, 1], acc_in[h],
        )
        if last:
            acc_ref[h] = (acc * scale).T.astype(jnp.bfloat16)
        else:
            acc_ref[h] = acc


def run_corner(live, q, g, stats, blocks, flags, factor, scale):
    heads, rows, depth = q.shape
    out_shape = [jax.ShapeDtypeStruct(b.shape, jnp.bfloat16) for b in blocks]
    out_shape.append(jax.ShapeDtypeStruct((heads, 2, 8, rows), jnp.float32))
    out_shape.append(jax.ShapeDtypeStruct((heads, depth, rows), jnp.float32))
    return pl.pallas_call(
        functools.partial(corner_kernel, flags, factor, scale),
        out_shape=out_shape,
        in_specs=[SMEM] + [VMEM] * (3 + len(blocks)),
        out_specs=[VMEM] * len(out_shape),
        cost_estimate=pl.CostEstimate(flops=1000, bytes_accessed=1000, transcendentals=0),
        compiler_params=pltpu.CompilerParams(vmem_limit_bytes=VMEM_LIMIT),
        name="corner",
    )(live, q, g, stats, *blocks)


def run_stats(live, q, g, blocks, flags, stats, factor, cost=1000):
    heads, rows, _ = q.shape
    first = stats is None
    args = [live, q, g, *blocks] + ([] if first else [stats])
    return pl.pallas_call(
        functools.partial(stats_kernel, flags, first, factor),
        out_shape=jax.ShapeDtypeStruct((heads, 3, 8, rows), jnp.float32),
        in_specs=[SMEM] + [VMEM] * (len(args) - 1),
        out_specs=VMEM,
        cost_estimate=pl.CostEstimate(flops=cost, bytes_accessed=1000, transcendentals=0),
        compiler_params=pltpu.CompilerParams(vmem_limit_bytes=VMEM_LIMIT),
        name="stats",
    )(*args)


def run_grads(live, q, g, ends, blocks, flags, acc, factor, scale, part, last=False):
    args = [live, q, g, ends, *blocks, acc]
    end = jax.ShapeDtypeStruct(*((q.shape, q.dtype) if last else (acc.shape, acc.dtype)))
    return pl.pallas_call(
        functools.partial(grads_kernel, flags, last, factor, scale),
        out_shape=[jax.ShapeDtypeStruct(b.shape, part) for b in blocks] + [end],
        in_specs=[SMEM] + [VMEM] * (len(args) - 1),
        out_specs=[VMEM] * (len(blocks) + 1),
        input_output_aliases={} if last else {len(args) - 1: len(blocks)},
        cost_estimate=pl.CostEstimate(flops=1000, bytes_accessed=1000, transcendentals=0),
        compiler_params=pltpu.CompilerParams(vmem_limit_bytes=VMEM_LIMIT),
        name="grads",
    )(*args)


def join_kernel(a_ref, b_ref, out_ref):
    out_ref[0] = a_ref[0]
    out_ref[1] = b_ref[0]


def run_join(a, b):
    return pl.pallas_call(
        join_kernel,
        out_shape=jax.ShapeDtypeStruct((2,) + a.shape[1:], a.dtype),
        in_specs=[VMEM] * 2,
        out_specs=VMEM,
        cost_estimate=pl.CostEstimate(flops=1000, bytes_accessed=1000, transcendentals=0),
        compiler_params=pltpu.CompilerParams(vmem_limit_bytes=VMEM_LIMIT),
        name="join",
    )(a, b)


def relay_kernel(own_a, own_b, from_a, from_b, out_a, out_b):
    for block, (own, out) in enumerate(((own_a, out_a), (own_b, out_b))):
        out[0] = (
            own[0]
            + from_a[block].astype(jnp.float32)
            + from_b[block].astype(jnp.float32)
        ).astype(out.dtype)


def run_relay(own_a, own_b, from_a, from_b):
    return pl.pallas_call(
        relay_kernel,
        out_shape=[jax.ShapeDtypeStruct(own_a.shape, jnp.bfloat16)] * 2,
        in_specs=[VMEM] * 4,
        out_specs=[VMEM] * 2,
        cost_estimate=pl.CostEstimate(flops=1000, bytes_accessed=1000, transcendentals=0),
        compiler_params=pltpu.CompilerParams(vmem_limit_bytes=VMEM_LIMIT),
        name="relay",
    )(own_a, own_b, from_a, from_b)


def total_kernel(own, *refs):
    parts, outs = refs[:-2], refs[-2:]
    for which, out in enumerate(outs):
        total = own[0, which]
        for part in parts:
            total = total + part[0, which].astype(jnp.float32)
        out[...] = total.astype(out.dtype)


def run_total(own, parts):
    return pl.pallas_call(
        total_kernel,
        out_shape=[jax.ShapeDtypeStruct(own.shape[2:], jnp.bfloat16)] * 2,
        in_specs=[VMEM] * (1 + len(parts)),
        out_specs=[VMEM] * 2,
        cost_estimate=pl.CostEstimate(flops=1000, bytes_accessed=1000, transcendentals=0),
        compiler_params=pltpu.CompilerParams(vmem_limit_bytes=VMEM_LIMIT),
        name="total",
    )(own, *parts)


def partner(at, pair):
    odd = at % 2
    return at + (1 - 2 * odd) * (1 - 2 * pair)


def swapped(x, stage, pair, sizes):
    frames, rows, heads = sizes
    route = []
    for f in range(frames):
        for r in range(rows):
            for h in range(heads):
                along_rows = (h + stage) % 2
                to_f = f if along_rows else partner(f, pair)
                to_r = partner(r, pair) if along_rows else r
                if 0 <= to_f < frames and 0 <= to_r < rows:
                    route.append(
                        ((f * rows + r) * heads + h, (to_f * rows + to_r) * heads + h)
                    )
    return lax.ppermute(x, ("tm", "height", "head"), route)


def local(query_in, key_in, value_in, out_grad):
    shape = query_in.shape
    heads, depth = shape[0], shape[-1]
    flat = (heads, math.prod(shape[1:4]), depth)
    scale = depth**-0.5
    factor = scale * math.log2(math.e)
    q, g = query_in.reshape(flat), out_grad.reshape(flat)
    kv = jnp.stack([key_in.reshape(flat), value_in.reshape(flat)])[None]
    sizes = tuple(lax.axis_size(a) for a in ("tm", "height", "head"))
    frame, row = lax.axis_index("tm"), lax.axis_index("height")
    frames_first = lax.axis_index("head") % 2 == 0
    place = (jnp.where(frames_first, frame, row), jnp.where(frames_first, row, frame))
    size = (
        jnp.where(frames_first, sizes[0], sizes[1]),
        jnp.where(frames_first, sizes[1], sizes[0]),
    )
    met = [[partner(place[i], pair) for pair in (0, 1)] for i in (0, 1)]
    first, second = [
        [((m >= 0) & (m < size[i])).astype(jnp.int32) for m in met[i]] for i in (0, 1)
    ]
    live = jnp.stack(first + second + [b * a for b in second for a in first])

    first_a, first_b = (swapped(kv, 0, pair, sizes) for pair in (0, 1))
    stats = run_stats(live, q, g, [kv], [[None]], None, factor)
    later, stats, first_a = lax.optimization_barrier((kv, stats, first_a))
    second_a, second_b = (swapped(later, 1, pair, sizes) for pair in (0, 1))
    both = run_join(first_a, first_b)
    corner_a, corner_b = (swapped(both, 1, pair, sizes) for pair in (0, 1))

    near, near_flags = [first_a, first_b, kv], [[0], [1], [None]]
    side, side_flags = [second_a, second_b], [[2], [3]]
    corner, corner_flags = [corner_a, corner_b], [[4, 5], [6, 7]]
    stats = run_stats(live, q, g, near[:2], near_flags[:2], stats, factor)
    stats = run_stats(live, q, g, side, side_flags, stats, factor, cost=20 * 10**12)
    part_a, part_b, ends, acc = run_corner(
        live, q, g, stats, corner, corner_flags, factor, scale
    )
    back_a, back_b = swapped(part_a, 1, 0, sizes), swapped(part_b, 1, 1, sizes)
    grads = functools.partial(run_grads, live, q, g, ends)
    side_a, side_b, acc = grads(side, side_flags, acc, factor, scale, jnp.bfloat16)
    total_parts = [swapped(side_a, 1, 0, sizes), swapped(side_b, 1, 1, sizes)]
    own_a, own_b, own, dq = grads(near, near_flags, acc, factor, scale, jnp.float32, last=True)
    send_a, send_b = run_relay(own_a, own_b, back_a, back_b)
    total_parts += [swapped(send_a, 0, 0, sizes), swapped(send_b, 0, 1, sizes)]
    dk, dv = run_total(own, total_parts)
    return dq.reshape(shape), dk.reshape(shape), dv.reshape(shape)


def solution(mesh):
    spec = P("head", "tm", "height", None, None)
    return jax.shard_map(
        local, mesh=mesh, in_specs=(spec,) * 4, out_specs=(spec,) * 3, check_vma=False
    )
```

time: 109 us -> 104 us (0.954)
  Pallas kernels: 38.1 us -> 34.3 us
  waiting for transfers between devices: 44.7 us -> 41.2 us
  starting transfers between devices: 22.6 us -> 24.9 us
    ppermute x12, waiting for transfers between devices: 44.7 us -> 41.2 us  [swapped(): return lax.ppermute(x, ('tm', 'height', 'head'), route)]
    ppermute x12, starting transfers between devices: 22.6 us -> 24.9 us  [swapped(): return lax.ppermute(x, ('tm', 'height', 'head'), route)]
    pallas_call x1, Pallas kernels: 15.4 us -> 13.2 us  [run_corner(): pl.pallas_call(functools.partial(corner_kernel, flags, factor, scale), ou...]
    pallas_call x3, Pallas kernels: 7.98 us -> 6.49 us  [run_stats(): pl.pallas_call(functools.partial(stats_kernel, flags, first, factor), out...]
  transfers between devices with their start and end apart: 12 -> 12, of which waited for: 8 -> 12; matrix products, arithmetic and copies ran while one was open for 0% -> 0% of each run, Pallas kernels for 20% -> 19%
where the time goes in v5:
time: 104 us; the launch traced here: 103 us
  waiting for transfers between devices  41.2 us (40%)
  Pallas kernels  34.3 us (33%)
  starting transfers between devices  24.9 us (24%)
  other arithmetic  1.26 us (1%)
    ppermute x12, waiting for transfers between devices, swapped(): return lax.ppermute(x, ('tm', 'height', 'head'), route)  41.2 us
    ppermute x12, starting transfers between devices, swapped(): return lax.ppermute(x, ('tm', 'height', 'head'), route)  24.9 us
    pallas_call x1, Pallas kernels, run_corner(): pl.pallas_call(functools.partial(corner_kernel, flags, factor, scale), ou...  13.2 us
    pallas_call x2, Pallas kernels, run_grads(): pl.pallas_call(functools.partial(grads_kernel, flags, last, factor, scale...  11.6 us
    pallas_call x3, Pallas kernels, run_stats(): pl.pallas_call(functools.partial(stats_kernel, flags, first, factor), out...  6.49 us
  transfers between devices with their start and end apart: 12, of which 12 were waited for; matrix products, arithmetic and copies ran while one was open for 0% of the time, Pallas kernels for 19%

profile of v5, /device:TPU:98, one launch (start us, length us, event | category | flops | bytes accessed | tf_op | source)
XLA Modules:
  0.0 102.6 jit_solution(7579201984781712524)
XLA Ops:
  0.6 0.0 copy-start.1
  0.6 0.0 copy-start
  0.7 1.3 %maximum_bitcast_fusion.refs_0_.refs_2_ = bf16[1,2,3,512,128]{4,3,2,1,0:T(8,128)(2,1)S(1)} fusion(bf16[1,3,512,128]{3,2,1,0:T(8,128)(2,1)} %bitcast.29, bf16[1,3,512,128]{3,2,1,0:T(8,128)(2,1)} %bitcast.30), kind=kLoop, calls=%fused_computation | loop fusion | flops 393216 | bytes 1572864 | tf_op jit(solution)/shard_map/broadcast_in_dim | solution.py:246
  1.9 0.5 collective-permute-start
  2.4 5.2 %collective-permute-start.3 = (bf16[1,2,3,512,128]{4,3,2,1,0:T(8,128)(2,1)S(1)}, bf16[1,2,3,512,128]{4,3,2,1,0:T(8,128)(2,1)S(1)}, u32[]{:S(2)}, u32[]{:S(2)}) collective-permute-start(bf16[1,2,3,512,128]{4,3,2,1,0:T(8,128)(2,1)S(1)} %maximum_bitcast_fusion.refs_0_.refs_2_), channel_id=1, source_target_pairs={{5,9},{7,11},{9,5},{11,7},{16,32},{18,34},{20,36},{21,25},{22,38},... | collective-permute-start | bytes 2359304 | tf_op jit(solution)/shard_map/ppermute | solution.py:236
  7.7 0.1 stack.46.live
  7.8 0.0 copy-done.1
  7.8 0.0 copy-done
  7.8 1.6 %stats.3.refs_2_ = f32[3,3,8,512]{3,2,1,0:T(8,128)S(1)} custom-call(s32[8]{0:T(128)S(1)} %stack.46.live, bf16[3,512,128]{2,1,0:T(8,128)(2,1)S(1)} %bitcast.17, bf16[3,512,128]{2,1,0:T(8,128)(2,1)S(1)} %bitcast.23, bf16[1,2,3,512,128]{4,3,2,1,0:T(8,128)(2,1)S(1)} %maximum_bitcast_fusion.refs_0_.refs_2_), custom_call_target="tpu_custom_call" | custom-call | flops 1000 | bytes 1000 | tf_op jit(solution)/shard_map/stats/pallas_call | solution.py:133
  9.4 4.6 %collective-permute-done.refs_0_.a_ref = bf16[1,2,3,512,128]{4,3,2,1,0:T(8,128)(2,1)S(1)} collective-permute-done((bf16[1,2,3,512,128]{4,3,2,1,0:T(8,128)(2,1)S(1)}, bf16[1,2,3,512,128]{4,3,2,1,0:T(8,128)(2,1)S(1)}, u32[]{:S(2)}, u32[]{:S(2)}) %collective-permute-start) | collective-permute-done | bytes 786464 | tf_op jit(solution)/shard_map/ppermute | solution.py:236
  14.0 3.4 %collective-permute-start.2 = (bf16[1,2,3,512,128]{4,3,2,1,0:T(8,128)(2,1)S(1)}, bf16[1,2,3,512,128]{4,3,2,1,0:T(8,128)(2,1)S(1)}, u32[]{:S(2)}, u32[]{:S(2)}) collective-permute-start(bf16[1,2,3,512,128]{4,3,2,1,0:T(8,128)(2,1)S(1)} %maximum_bitcast_fusion.refs_0_.refs_2_), channel_id=1, source_target_pairs={{4,8},{6,10},{8,4},{10,6},{17,33},{19,35},{20,24},{21,37},{22,26},... | collective-permute-start | bytes 2359304 | tf_op jit(solution)/shard_map/ppermute | solution.py:236
  17.4 0.1 collective-permute-start.1
  17.5 2.4 %collective-permute-done.3.refs_1_.b_ref = bf16[1,2,3,512,128]{4,3,2,1,0:T(8,128)(2,1)S(1)} collective-permute-done((bf16[1,2,3,512,128]{4,3,2,1,0:T(8,128)(2,1)S(1)}, bf16[1,2,3,512,128]{4,3,2,1,0:T(8,128)(2,1)S(1)}, u32[]{:S(2)}, u32[]{:S(2)}) %collective-permute-start.3) | collective-permute-done | bytes 786464 | tf_op jit(solution)/shard_map/ppermute | solution.py:236
  19.9 1.3 %join.1 = bf16[2,2,3,512,128]{4,3,2,1,0:T(8,128)(2,1)} custom-call(bf16[1,2,3,512,128]{4,3,2,1,0:T(8,128)(2,1)S(1)} %collective-permute-done.refs_0_.a_ref, bf16[1,2,3,512,128]{4,3,2,1,0:T(8,128)(2,1)S(1)} %collective-permute-done.3.refs_1_.b_ref), custom_call_target="tpu_custom_call" | custom-call | flops 1000 | bytes 1000 | tf_op jit(solution)/shard_map/join/pallas_call | solution.py:165
  21.2 3.4 %collective-permute-start.5 = (bf16[2,2,3,512,128]{4,3,2,1,0:T(8,128)(2,1)}, bf16[2,2,3,512,128]{4,3,2,1,0:T(8,128)(2,1)}, u32[]{:S(2)}, u32[]{:S(2)}) collective-permute-start(bf16[2,2,3,512,128]{4,3,2,1,0:T(8,128)(2,1)} %join.1), channel_id=1, source_target_pairs={{4,8},{6,10},{8,4},{10,6},{17,33},{19,35},{20,24},{21,37},{22,26},... | collective-permute-start | bytes 4718600 | tf_op jit(solution)/shard_map/ppermute | solution.py:236
  24.6 0.3 collective-permute-start.4
  24.8 2.4 %stats.4.refs_2_ = f32[3,3,8,512]{3,2,1,0:T(8,128)S(1)} custom-call(s32[8]{0:T(128)S(1)} %stack.46.live, bf16[3,512,128]{2,1,0:T(8,128)(2,1)S(1)} %bitcast.18, bf16[3,512,128]{2,1,0:T(8,128)(2,1)S(1)} %bitcast.24, bf16[1,2,3,512,128]{4,3,2,1,0:T(8,128)(2,1)S(1)} %collective-permute-done.refs_0_.a_ref, ...), custom_call_target="tpu_custom_call" | custom-call | flops 1000 | bytes 1000 | tf_op jit(solution)/shard_map/stats/pallas_call | solution.py:133
  27.3 0.6 collective-permute-done.2.refs_1_
  27.9 1.6 %collective-permute-done.1.refs_0_ = bf16[1,2,3,512,128]{4,3,2,1,0:T(8,128)(2,1)S(1)} collective-permute-done((bf16[1,2,3,512,128]{4,3,2,1,0:T(8,128)(2,1)S(1)}, bf16[1,2,3,512,128]{4,3,2,1,0:T(8,128)(2,1)S(1)}, u32[]{:S(2)}, u32[]{:S(2)}) %collective-permute-start.1) | collective-permute-done | bytes 786464 | tf_op jit(solution)/shard_map/ppermute | solution.py:236
  29.4 2.5 %stats.5.st_ref = f32[3,3,8,512]{3,2,1,0:T(8,128)S(1)} custom-call(s32[8]{0:T(128)S(1)} %stack.46.live, bf16[3,512,128]{2,1,0:T(8,128)(2,1)S(1)} %bitcast.19, bf16[3,512,128]{2,1,0:T(8,128)(2,1)S(1)} %bitcast.25, bf16[1,2,3,512,128]{4,3,2,1,0:T(8,128)(2,1)S(1)} %collective-permute-done.1.refs_0_, ...), custom_call_target="tpu_custom_call" | custom-call | flops 19999999655936 | bytes 1000 | tf_op jit(solution)/shard_map/stats/pallas_call | solution.py:133
  31.9 12.9 %collective-permute-done.5.refs_1_ = bf16[2,2,3,512,128]{4,3,2,1,0:T(8,128)(2,1)} collective-permute-done((bf16[2,2,3,512,128]{4,3,2,1,0:T(8,128)(2,1)}, bf16[2,2,3,512,128]{4,3,2,1,0:T(8,128)(2,1)}, u32[]{:S(2)}, u32[]{:S(2)}) %collective-permute-start.5) | collective-permute-done | bytes 1572896 | tf_op jit(solution)/shard_map/ppermute | solution.py:236
  44.8 1.6 %collective-permute-done.4.refs_0_ = bf16[2,2,3,512,128]{4,3,2,1,0:T(8,128)(2,1)} collective-permute-done((bf16[2,2,3,512,128]{4,3,2,1,0:T(8,128)(2,1)}, bf16[2,2,3,512,128]{4,3,2,1,0:T(8,128)(2,1)}, u32[]{:S(2)}, u32[]{:S(2)}) %collective-permute-start.4) | collective-permute-done | bytes 1572896 | tf_op jit(solution)/shard_map/ppermute | solution.py:236
  46.4 13.2 %corner.1 = (bf16[2,2,3,512,128]{4,3,2,1,0:T(8,128)(2,1)S(1)}, bf16[2,2,3,512,128]{4,3,2,1,0:T(8,128)(2,1)S(1)}, f32[3,2,8,512]{3,2,1,0:T(8,128)S(1)}, f32[3,128,512]{2,1,0:T(8,128)S(1)}) custom-call(s32[8]{0:T(128)S(1)} %stack.46.live, bf16[3,512,128]{2,1,0:T(8,128)(2,1)S(1)} %bitcast.20, bf16[3,512,128]{2,1,0:T(8,128)(2,1)S(1)} %bitcast.26, ...), custom_call_target="tpu_custom_call" | custom-call | flops 1000 | bytes 1000 | tf_op jit(solution)/shard_map/corner/pallas_call | solution.py:118
  59.6 0.1 collective-permute-start.8
  59.7 2.4 %collective-permute-start.9 = (bf16[2,2,3,512,128]{4,3,2,1,0:T(8,128)(2,1)S(1)}, bf16[2,2,3,512,128]{4,3,2,1,0:T(8,128)(2,1)S(1)}, u32[]{:S(2)}, u32[]{:S(2)}) collective-permute-start(bf16[2,2,3,512,128]{4,3,2,1,0:T(8,128)(2,1)S(1)} %get-tuple-element.34), channel_id=1, source_target_pairs={{4,8},{6,10},{8,4},{10,6},{17,33},{19,35},{20,24},{21,37},{22,26},... | collective-permute-start | bytes 4718600 | tf_op jit(solution)/shard_map/ppermute | solution.py:236
  62.2 4.5 %grads.2 = (bf16[1,2,3,512,128]{4,3,2,1,0:T(8,128)(2,1)S(1)}, bf16[1,2,3,512,128]{4,3,2,1,0:T(8,128)(2,1)S(1)}, f32[3,128,512]{2,1,0:T(8,128)S(1)}) custom-call(s32[8]{0:T(128)S(1)} %stack.46.live, bf16[3,512,128]{2,1,0:T(8,128)(2,1)S(1)} %bitcast.21, bf16[3,512,128]{2,1,0:T(8,128)(2,1)S(1)} %bitcast.27, ...), custom_call_target="tpu_custom_call", output_to_operand_aliasing={{2}: (6, {})} | custom-call | flops 1000 | bytes 1000 | tf_op jit(solution)/shard_map/grads/pallas_call | solution.py:147
  66.7 0.4 collective-permute-start.6
  67.1 3.4 %collective-permute-start.7 = (bf16[1,2,3,512,128]{4,3,2,1,0:T(8,128)(2,1)S(1)}, bf16[1,2,3,512,128]{4,3,2,1,0:T(8,128)(2,1)S(1)}, u32[]{:S(2)}, u32[]{:S(2)}) collective-permute-start(bf16[1,2,3,512,128]{4,3,2,1,0:T(8,128)(2,1)S(1)} %get-tuple-element.30), channel_id=1, source_target_pairs={{4,8},{6,10},{8,4},{10,6},{17,33},{19,35},{20,24},{21,37},{22,26},... | collective-permute-start | bytes 2359304 | tf_op jit(solution)/shard_map/ppermute | solution.py:236
  70.5 7.1 %grads.3 = (f32[1,2,3,512,128]{4,3,2,1,0:T(8,128)S(1)}, f32[1,2,3,512,128]{4,3,2,1,0:T(8,128)S(1)}, f32[1,2,3,512,128]{4,3,2,1,0:T(8,128)S(1)}, bf16[3,512,128]{2,1,0:T(8,128)(2,1)}) custom-call(s32[8]{0:T(128)S(1)} %stack.46.live, bf16[3,512,128]{2,1,0:T(8,128)(2,1)S(1)} %bitcast.22, bf16[3,512,128]{2,1,0:T(8,128)(2,1)S(1)} %bitcast.28, ...), custom_call_target="tpu_custom_call" | custom-call | flops 1000 | bytes 1000 | tf_op jit(solution)/shard_map/grads/pallas_call | solution.py:147
  77.6 2.6 %collective-permute-done.8.from_a = bf16[2,2,3,512,128]{4,3,2,1,0:T(8,128)(2,1)S(1)} collective-permute-done((bf16[2,2,3,512,128]{4,3,2,1,0:T(8,128)(2,1)S(1)}, bf16[2,2,3,512,128]{4,3,2,1,0:T(8,128)(2,1)S(1)}, u32[]{:S(2)}, u32[]{:S(2)}) %collective-permute-start.8) | collective-permute-done | bytes 1572896 | tf_op jit(solution)/shard_map/ppermute | solution.py:236
  80.1 1.9 %collective-permute-done.9.from_b = bf16[2,2,3,512,128]{4,3,2,1,0:T(8,128)(2,1)S(1)} collective-permute-done((bf16[2,2,3,512,128]{4,3,2,1,0:T(8,128)(2,1)S(1)}, bf16[2,2,3,512,128]{4,3,2,1,0:T(8,128)(2,1)S(1)}, u32[]{:S(2)}, u32[]{:S(2)}) %collective-permute-start.9) | collective-permute-done | bytes 1572896 | tf_op jit(solution)/shard_map/ppermute | solution.py:236
  82.0 0.5 relay.1
  82.6 0.5 collective-permute-start.10
  83.0 5.2 %collective-permute-start.11 = (bf16[1,2,3,512,128]{4,3,2,1,0:T(8,128)(2,1)S(1)}, bf16[1,2,3,512,128]{4,3,2,1,0:T(8,128)(2,1)S(1)}, u32[]{:S(2)}, u32[]{:S(2)}) collective-permute-start(bf16[1,2,3,512,128]{4,3,2,1,0:T(8,128)(2,1)S(1)} %get-tuple-element.36), channel_id=1, source_target_pairs={{5,9},{7,11},{9,5},{11,7},{16,32},{18,34},{20,36},{21,25},{22,38},... | collective-permute-start | bytes 2359304 | tf_op jit(solution)/shard_map/ppermute | solution.py:236
  88.3 1.2 %collective-permute-done.6.refs_0_ = bf16[1,2,3,512,128]{4,3,2,1,0:T(8,128)(2,1)S(1)} collective-permute-done((bf16[1,2,3,512,128]{4,3,2,1,0:T(8,128)(2,1)S(1)}, bf16[1,2,3,512,128]{4,3,2,1,0:T(8,128)(2,1)S(1)}, u32[]{:S(2)}, u32[]{:S(2)}) %collective-permute-start.6) | collective-permute-done | bytes 786464 | tf_op jit(solution)/shard_map/ppermute | solution.py:236
  89.5 1.3 %collective-permute-done.7.refs_1_ = bf16[1,2,3,512,128]{4,3,2,1,0:T(8,128)(2,1)S(1)} collective-permute-done((bf16[1,2,3,512,128]{4,3,2,1,0:T(8,128)(2,1)S(1)}, bf16[1,2,3,512,128]{4,3,2,1,0:T(8,128)(2,1)S(1)}, u32[]{:S(2)}, u32[]{:S(2)}) %collective-permute-start.7) | collective-permute-done | bytes 786464 | tf_op jit(solution)/shard_map/ppermute | solution.py:236
  90.8 5.1 %collective-permute-done.10.refs_2_ = bf16[1,2,3,512,128]{4,3,2,1,0:T(8,128)(2,1)S(1)} collective-permute-done((bf16[1,2,3,512,128]{4,3,2,1,0:T(8,128)(2,1)S(1)}, bf16[1,2,3,512,128]{4,3,2,1,0:T(8,128)(2,1)S(1)}, u32[]{:S(2)}, u32[]{:S(2)}) %collective-permute-start.10) | collective-permute-done | bytes 786464 | tf_op jit(solution)/shard_map/ppermute | solution.py:236
  95.9 5.5 %collective-permute-done.11.refs_3_ = bf16[1,2,3,512,128]{4,3,2,1,0:T(8,128)(2,1)S(1)} collective-permute-done((bf16[1,2,3,512,128]{4,3,2,1,0:T(8,128)(2,1)S(1)}, bf16[1,2,3,512,128]{4,3,2,1,0:T(8,128)(2,1)S(1)}, u32[]{:S(2)}, u32[]{:S(2)}) %collective-permute-start.11) | collective-permute-done | bytes 786464 | tf_op jit(solution)/shard_map/ppermute | solution.py:236
  101.4 1.2 %total.1 = (bf16[3,512,128]{2,1,0:T(8,128)(2,1)}, bf16[3,512,128]{2,1,0:T(8,128)(2,1)}) custom-call(f32[1,2,3,512,128]{4,3,2,1,0:T(8,128)S(1)} %get-tuple-element.28.own, bf16[1,2,3,512,128]{4,3,2,1,0:T(8,128)(2,1)S(1)} %collective-permute-done.6.refs_0_, bf16[1,2,3,512,128]{4,3,2,1,0:T(8,128)(2,1)S(1)} %collective-permute-done.7.refs_1_, ...), custom_call_target="tpu_custom_call" | custom-call | flops 1000 | bytes 1000 | tf_op jit(solution)/shard_map/total/pallas_call | solution.py:207
Async XLA Ops:
  0.6 7.2 %copy-start.1 = (bf16[3,4,8,16,128]{4,3,2,1,0:T(8,128)(2,1)S(1)}, bf16[3,4,8,16,128]{4,3,2,1,0:T(8,128)(2,1)}, u32[]{:S(2)}) copy-start(bf16[3,4,8,16,128]{4,3,2,1,0:T(8,128)(2,1)} %param.7) | copy-start | bytes 1179652
  0.6 7.2 %copy-start = (bf16[3,4,8,16,128]{4,3,2,1,0:T(8,128)(2,1)S(1)}, bf16[3,4,8,16,128]{4,3,2,1,0:T(8,128)(2,1)}, u32[]{:S(2)}) copy-start(bf16[3,4,8,16,128]{4,3,2,1,0:T(8,128)(2,1)} %param.4) | copy-start | bytes 1179652
  1.9 12.1 %collective-permute-start = (bf16[1,2,3,512,128]{4,3,2,1,0:T(8,128)(2,1)S(1)}, bf16[1,2,3,512,128]{4,3,2,1,0:T(8,128)(2,1)S(1)}, u32[]{:S(2)}, u32[]{:S(2)}) collective-permute-start(bf16[1,2,3,512,128]{4,3,2,1,0:T(8,128)(2,1)S(1)} %maximum_bitcast_fusion.refs_0_.refs_2_), channel_id=1, source_target_pairs={{0,16},{1,5},{2,18},{3,7},{4,20},{5,1},{6,22},{7,3},{8,24},{9,13},... | collective-permute-start | bytes 2359304 | tf_op jit(solution)/shard_map/ppermute | solution.py:236
  2.4 17.5 %collective-permute-start.3 = (bf16[1,2,3,512,128]{4,3,2,1,0:T(8,128)(2,1)S(1)}, bf16[1,2,3,512,128]{4,3,2,1,0:T(8,128)(2,1)S(1)}, u32[]{:S(2)}, u32[]{:S(2)}) collective-permute-start(bf16[1,2,3,512,128]{4,3,2,1,0:T(8,128)(2,1)S(1)} %maximum_bitcast_fusion.refs_0_.refs_2_), channel_id=1, source_target_pairs={{5,9},{7,11},{9,5},{11,7},{16,32},{18,34},{20,36},{21,25},{22,38},... | collective-permute-start | bytes 2359304 | tf_op jit(solution)/shard_map/ppermute | solution.py:236
  14.0 13.9 %collective-permute-start.2 = (bf16[1,2,3,512,128]{4,3,2,1,0:T(8,128)(2,1)S(1)}, bf16[1,2,3,512,128]{4,3,2,1,0:T(8,128)(2,1)S(1)}, u32[]{:S(2)}, u32[]{:S(2)}) collective-permute-start(bf16[1,2,3,512,128]{4,3,2,1,0:T(8,128)(2,1)S(1)} %maximum_bitcast_fusion.refs_0_.refs_2_), channel_id=1, source_target_pairs={{4,8},{6,10},{8,4},{10,6},{17,33},{19,35},{20,24},{21,37},{22,26},... | collective-permute-start | bytes 2359304 | tf_op jit(solution)/shard_map/ppermute | solution.py:236
  17.4 12.1 %collective-permute-start.1 = (bf16[1,2,3,512,128]{4,3,2,1,0:T(8,128)(2,1)S(1)}, bf16[1,2,3,512,128]{4,3,2,1,0:T(8,128)(2,1)S(1)}, u32[]{:S(2)}, u32[]{:S(2)}) collective-permute-start(bf16[1,2,3,512,128]{4,3,2,1,0:T(8,128)(2,1)S(1)} %maximum_bitcast_fusion.refs_0_.refs_2_), channel_id=1, source_target_pairs={{0,4},{1,17},{2,6},{3,19},{4,0},{5,21},{6,2},{7,23},{8,12},{9,25},... | collective-permute-start | bytes 2359304 | tf_op jit(solution)/shard_map/ppermute | solution.py:236
  21.2 23.7 %collective-permute-start.5 = (bf16[2,2,3,512,128]{4,3,2,1,0:T(8,128)(2,1)}, bf16[2,2,3,512,128]{4,3,2,1,0:T(8,128)(2,1)}, u32[]{:S(2)}, u32[]{:S(2)}) collective-permute-start(bf16[2,2,3,512,128]{4,3,2,1,0:T(8,128)(2,1)} %join.1), channel_id=1, source_target_pairs={{4,8},{6,10},{8,4},{10,6},{17,33},{19,35},{20,24},{21,37},{22,26},... | collective-permute-start | bytes 4718600 | tf_op jit(solution)/shard_map/ppermute | solution.py:236
  24.6 21.9 %collective-permute-start.4 = (bf16[2,2,3,512,128]{4,3,2,1,0:T(8,128)(2,1)}, bf16[2,2,3,512,128]{4,3,2,1,0:T(8,128)(2,1)}, u32[]{:S(2)}, u32[]{:S(2)}) collective-permute-start(bf16[2,2,3,512,128]{4,3,2,1,0:T(8,128)(2,1)} %join.1), channel_id=1, source_target_pairs={{0,4},{1,17},{2,6},{3,19},{4,0},{5,21},{6,2},{7,23},{8,12},{9,25},... | collective-permute-start | bytes 4718600 | tf_op jit(solution)/shard_map/ppermute | solution.py:236
  59.6 20.5 %collective-permute-start.8 = (bf16[2,2,3,512,128]{4,3,2,1,0:T(8,128)(2,1)S(1)}, bf16[2,2,3,512,128]{4,3,2,1,0:T(8,128)(2,1)S(1)}, u32[]{:S(2)}, u32[]{:S(2)}) collective-permute-start(bf16[2,2,3,512,128]{4,3,2,1,0:T(8,128)(2,1)S(1)} %get-tuple-element.33), channel_id=1, source_target_pairs={{0,4},{1,17},{2,6},{3,19},{4,0},{5,21},{6,2},{7,23},{8,12},{9,25},... | collective-permute-start | bytes 4718600 | tf_op jit(solution)/shard_map/ppermute | solution.py:236
  59.7 22.3 %collective-permute-start.9 = (bf16[2,2,3,512,128]{4,3,2,1,0:T(8,128)(2,1)S(1)}, bf16[2,2,3,512,128]{4,3,2,1,0:T(8,128)(2,1)S(1)}, u32[]{:S(2)}, u32[]{:S(2)}) collective-permute-start(bf16[2,2,3,512,128]{4,3,2,1,0:T(8,128)(2,1)S(1)} %get-tuple-element.34), channel_id=1, source_target_pairs={{4,8},{6,10},{8,4},{10,6},{17,33},{19,35},{20,24},{21,37},{22,26},... | collective-permute-start | bytes 4718600 | tf_op jit(solution)/shard_map/ppermute | solution.py:236
  66.7 22.8 %collective-permute-start.6 = (bf16[1,2,3,512,128]{4,3,2,1,0:T(8,128)(2,1)S(1)}, bf16[1,2,3,512,128]{4,3,2,1,0:T(8,128)(2,1)S(1)}, u32[]{:S(2)}, u32[]{:S(2)}) collective-permute-start(bf16[1,2,3,512,128]{4,3,2,1,0:T(8,128)(2,1)S(1)} %get-tuple-element.29), channel_id=1, source_target_pairs={{0,4},{1,17},{2,6},{3,19},{4,0},{5,21},{6,2},{7,23},{8,12},{9,25},... | collective-permute-start | bytes 2359304 | tf_op jit(solution)/shard_map/ppermute | solution.py:236
  67.1 23.7 %collective-permute-start.7 = (bf16[1,2,3,512,128]{4,3,2,1,0:T(8,128)(2,1)S(1)}, bf16[1,2,3,512,128]{4,3,2,1,0:T(8,128)(2,1)S(1)}, u32[]{:S(2)}, u32[]{:S(2)}) collective-permute-start(bf16[1,2,3,512,128]{4,3,2,1,0:T(8,128)(2,1)S(1)} %get-tuple-element.30), channel_id=1, source_target_pairs={{4,8},{6,10},{8,4},{10,6},{17,33},{19,35},{20,24},{21,37},{22,26},... | collective-permute-start | bytes 2359304 | tf_op jit(solution)/shard_map/ppermute | solution.py:236
  82.6 13.3 %collective-permute-start.10 = (bf16[1,2,3,512,128]{4,3,2,1,0:T(8,128)(2,1)S(1)}, bf16[1,2,3,512,128]{4,3,2,1,0:T(8,128)(2,1)S(1)}, u32[]{:S(2)}, u32[]{:S(2)}) collective-permute-start(bf16[1,2,3,512,128]{4,3,2,1,0:T(8,128)(2,1)S(1)} %get-tuple-element.35), channel_id=1, source_target_pairs={{0,16},{1,5},{2,18},{3,7},{4,20},{5,1},{6,22},{7,3},{8,24},{9,13},... | collective-permute-start | bytes 2359304 | tf_op jit(solution)/shard_map/ppermute | solution.py:236
  83.0 18.3 %collective-permute-start.11 = (bf16[1,2,3,512,128]{4,3,2,1,0:T(8,128)(2,1)S(1)}, bf16[1,2,3,512,128]{4,3,2,1,0:T(8,128)(2,1)S(1)}, u32[]{:S(2)}, u32[]{:S(2)}) collective-permute-start(bf16[1,2,3,512,128]{4,3,2,1,0:T(8,128)(2,1)S(1)} %get-tuple-element.36), channel_id=1, source_target_pairs={{5,9},{7,11},{9,5},{11,7},{16,32},{18,34},{20,36},{21,25},{22,38},... | collective-permute-start | bytes 2359304 | tf_op jit(solution)/shard_map/ppermute | solution.py:236

commit v6 on v5

--- a/solution.py
+++ b/solution.py
@@ -263,23 +263,26 @@
     later, stats, first_a = lax.optimization_barrier((kv, stats, first_a))
     second_a, second_b = (swapped(later, 1, pair, sizes) for pair in (0, 1))
     both = run_join(first_a, first_b)
-    corner_a, corner_b = (swapped(both, 1, pair, sizes) for pair in (0, 1))
+    corner_b, corner_a = (swapped(both, 1, pair, sizes) for pair in (1, 0))
 
     near, near_flags = [first_a, first_b, kv], [[0], [1], [None]]
     side, side_flags = [second_a, second_b], [[2], [3]]
-    corner, corner_flags = [corner_a, corner_b], [[4, 5], [6, 7]]
+    corner, corner_flags = [corner_b, corner_a], [[6, 7], [4, 5]]
     stats = run_stats(live, q, g, near[:2], near_flags[:2], stats, factor)
     stats = run_stats(live, q, g, side, side_flags, stats, factor, cost=20 * 10**12)
-    part_a, part_b, ends, acc = run_corner(
+    part_b, part_a, ends, acc = run_corner(
         live, q, g, stats, corner, corner_flags, factor, scale
     )
-    back_a, back_b = swapped(part_a, 1, 0, sizes), swapped(part_b, 1, 1, sizes)
+    back_b = swapped(part_b, 1, 1, sizes)
+    back_a = swapped(part_a, 1, 0, sizes)
     grads = functools.partial(run_grads, live, q, g, ends)
     side_a, side_b, acc = grads(side, side_flags, acc, factor, scale, jnp.bfloat16)
-    total_parts = [swapped(side_a, 1, 0, sizes), swapped(side_b, 1, 1, sizes)]
+    from_b = swapped(side_b, 1, 1, sizes)
+    total_parts = [from_b, swapped(side_a, 1, 0, sizes)]
     own_a, own_b, own, dq = grads(near, near_flags, acc, factor, scale, jnp.float32, last=True)
-    send_a, send_b = run_relay(own_a, own_b, back_a, back_b)
-    total_parts += [swapped(send_a, 0, 0, sizes), swapped(send_b, 0, 1, sizes)]
+    send_a, send_b = run_relay(own_a, own_b, back_b, back_a)
+    got_b = swapped(send_b, 0, 1, sizes)
+    total_parts += [got_b, swapped(send_a, 0, 0, sizes)]
     dk, dv = run_total(own, total_parts)
     return dq.reshape(shape), dk.reshape(shape), dv.reshape(shape)
 

time: 104 us -> 104 us (level)
  transfers between devices with their start and end apart: 12 -> 12, of which waited for: 12 -> 8; matrix products, arithmetic and copies ran while one was open for 0% -> 0% of each run, Pallas kernels for 19% -> 19%
where the time goes in v6:
time: 104 us; the launch traced here: 103 us
  waiting for transfers between devices  40.6 us (39%)
  Pallas kernels  34.3 us (33%)
  starting transfers between devices  25.4 us (24%)
  other arithmetic  1.26 us (1%)
    ppermute x12, waiting for transfers between devices, swapped(): return lax.ppermute(x, ('tm', 'height', 'head'), route)  40.6 us
    ppermute x12, starting transfers between devices, swapped(): return lax.ppermute(x, ('tm', 'height', 'head'), route)  25.4 us
    pallas_call x1, Pallas kernels, run_corner(): pl.pallas_call(functools.partial(corner_kernel, flags, factor, scale), ou...  13.2 us
    pallas_call x2, Pallas kernels, run_grads(): pl.pallas_call(functools.partial(grads_kernel, flags, last, factor, scale...  11.6 us
    pallas_call x3, Pallas kernels, run_stats(): pl.pallas_call(functools.partial(stats_kernel, flags, first, factor), out...  6.49 us
  transfers between devices with their start and end apart: 12, of which 8 were waited for; matrix products, arithmetic and copies ran while one was open for 0% of the time, Pallas kernels for 19%

profile of v6, /device:TPU:98, one launch (start us, length us, event | category | flops | bytes accessed | tf_op | source)
XLA Modules:
  0.0 102.5 jit_solution(10213593373775397710)
XLA Ops:
  0.6 0.0 copy-start.1
  0.6 0.0 copy-start
  0.7 1.3 %maximum_bitcast_fusion.refs_0_.refs_2_ = bf16[1,2,3,512,128]{4,3,2,1,0:T(8,128)(2,1)S(1)} fusion(bf16[1,3,512,128]{3,2,1,0:T(8,128)(2,1)} %bitcast.29, bf16[1,3,512,128]{3,2,1,0:T(8,128)(2,1)} %bitcast.30), kind=kLoop, calls=%fused_computation | loop fusion | flops 393216 | bytes 1572864 | tf_op jit(solution)/shard_map/broadcast_in_dim | solution.py:246
  1.9 0.5 collective-permute-start
  2.4 5.2 %collective-permute-start.3 = (bf16[1,2,3,512,128]{4,3,2,1,0:T(8,128)(2,1)S(1)}, bf16[1,2,3,512,128]{4,3,2,1,0:T(8,128)(2,1)S(1)}, u32[]{:S(2)}, u32[]{:S(2)}) collective-permute-start(bf16[1,2,3,512,128]{4,3,2,1,0:T(8,128)(2,1)S(1)} %maximum_bitcast_fusion.refs_0_.refs_2_), channel_id=1, source_target_pairs={{5,9},{7,11},{9,5},{11,7},{16,32},{18,34},{20,36},{21,25},{22,38},... | collective-permute-start | bytes 2359304 | tf_op jit(solution)/shard_map/ppermute | solution.py:236
  7.7 0.1 stack.46.live
  7.8 0.0 copy-done.1
  7.8 0.0 copy-done
  7.8 1.6 %stats.3.refs_2_ = f32[3,3,8,512]{3,2,1,0:T(8,128)S(1)} custom-call(s32[8]{0:T(128)S(1)} %stack.46.live, bf16[3,512,128]{2,1,0:T(8,128)(2,1)S(1)} %bitcast.17, bf16[3,512,128]{2,1,0:T(8,128)(2,1)S(1)} %bitcast.23, bf16[1,2,3,512,128]{4,3,2,1,0:T(8,128)(2,1)S(1)} %maximum_bitcast_fusion.refs_0_.refs_2_), custom_call_target="tpu_custom_call" | custom-call | flops 1000 | bytes 1000 | tf_op jit(solution)/shard_map/stats/pallas_call | solution.py:133
  9.4 4.6 %collective-permute-done.refs_0_.a_ref = bf16[1,2,3,512,128]{4,3,2,1,0:T(8,128)(2,1)S(1)} collective-permute-done((bf16[1,2,3,512,128]{4,3,2,1,0:T(8,128)(2,1)S(1)}, bf16[1,2,3,512,128]{4,3,2,1,0:T(8,128)(2,1)S(1)}, u32[]{:S(2)}, u32[]{:S(2)}) %collective-permute-start) | collective-permute-done | bytes 786464 | tf_op jit(solution)/shard_map/ppermute | solution.py:236
  14.0 3.4 %collective-permute-start.2 = (bf16[1,2,3,512,128]{4,3,2,1,0:T(8,128)(2,1)S(1)}, bf16[1,2,3,512,128]{4,3,2,1,0:T(8,128)(2,1)S(1)}, u32[]{:S(2)}, u32[]{:S(2)}) collective-permute-start(bf16[1,2,3,512,128]{4,3,2,1,0:T(8,128)(2,1)S(1)} %maximum_bitcast_fusion.refs_0_.refs_2_), channel_id=1, source_target_pairs={{4,8},{6,10},{8,4},{10,6},{17,33},{19,35},{20,24},{21,37},{22,26},... | collective-permute-start | bytes 2359304 | tf_op jit(solution)/shard_map/ppermute | solution.py:236
  17.4 0.1 collective-permute-start.1
  17.5 2.4 %collective-permute-done.3.refs_1_.b_ref = bf16[1,2,3,512,128]{4,3,2,1,0:T(8,128)(2,1)S(1)} collective-permute-done((bf16[1,2,3,512,128]{4,3,2,1,0:T(8,128)(2,1)S(1)}, bf16[1,2,3,512,128]{4,3,2,1,0:T(8,128)(2,1)S(1)}, u32[]{:S(2)}, u32[]{:S(2)}) %collective-permute-start.3) | collective-permute-done | bytes 786464 | tf_op jit(solution)/shard_map/ppermute | solution.py:236
  19.9 1.3 %join.1 = bf16[2,2,3,512,128]{4,3,2,1,0:T(8,128)(2,1)} custom-call(bf16[1,2,3,512,128]{4,3,2,1,0:T(8,128)(2,1)S(1)} %collective-permute-done.refs_0_.a_ref, bf16[1,2,3,512,128]{4,3,2,1,0:T(8,128)(2,1)S(1)} %collective-permute-done.3.refs_1_.b_ref), custom_call_target="tpu_custom_call" | custom-call | flops 1000 | bytes 1000 | tf_op jit(solution)/shard_map/join/pallas_call | solution.py:165
  21.2 0.5 collective-permute-start.5
  21.7 4.2 %collective-permute-start.4 = (bf16[2,2,3,512,128]{4,3,2,1,0:T(8,128)(2,1)}, bf16[2,2,3,512,128]{4,3,2,1,0:T(8,128)(2,1)}, u32[]{:S(2)}, u32[]{:S(2)}) collective-permute-start(bf16[2,2,3,512,128]{4,3,2,1,0:T(8,128)(2,1)} %join.1), channel_id=1, source_target_pairs={{4,8},{6,10},{8,4},{10,6},{17,33},{19,35},{20,24},{21,37},{22,26},... | collective-permute-start | bytes 4718600 | tf_op jit(solution)/shard_map/ppermute | solution.py:236
  25.9 2.4 %stats.4.refs_2_ = f32[3,3,8,512]{3,2,1,0:T(8,128)S(1)} custom-call(s32[8]{0:T(128)S(1)} %stack.46.live, bf16[3,512,128]{2,1,0:T(8,128)(2,1)S(1)} %bitcast.18, bf16[3,512,128]{2,1,0:T(8,128)(2,1)S(1)} %bitcast.24, bf16[1,2,3,512,128]{4,3,2,1,0:T(8,128)(2,1)S(1)} %collective-permute-done.refs_0_.a_ref, ...), custom_call_target="tpu_custom_call" | custom-call | flops 1000 | bytes 1000 | tf_op jit(solution)/shard_map/stats/pallas_call | solution.py:133
  28.4 0.0 collective-permute-done.2.refs_1_
  28.4 1.1 %collective-permute-done.1.refs_0_ = bf16[1,2,3,512,128]{4,3,2,1,0:T(8,128)(2,1)S(1)} collective-permute-done((bf16[1,2,3,512,128]{4,3,2,1,0:T(8,128)(2,1)S(1)}, bf16[1,2,3,512,128]{4,3,2,1,0:T(8,128)(2,1)S(1)}, u32[]{:S(2)}, u32[]{:S(2)}) %collective-permute-start.1) | collective-permute-done | bytes 786464 | tf_op jit(solution)/shard_map/ppermute | solution.py:236
  29.4 2.5 %stats.5.st_ref = f32[3,3,8,512]{3,2,1,0:T(8,128)S(1)} custom-call(s32[8]{0:T(128)S(1)} %stack.46.live, bf16[3,512,128]{2,1,0:T(8,128)(2,1)S(1)} %bitcast.19, bf16[3,512,128]{2,1,0:T(8,128)(2,1)S(1)} %bitcast.25, bf16[1,2,3,512,128]{4,3,2,1,0:T(8,128)(2,1)S(1)} %collective-permute-done.1.refs_0_, ...), custom_call_target="tpu_custom_call" | custom-call | flops 19999999655936 | bytes 1000 | tf_op jit(solution)/shard_map/stats/pallas_call | solution.py:133
  31.9 14.5 %collective-permute-done.5.refs_1_ = bf16[2,2,3,512,128]{4,3,2,1,0:T(8,128)(2,1)} collective-permute-done((bf16[2,2,3,512,128]{4,3,2,1,0:T(8,128)(2,1)}, bf16[2,2,3,512,128]{4,3,2,1,0:T(8,128)(2,1)}, u32[]{:S(2)}, u32[]{:S(2)}) %collective-permute-start.5) | collective-permute-done | bytes 1572896 | tf_op jit(solution)/shard_map/ppermute | solution.py:236
  46.4 0.0 collective-permute-done.4.refs_0_
  46.4 13.2 %corner.1 = (bf16[2,2,3,512,128]{4,3,2,1,0:T(8,128)(2,1)S(1)}, bf16[2,2,3,512,128]{4,3,2,1,0:T(8,128)(2,1)S(1)}, f32[3,2,8,512]{3,2,1,0:T(8,128)S(1)}, f32[3,128,512]{2,1,0:T(8,128)S(1)}) custom-call(s32[8]{0:T(128)S(1)} %stack.46.live, bf16[3,512,128]{2,1,0:T(8,128)(2,1)S(1)} %bitcast.20, bf16[3,512,128]{2,1,0:T(8,128)(2,1)S(1)} %bitcast.26, ...), custom_call_target="tpu_custom_call" | custom-call | flops 1000 | bytes 1000 | tf_op jit(solution)/shard_map/corner/pallas_call | solution.py:118
  59.7 2.4 %collective-permute-start.8 = (bf16[2,2,3,512,128]{4,3,2,1,0:T(8,128)(2,1)S(1)}, bf16[2,2,3,512,128]{4,3,2,1,0:T(8,128)(2,1)S(1)}, u32[]{:S(2)}, u32[]{:S(2)}) collective-permute-start(bf16[2,2,3,512,128]{4,3,2,1,0:T(8,128)(2,1)S(1)} %get-tuple-element.33), channel_id=1, source_target_pairs={{4,8},{6,10},{8,4},{10,6},{17,33},{19,35},{20,24},{21,37},{22,26},... | collective-permute-start | bytes 4718600 | tf_op jit(solution)/shard_map/ppermute | solution.py:236
  62.1 0.1 collective-permute-start.9
  62.2 4.5 %grads.2 = (bf16[1,2,3,512,128]{4,3,2,1,0:T(8,128)(2,1)S(1)}, bf16[1,2,3,512,128]{4,3,2,1,0:T(8,128)(2,1)S(1)}, f32[3,128,512]{2,1,0:T(8,128)S(1)}) custom-call(s32[8]{0:T(128)S(1)} %stack.46.live, bf16[3,512,128]{2,1,0:T(8,128)(2,1)S(1)} %bitcast.21, bf16[3,512,128]{2,1,0:T(8,128)(2,1)S(1)} %bitcast.27, ...), custom_call_target="tpu_custom_call", output_to_operand_aliasing={{2}: (6, {})} | custom-call | flops 1000 | bytes 1000 | tf_op jit(solution)/shard_map/grads/pallas_call | solution.py:147
  66.7 3.4 %collective-permute-start.6 = (bf16[1,2,3,512,128]{4,3,2,1,0:T(8,128)(2,1)S(1)}, bf16[1,2,3,512,128]{4,3,2,1,0:T(8,128)(2,1)S(1)}, u32[]{:S(2)}, u32[]{:S(2)}) collective-permute-start(bf16[1,2,3,512,128]{4,3,2,1,0:T(8,128)(2,1)S(1)} %get-tuple-element.29), channel_id=1, source_target_pairs={{4,8},{6,10},{8,4},{10,6},{17,33},{19,35},{20,24},{21,37},{22,26},... | collective-permute-start | bytes 2359304 | tf_op jit(solution)/shard_map/ppermute | solution.py:236
  70.1 0.3 collective-permute-start.7
  70.5 7.1 %grads.3 = (f32[1,2,3,512,128]{4,3,2,1,0:T(8,128)S(1)}, f32[1,2,3,512,128]{4,3,2,1,0:T(8,128)S(1)}, f32[1,2,3,512,128]{4,3,2,1,0:T(8,128)S(1)}, bf16[3,512,128]{2,1,0:T(8,128)(2,1)}) custom-call(s32[8]{0:T(128)S(1)} %stack.46.live, bf16[3,512,128]{2,1,0:T(8,128)(2,1)S(1)} %bitcast.22, bf16[3,512,128]{2,1,0:T(8,128)(2,1)S(1)} %bitcast.28, ...), custom_call_target="tpu_custom_call" | custom-call | flops 1000 | bytes 1000 | tf_op jit(solution)/shard_map/grads/pallas_call | solution.py:147
  77.6 4.4 %collective-permute-done.8.from_a = bf16[2,2,3,512,128]{4,3,2,1,0:T(8,128)(2,1)S(1)} collective-permute-done((bf16[2,2,3,512,128]{4,3,2,1,0:T(8,128)(2,1)S(1)}, bf16[2,2,3,512,128]{4,3,2,1,0:T(8,128)(2,1)S(1)}, u32[]{:S(2)}, u32[]{:S(2)}) %collective-permute-start.8) | collective-permute-done | bytes 1572896 | tf_op jit(solution)/shard_map/ppermute | solution.py:236
  82.0 0.6 collective-permute-done.9.from_b
  82.6 0.5 relay.1
  83.1 5.0 %collective-permute-start.10 = (bf16[1,2,3,512,128]{4,3,2,1,0:T(8,128)(2,1)S(1)}, bf16[1,2,3,512,128]{4,3,2,1,0:T(8,128)(2,1)S(1)}, u32[]{:S(2)}, u32[]{:S(2)}) collective-permute-start(bf16[1,2,3,512,128]{4,3,2,1,0:T(8,128)(2,1)S(1)} %get-tuple-element.35), channel_id=1, source_target_pairs={{5,9},{7,11},{9,5},{11,7},{16,32},{18,34},{20,36},{21,25},{22,38},... | collective-permute-start | bytes 2359304 | tf_op jit(solution)/shard_map/ppermute | solution.py:236
  88.2 0.1 collective-permute-start.11
  88.3 3.2 %collective-permute-done.6.refs_0_ = bf16[1,2,3,512,128]{4,3,2,1,0:T(8,128)(2,1)S(1)} collective-permute-done((bf16[1,2,3,512,128]{4,3,2,1,0:T(8,128)(2,1)S(1)}, bf16[1,2,3,512,128]{4,3,2,1,0:T(8,128)(2,1)S(1)}, u32[]{:S(2)}, u32[]{:S(2)}) %collective-permute-start.6) | collective-permute-done | bytes 786464 | tf_op jit(solution)/shard_map/ppermute | solution.py:236
  91.4 0.0 collective-permute-done.7.refs_1_
  91.4 9.9 %collective-permute-done.10.refs_2_ = bf16[1,2,3,512,128]{4,3,2,1,0:T(8,128)(2,1)S(1)} collective-permute-done((bf16[1,2,3,512,128]{4,3,2,1,0:T(8,128)(2,1)S(1)}, bf16[1,2,3,512,128]{4,3,2,1,0:T(8,128)(2,1)S(1)}, u32[]{:S(2)}, u32[]{:S(2)}) %collective-permute-start.10) | collective-permute-done | bytes 786464 | tf_op jit(solution)/shard_map/ppermute | solution.py:236
  101.3 0.0 collective-permute-done.11.refs_3_
  101.3 1.2 %total.1 = (bf16[3,512,128]{2,1,0:T(8,128)(2,1)}, bf16[3,512,128]{2,1,0:T(8,128)(2,1)}) custom-call(f32[1,2,3,512,128]{4,3,2,1,0:T(8,128)S(1)} %get-tuple-element.28.own, bf16[1,2,3,512,128]{4,3,2,1,0:T(8,128)(2,1)S(1)} %collective-permute-done.6.refs_0_, bf16[1,2,3,512,128]{4,3,2,1,0:T(8,128)(2,1)S(1)} %collective-permute-done.7.refs_1_, ...), custom_call_target="tpu_custom_call" | custom-call | flops 1000 | bytes 1000 | tf_op jit(solution)/shard_map/total/pallas_call | solution.py:207
Async XLA Ops:
  0.6 7.2 %copy-start.1 = (bf16[3,4,8,16,128]{4,3,2,1,0:T(8,128)(2,1)S(1)}, bf16[3,4,8,16,128]{4,3,2,1,0:T(8,128)(2,1)}, u32[]{:S(2)}) copy-start(bf16[3,4,8,16,128]{4,3,2,1,0:T(8,128)(2,1)} %param.7) | copy-start | bytes 1179652
  0.6 7.2 %copy-start = (bf16[3,4,8,16,128]{4,3,2,1,0:T(8,128)(2,1)S(1)}, bf16[3,4,8,16,128]{4,3,2,1,0:T(8,128)(2,1)}, u32[]{:S(2)}) copy-start(bf16[3,4,8,16,128]{4,3,2,1,0:T(8,128)(2,1)} %param.4) | copy-start | bytes 1179652
  1.9 12.1 %collective-permute-start = (bf16[1,2,3,512,128]{4,3,2,1,0:T(8,128)(2,1)S(1)}, bf16[1,2,3,512,128]{4,3,2,1,0:T(8,128)(2,1)S(1)}, u32[]{:S(2)}, u32[]{:S(2)}) collective-permute-start(bf16[1,2,3,512,128]{4,3,2,1,0:T(8,128)(2,1)S(1)} %maximum_bitcast_fusion.refs_0_.refs_2_), channel_id=1, source_target_pairs={{0,16},{1,5},{2,18},{3,7},{4,20},{5,1},{6,22},{7,3},{8,24},{9,13},... | collective-permute-start | bytes 2359304 | tf_op jit(solution)/shard_map/ppermute | solution.py:236
  2.4 17.5 %collective-permute-start.3 = (bf16[1,2,3,512,128]{4,3,2,1,0:T(8,128)(2,1)S(1)}, bf16[1,2,3,512,128]{4,3,2,1,0:T(8,128)(2,1)S(1)}, u32[]{:S(2)}, u32[]{:S(2)}) collective-permute-start(bf16[1,2,3,512,128]{4,3,2,1,0:T(8,128)(2,1)S(1)} %maximum_bitcast_fusion.refs_0_.refs_2_), channel_id=1, source_target_pairs={{5,9},{7,11},{9,5},{11,7},{16,32},{18,34},{20,36},{21,25},{22,38},... | collective-permute-start | bytes 2359304 | tf_op jit(solution)/shard_map/ppermute | solution.py:236
  14.0 14.4 %collective-permute-start.2 = (bf16[1,2,3,512,128]{4,3,2,1,0:T(8,128)(2,1)S(1)}, bf16[1,2,3,512,128]{4,3,2,1,0:T(8,128)(2,1)S(1)}, u32[]{:S(2)}, u32[]{:S(2)}) collective-permute-start(bf16[1,2,3,512,128]{4,3,2,1,0:T(8,128)(2,1)S(1)} %maximum_bitcast_fusion.refs_0_.refs_2_), channel_id=1, source_target_pairs={{4,8},{6,10},{8,4},{10,6},{17,33},{19,35},{20,24},{21,37},{22,26},... | collective-permute-start | bytes 2359304 | tf_op jit(solution)/shard_map/ppermute | solution.py:236
  17.4 12.1 %collective-permute-start.1 = (bf16[1,2,3,512,128]{4,3,2,1,0:T(8,128)(2,1)S(1)}, bf16[1,2,3,512,128]{4,3,2,1,0:T(8,128)(2,1)S(1)}, u32[]{:S(2)}, u32[]{:S(2)}) collective-permute-start(bf16[1,2,3,512,128]{4,3,2,1,0:T(8,128)(2,1)S(1)} %maximum_bitcast_fusion.refs_0_.refs_2_), channel_id=1, source_target_pairs={{0,4},{1,17},{2,6},{3,19},{4,0},{5,21},{6,2},{7,23},{8,12},{9,25},... | collective-permute-start | bytes 2359304 | tf_op jit(solution)/shard_map/ppermute | solution.py:236
  21.2 25.3 %collective-permute-start.5 = (bf16[2,2,3,512,128]{4,3,2,1,0:T(8,128)(2,1)}, bf16[2,2,3,512,128]{4,3,2,1,0:T(8,128)(2,1)}, u32[]{:S(2)}, u32[]{:S(2)}) collective-permute-start(bf16[2,2,3,512,128]{4,3,2,1,0:T(8,128)(2,1)} %join.1), channel_id=1, source_target_pairs={{0,4},{1,17},{2,6},{3,19},{4,0},{5,21},{6,2},{7,23},{8,12},{9,25},... | collective-permute-start | bytes 4718600 | tf_op jit(solution)/shard_map/ppermute | solution.py:236
  21.7 24.7 %collective-permute-start.4 = (bf16[2,2,3,512,128]{4,3,2,1,0:T(8,128)(2,1)}, bf16[2,2,3,512,128]{4,3,2,1,0:T(8,128)(2,1)}, u32[]{:S(2)}, u32[]{:S(2)}) collective-permute-start(bf16[2,2,3,512,128]{4,3,2,1,0:T(8,128)(2,1)} %join.1), channel_id=1, source_target_pairs={{4,8},{6,10},{8,4},{10,6},{17,33},{19,35},{20,24},{21,37},{22,26},... | collective-permute-start | bytes 4718600 | tf_op jit(solution)/shard_map/ppermute | solution.py:236
  59.7 22.3 %collective-permute-start.8 = (bf16[2,2,3,512,128]{4,3,2,1,0:T(8,128)(2,1)S(1)}, bf16[2,2,3,512,128]{4,3,2,1,0:T(8,128)(2,1)S(1)}, u32[]{:S(2)}, u32[]{:S(2)}) collective-permute-start(bf16[2,2,3,512,128]{4,3,2,1,0:T(8,128)(2,1)S(1)} %get-tuple-element.33), channel_id=1, source_target_pairs={{4,8},{6,10},{8,4},{10,6},{17,33},{19,35},{20,24},{21,37},{22,26},... | collective-permute-start | bytes 4718600 | tf_op jit(solution)/shard_map/ppermute | solution.py:236
  62.1 20.5 %collective-permute-start.9 = (bf16[2,2,3,512,128]{4,3,2,1,0:T(8,128)(2,1)S(1)}, bf16[2,2,3,512,128]{4,3,2,1,0:T(8,128)(2,1)S(1)}, u32[]{:S(2)}, u32[]{:S(2)}) collective-permute-start(bf16[2,2,3,512,128]{4,3,2,1,0:T(8,128)(2,1)S(1)} %get-tuple-element.34), channel_id=1, source_target_pairs={{0,4},{1,17},{2,6},{3,19},{4,0},{5,21},{6,2},{7,23},{8,12},{9,25},... | collective-permute-start | bytes 4718600 | tf_op jit(solution)/shard_map/ppermute | solution.py:236
  66.7 24.7 %collective-permute-start.6 = (bf16[1,2,3,512,128]{4,3,2,1,0:T(8,128)(2,1)S(1)}, bf16[1,2,3,512,128]{4,3,2,1,0:T(8,128)(2,1)S(1)}, u32[]{:S(2)}, u32[]{:S(2)}) collective-permute-start(bf16[1,2,3,512,128]{4,3,2,1,0:T(8,128)(2,1)S(1)} %get-tuple-element.29), channel_id=1, source_target_pairs={{4,8},{6,10},{8,4},{10,6},{17,33},{19,35},{20,24},{21,37},{22,26},... | collective-permute-start | bytes 2359304 | tf_op jit(solution)/shard_map/ppermute | solution.py:236
  70.1 21.3 %collective-permute-start.7 = (bf16[1,2,3,512,128]{4,3,2,1,0:T(8,128)(2,1)S(1)}, bf16[1,2,3,512,128]{4,3,2,1,0:T(8,128)(2,1)S(1)}, u32[]{:S(2)}, u32[]{:S(2)}) collective-permute-start(bf16[1,2,3,512,128]{4,3,2,1,0:T(8,128)(2,1)S(1)} %get-tuple-element.30), channel_id=1, source_target_pairs={{0,4},{1,17},{2,6},{3,19},{4,0},{5,21},{6,2},{7,23},{8,12},{9,25},... | collective-permute-start | bytes 2359304 | tf_op jit(solution)/shard_map/ppermute | solution.py:236
  83.1 18.2 %collective-permute-start.10 = (bf16[1,2,3,512,128]{4,3,2,1,0:T(8,128)(2,1)S(1)}, bf16[1,2,3,512,128]{4,3,2,1,0:T(8,128)(2,1)S(1)}, u32[]{:S(2)}, u32[]{:S(2)}) collective-permute-start(bf16[1,2,3,512,128]{4,3,2,1,0:T(8,128)(2,1)S(1)} %get-tuple-element.35), channel_id=1, source_target_pairs={{5,9},{7,11},{9,5},{11,7},{16,32},{18,34},{20,36},{21,25},{22,38},... | collective-permute-start | bytes 2359304 | tf_op jit(solution)/shard_map/ppermute | solution.py:236
  88.2 13.1 %collective-permute-start.11 = (bf16[1,2,3,512,128]{4,3,2,1,0:T(8,128)(2,1)S(1)}, bf16[1,2,3,512,128]{4,3,2,1,0:T(8,128)(2,1)S(1)}, u32[]{:S(2)}, u32[]{:S(2)}) collective-permute-start(bf16[1,2,3,512,128]{4,3,2,1,0:T(8,128)(2,1)S(1)} %get-tuple-element.36), channel_id=1, source_target_pairs={{0,16},{1,5},{2,18},{3,7},{4,20},{5,1},{6,22},{7,3},{8,24},{9,13},... | collective-permute-start | bytes 2359304 | tf_op jit(solution)/shard_map/ppermute | solution.py:236

commit v7 on v6

--- a/solution.py
+++ b/solution.py
@@ -141,12 +141,12 @@
     )(*args)
 
 
-def run_grads(live, q, g, ends, blocks, flags, acc, factor, scale, part, last=False):
+def run_grads(live, q, g, ends, blocks, flags, acc, factor, scale, types, last=False):
     args = [live, q, g, ends, *blocks, acc]
     end = jax.ShapeDtypeStruct(*((q.shape, q.dtype) if last else (acc.shape, acc.dtype)))
     return pl.pallas_call(
         functools.partial(grads_kernel, flags, last, factor, scale),
-        out_shape=[jax.ShapeDtypeStruct(b.shape, part) for b in blocks] + [end],
+        out_shape=[jax.ShapeDtypeStruct(b.shape, t) for b, t in zip(blocks, types)] + [end],
         in_specs=[SMEM] + [VMEM] * (len(args) - 1),
         out_specs=[VMEM] * (len(blocks) + 1),
         input_output_aliases={} if last else {len(args) - 1: len(blocks)},
@@ -275,11 +275,12 @@
     )
     back_b = swapped(part_b, 1, 1, sizes)
     back_a = swapped(part_a, 1, 0, sizes)
-    grads = functools.partial(run_grads, live, q, g, ends)
-    side_a, side_b, acc = grads(side, side_flags, acc, factor, scale, jnp.bfloat16)
+    types = [jnp.bfloat16] * 2 + [jnp.float32] * 3
+    side_a, side_b, own_a, own_b, own, dq = run_grads(
+        live, q, g, ends, side + near, side_flags + near_flags, acc, factor, scale, types, last=True
+    )
     from_b = swapped(side_b, 1, 1, sizes)
     total_parts = [from_b, swapped(side_a, 1, 0, sizes)]
-    own_a, own_b, own, dq = grads(near, near_flags, acc, factor, scale, jnp.float32, last=True)
     send_a, send_b = run_relay(own_a, own_b, back_b, back_a)
     got_b = swapped(send_b, 0, 1, sizes)
     total_parts += [got_b, swapped(send_a, 0, 0, sizes)]

time: 104 us -> 104 us (level)
  waiting for transfers between devices: 40.6 us -> 41.7 us
    ppermute x12, waiting for transfers between devices: 40.6 us -> 41.7 us  [swapped(): return lax.ppermute(x, ('tm', 'height', 'head'), route)]
    pallas_call x2 -> x1, Pallas kernels: 11.6 us -> 10.8 us  [run_grads(): pl.pallas_call(functools.partial(grads_kernel, flags, last, factor, scale...]
where the time goes in v7:
time: 104 us; the launch traced here: 103 us
  waiting for transfers between devices  41.7 us (40%)
  Pallas kernels  33.5 us (32%)
  starting transfers between devices  25.1 us (24%)
  other arithmetic  1.26 us (1%)
    ppermute x12, waiting for transfers between devices, swapped(): return lax.ppermute(x, ('tm', 'height', 'head'), route)  41.7 us
    ppermute x12, starting transfers between devices, swapped(): return lax.ppermute(x, ('tm', 'height', 'head'), route)  25.1 us
    pallas_call x1, Pallas kernels, run_corner(): pl.pallas_call(functools.partial(corner_kernel, flags, factor, scale), ou...  13.2 us
    pallas_call x1, Pallas kernels, run_grads(): pl.pallas_call(functools.partial(grads_kernel, flags, last, factor, scale...  10.8 us
    pallas_call x3, Pallas kernels, run_stats(): pl.pallas_call(functools.partial(stats_kernel, flags, first, factor), out...  6.48 us
  transfers between devices with their start and end apart: 12, of which 8 were waited for; matrix products, arithmetic and copies ran while one was open for 0% of the time, Pallas kernels for 19%

profile of v7, /device:TPU:98, one launch (start us, length us, event | category | flops | bytes accessed | tf_op | source)
XLA Modules:
  0.0 102.6 jit_solution(8405671143122480881)
XLA Ops:
  0.6 0.0 copy-start.1
  0.6 0.0 copy-start
  0.7 1.3 %maximum_bitcast_fusion.refs_0_.refs_4_ = bf16[1,2,3,512,128]{4,3,2,1,0:T(8,128)(2,1)S(1)} fusion(bf16[1,3,512,128]{3,2,1,0:T(8,128)(2,1)} %bitcast.27, bf16[1,3,512,128]{3,2,1,0:T(8,128)(2,1)} %bitcast.28), kind=kLoop, calls=%fused_computation | loop fusion | flops 393216 | bytes 1572864 | tf_op jit(solution)/shard_map/broadcast_in_dim | solution.py:246
  1.9 0.5 collective-permute-start
  2.4 5.2 %collective-permute-start.3 = (bf16[1,2,3,512,128]{4,3,2,1,0:T(8,128)(2,1)S(1)}, bf16[1,2,3,512,128]{4,3,2,1,0:T(8,128)(2,1)S(1)}, u32[]{:S(2)}, u32[]{:S(2)}) collective-permute-start(bf16[1,2,3,512,128]{4,3,2,1,0:T(8,128)(2,1)S(1)} %maximum_bitcast_fusion.refs_0_.refs_4_), channel_id=1, source_target_pairs={{5,9},{7,11},{9,5},{11,7},{16,32},{18,34},{20,36},{21,25},{22,38},... | collective-permute-start | bytes 2359304 | tf_op jit(solution)/shard_map/ppermute | solution.py:236
  7.7 0.1 stack.46.live
  7.8 0.0 copy-done.1
  7.8 0.0 copy-done
  7.8 1.6 %stats.3.refs_2_ = f32[3,3,8,512]{3,2,1,0:T(8,128)S(1)} custom-call(s32[8]{0:T(128)S(1)} %stack.46.live, bf16[3,512,128]{2,1,0:T(8,128)(2,1)S(1)} %bitcast.17, bf16[3,512,128]{2,1,0:T(8,128)(2,1)S(1)} %bitcast.22, bf16[1,2,3,512,128]{4,3,2,1,0:T(8,128)(2,1)S(1)} %maximum_bitcast_fusion.refs_0_.refs_4_), custom_call_target="tpu_custom_call" | custom-call | flops 1000 | bytes 1000 | tf_op jit(solution)/shard_map/stats/pallas_call | solution.py:133
  9.4 4.6 %collective-permute-done.refs_0_.a_ref.refs_2_ = bf16[1,2,3,512,128]{4,3,2,1,0:T(8,128)(2,1)S(1)} collective-permute-done((bf16[1,2,3,512,128]{4,3,2,1,0:T(8,128)(2,1)S(1)}, bf16[1,2,3,512,128]{4,3,2,1,0:T(8,128)(2,1)S(1)}, u32[]{:S(2)}, u32[]{:S(2)}) %collective-permute-start) | collective-permute-done | bytes 786464 | tf_op jit(solution)/shard_map/ppermute | solution.py:236
  14.0 3.4 %collective-permute-start.2 = (bf16[1,2,3,512,128]{4,3,2,1,0:T(8,128)(2,1)S(1)}, bf16[1,2,3,512,128]{4,3,2,1,0:T(8,128)(2,1)S(1)}, u32[]{:S(2)}, u32[]{:S(2)}) collective-permute-start(bf16[1,2,3,512,128]{4,3,2,1,0:T(8,128)(2,1)S(1)} %maximum_bitcast_fusion.refs_0_.refs_4_), channel_id=1, source_target_pairs={{4,8},{6,10},{8,4},{10,6},{17,33},{19,35},{20,24},{21,37},{22,26},... | collective-permute-start | bytes 2359304 | tf_op jit(solution)/shard_map/ppermute | solution.py:236
  17.4 0.1 collective-permute-start.1
  17.5 2.4 %collective-permute-done.3.refs_1_.b_ref.refs_3_ = bf16[1,2,3,512,128]{4,3,2,1,0:T(8,128)(2,1)S(1)} collective-permute-done((bf16[1,2,3,512,128]{4,3,2,1,0:T(8,128)(2,1)S(1)}, bf16[1,2,3,512,128]{4,3,2,1,0:T(8,128)(2,1)S(1)}, u32[]{:S(2)}, u32[]{:S(2)}) %collective-permute-start.3) | collective-permute-done | bytes 786464 | tf_op jit(solution)/shard_map/ppermute | solution.py:236
  19.9 1.3 %join.1 = bf16[2,2,3,512,128]{4,3,2,1,0:T(8,128)(2,1)} custom-call(bf16[1,2,3,512,128]{4,3,2,1,0:T(8,128)(2,1)S(1)} %collective-permute-done.refs_0_.a_ref.refs_2_, bf16[1,2,3,512,128]{4,3,2,1,0:T(8,128)(2,1)S(1)} %collective-permute-done.3.refs_1_.b_ref.refs_3_), custom_call_target="tpu_custom_call" | custom-call | flops 1000 | bytes 1000 | tf_op jit(solution)/shard_map/join/pallas_call | solution.py:165
  21.2 0.5 collective-permute-start.5
  21.7 4.2 %collective-permute-start.4 = (bf16[2,2,3,512,128]{4,3,2,1,0:T(8,128)(2,1)}, bf16[2,2,3,512,128]{4,3,2,1,0:T(8,128)(2,1)}, u32[]{:S(2)}, u32[]{:S(2)}) collective-permute-start(bf16[2,2,3,512,128]{4,3,2,1,0:T(8,128)(2,1)} %join.1), channel_id=1, source_target_pairs={{4,8},{6,10},{8,4},{10,6},{17,33},{19,35},{20,24},{21,37},{22,26},... | collective-permute-start | bytes 4718600 | tf_op jit(solution)/shard_map/ppermute | solution.py:236
  25.9 2.4 %stats.4.refs_2_ = f32[3,3,8,512]{3,2,1,0:T(8,128)S(1)} custom-call(s32[8]{0:T(128)S(1)} %stack.46.live, bf16[3,512,128]{2,1,0:T(8,128)(2,1)S(1)} %bitcast.18, bf16[3,512,128]{2,1,0:T(8,128)(2,1)S(1)} %bitcast.23, bf16[1,2,3,512,128]{4,3,2,1,0:T(8,128)(2,1)S(1)} %collective-permute-done.refs_0_.a_ref.refs_2_, ...), custom_call_target="tpu_custom_call" | custom-call | flops 1000 | bytes 1000 | tf_op jit(solution)/shard_map/stats/pallas_call | solution.py:133
  28.4 0.0 collective-permute-done.2.refs_1_
  28.4 1.1 %collective-permute-done.1.refs_0_ = bf16[1,2,3,512,128]{4,3,2,1,0:T(8,128)(2,1)S(1)} collective-permute-done((bf16[1,2,3,512,128]{4,3,2,1,0:T(8,128)(2,1)S(1)}, bf16[1,2,3,512,128]{4,3,2,1,0:T(8,128)(2,1)S(1)}, u32[]{:S(2)}, u32[]{:S(2)}) %collective-permute-start.1) | collective-permute-done | bytes 786464 | tf_op jit(solution)/shard_map/ppermute | solution.py:236
  29.4 2.5 %stats.5.st_ref = f32[3,3,8,512]{3,2,1,0:T(8,128)S(1)} custom-call(s32[8]{0:T(128)S(1)} %stack.46.live, bf16[3,512,128]{2,1,0:T(8,128)(2,1)S(1)} %bitcast.19, bf16[3,512,128]{2,1,0:T(8,128)(2,1)S(1)} %bitcast.24, bf16[1,2,3,512,128]{4,3,2,1,0:T(8,128)(2,1)S(1)} %collective-permute-done.1.refs_0_, ...), custom_call_target="tpu_custom_call" | custom-call | flops 19999999655936 | bytes 1000 | tf_op jit(solution)/shard_map/stats/pallas_call | solution.py:133
  31.9 14.5 %collective-permute-done.5.refs_1_ = bf16[2,2,3,512,128]{4,3,2,1,0:T(8,128)(2,1)} collective-permute-done((bf16[2,2,3,512,128]{4,3,2,1,0:T(8,128)(2,1)}, bf16[2,2,3,512,128]{4,3,2,1,0:T(8,128)(2,1)}, u32[]{:S(2)}, u32[]{:S(2)}) %collective-permute-start.5) | collective-permute-done | bytes 1572896 | tf_op jit(solution)/shard_map/ppermute | solution.py:236
  46.4 0.0 collective-permute-done.4.refs_0_
  46.4 13.2 %corner.1 = (bf16[2,2,3,512,128]{4,3,2,1,0:T(8,128)(2,1)S(1)}, bf16[2,2,3,512,128]{4,3,2,1,0:T(8,128)(2,1)S(1)}, f32[3,2,8,512]{3,2,1,0:T(8,128)S(1)}, f32[3,128,512]{2,1,0:T(8,128)S(1)}) custom-call(s32[8]{0:T(128)S(1)} %stack.46.live, bf16[3,512,128]{2,1,0:T(8,128)(2,1)S(1)} %bitcast.20, bf16[3,512,128]{2,1,0:T(8,128)(2,1)S(1)} %bitcast.25, ...), custom_call_target="tpu_custom_call" | custom-call | flops 1000 | bytes 1000 | tf_op jit(solution)/shard_map/corner/pallas_call | solution.py:118
  59.7 2.4 %collective-permute-start.8 = (bf16[2,2,3,512,128]{4,3,2,1,0:T(8,128)(2,1)S(1)}, bf16[2,2,3,512,128]{4,3,2,1,0:T(8,128)(2,1)S(1)}, u32[]{:S(2)}, u32[]{:S(2)}) collective-permute-start(bf16[2,2,3,512,128]{4,3,2,1,0:T(8,128)(2,1)S(1)} %get-tuple-element.31), channel_id=1, source_target_pairs={{4,8},{6,10},{8,4},{10,6},{17,33},{19,35},{20,24},{21,37},{22,26},... | collective-permute-start | bytes 4718600 | tf_op jit(solution)/shard_map/ppermute | solution.py:236
  62.1 0.1 collective-permute-start.9
  62.2 10.8 %grads.1 = (bf16[1,2,3,512,128]{4,3,2,1,0:T(8,128)(2,1)S(1)}, bf16[1,2,3,512,128]{4,3,2,1,0:T(8,128)(2,1)S(1)}, f32[1,2,3,512,128]{4,3,2,1,0:T(8,128)S(1)}, f32[...) custom-call(s32[8]{0:T(128)S(1)} %stack.46.live, ...), custom_call_target="tpu_custom_call" | custom-call | flops 1000 | bytes 1000 | tf_op jit(solution)/shard_map/grads/pallas_call | solution.py:147
  73.0 3.4 %collective-permute-start.6 = (bf16[1,2,3,512,128]{4,3,2,1,0:T(8,128)(2,1)S(1)}, bf16[1,2,3,512,128]{4,3,2,1,0:T(8,128)(2,1)S(1)}, u32[]{:S(2)}, u32[]{:S(2)}) collective-permute-start(bf16[1,2,3,512,128]{4,3,2,1,0:T(8,128)(2,1)S(1)} %get-tuple-element.27), channel_id=1, source_target_pairs={{4,8},{6,10},{8,4},{10,6},{17,33},{19,35},{20,24},{21,37},{22,26},... | collective-permute-start | bytes 2359304 | tf_op jit(solution)/shard_map/ppermute | solution.py:236
  76.4 0.1 collective-permute-start.7
  76.5 5.5 %collective-permute-done.8.from_a = bf16[2,2,3,512,128]{4,3,2,1,0:T(8,128)(2,1)S(1)} collective-permute-done((bf16[2,2,3,512,128]{4,3,2,1,0:T(8,128)(2,1)S(1)}, bf16[2,2,3,512,128]{4,3,2,1,0:T(8,128)(2,1)S(1)}, u32[]{:S(2)}, u32[]{:S(2)}) %collective-permute-start.8) | collective-permute-done | bytes 1572896 | tf_op jit(solution)/shard_map/ppermute | solution.py:236
  82.0 0.6 collective-permute-done.9.from_b
  82.6 0.5 relay.1
  83.1 5.0 %collective-permute-start.10 = (bf16[1,2,3,512,128]{4,3,2,1,0:T(8,128)(2,1)S(1)}, bf16[1,2,3,512,128]{4,3,2,1,0:T(8,128)(2,1)S(1)}, u32[]{:S(2)}, u32[]{:S(2)}) collective-permute-start(bf16[1,2,3,512,128]{4,3,2,1,0:T(8,128)(2,1)S(1)} %get-tuple-element.33), channel_id=1, source_target_pairs={{5,9},{7,11},{9,5},{11,7},{16,32},{18,34},{20,36},{21,25},{22,38},... | collective-permute-start | bytes 2359304 | tf_op jit(solution)/shard_map/ppermute | solution.py:236
  88.1 0.1 collective-permute-start.11
  88.2 3.2 %collective-permute-done.6.refs_0_ = bf16[1,2,3,512,128]{4,3,2,1,0:T(8,128)(2,1)S(1)} collective-permute-done((bf16[1,2,3,512,128]{4,3,2,1,0:T(8,128)(2,1)S(1)}, bf16[1,2,3,512,128]{4,3,2,1,0:T(8,128)(2,1)S(1)}, u32[]{:S(2)}, u32[]{:S(2)}) %collective-permute-start.6) | collective-permute-done | bytes 786464 | tf_op jit(solution)/shard_map/ppermute | solution.py:236
  91.5 0.0 collective-permute-done.7.refs_1_
  91.5 9.8 %collective-permute-done.10.refs_2_ = bf16[1,2,3,512,128]{4,3,2,1,0:T(8,128)(2,1)S(1)} collective-permute-done((bf16[1,2,3,512,128]{4,3,2,1,0:T(8,128)(2,1)S(1)}, bf16[1,2,3,512,128]{4,3,2,1,0:T(8,128)(2,1)S(1)}, u32[]{:S(2)}, u32[]{:S(2)}) %collective-permute-start.10) | collective-permute-done | bytes 786464 | tf_op jit(solution)/shard_map/ppermute | solution.py:236
  101.3 0.0 collective-permute-done.11.refs_3_
  101.3 1.3 %total.1 = (bf16[3,512,128]{2,1,0:T(8,128)(2,1)}, bf16[3,512,128]{2,1,0:T(8,128)(2,1)}) custom-call(f32[1,2,3,512,128]{4,3,2,1,0:T(8,128)S(1)} %get-tuple-element.26.own, bf16[1,2,3,512,128]{4,3,2,1,0:T(8,128)(2,1)S(1)} %collective-permute-done.6.refs_0_, bf16[1,2,3,512,128]{4,3,2,1,0:T(8,128)(2,1)S(1)} %collective-permute-done.7.refs_1_, ...), custom_call_target="tpu_custom_call" | custom-call | flops 1000 | bytes 1000 | tf_op jit(solution)/shard_map/total/pallas_call | solution.py:207
Async XLA Ops:
  0.6 7.2 %copy-start.1 = (bf16[3,4,8,16,128]{4,3,2,1,0:T(8,128)(2,1)S(1)}, bf16[3,4,8,16,128]{4,3,2,1,0:T(8,128)(2,1)}, u32[]{:S(2)}) copy-start(bf16[3,4,8,16,128]{4,3,2,1,0:T(8,128)(2,1)} %param.7) | copy-start | bytes 1179652
  0.6 7.2 %copy-start = (bf16[3,4,8,16,128]{4,3,2,1,0:T(8,128)(2,1)S(1)}, bf16[3,4,8,16,128]{4,3,2,1,0:T(8,128)(2,1)}, u32[]{:S(2)}) copy-start(bf16[3,4,8,16,128]{4,3,2,1,0:T(8,128)(2,1)} %param.4) | copy-start | bytes 1179652
  1.9 12.1 %collective-permute-start = (bf16[1,2,3,512,128]{4,3,2,1,0:T(8,128)(2,1)S(1)}, bf16[1,2,3,512,128]{4,3,2,1,0:T(8,128)(2,1)S(1)}, u32[]{:S(2)}, u32[]{:S(2)}) collective-permute-start(bf16[1,2,3,512,128]{4,3,2,1,0:T(8,128)(2,1)S(1)} %maximum_bitcast_fusion.refs_0_.refs_4_), channel_id=1, source_target_pairs={{0,16},{1,5},{2,18},{3,7},{4,20},{5,1},{6,22},{7,3},{8,24},{9,13},... | collective-permute-start | bytes 2359304 | tf_op jit(solution)/shard_map/ppermute | solution.py:236
  2.4 17.5 %collective-permute-start.3 = (bf16[1,2,3,512,128]{4,3,2,1,0:T(8,128)(2,1)S(1)}, bf16[1,2,3,512,128]{4,3,2,1,0:T(8,128)(2,1)S(1)}, u32[]{:S(2)}, u32[]{:S(2)}) collective-permute-start(bf16[1,2,3,512,128]{4,3,2,1,0:T(8,128)(2,1)S(1)} %maximum_bitcast_fusion.refs_0_.refs_4_), channel_id=1, source_target_pairs={{5,9},{7,11},{9,5},{11,7},{16,32},{18,34},{20,36},{21,25},{22,38},... | collective-permute-start | bytes 2359304 | tf_op jit(solution)/shard_map/ppermute | solution.py:236
  14.0 14.4 %collective-permute-start.2 = (bf16[1,2,3,512,128]{4,3,2,1,0:T(8,128)(2,1)S(1)}, bf16[1,2,3,512,128]{4,3,2,1,0:T(8,128)(2,1)S(1)}, u32[]{:S(2)}, u32[]{:S(2)}) collective-permute-start(bf16[1,2,3,512,128]{4,3,2,1,0:T(8,128)(2,1)S(1)} %maximum_bitcast_fusion.refs_0_.refs_4_), channel_id=1, source_target_pairs={{4,8},{6,10},{8,4},{10,6},{17,33},{19,35},{20,24},{21,37},{22,26},... | collective-permute-start | bytes 2359304 | tf_op jit(solution)/shard_map/ppermute | solution.py:236
  17.4 12.1 %collective-permute-start.1 = (bf16[1,2,3,512,128]{4,3,2,1,0:T(8,128)(2,1)S(1)}, bf16[1,2,3,512,128]{4,3,2,1,0:T(8,128)(2,1)S(1)}, u32[]{:S(2)}, u32[]{:S(2)}) collective-permute-start(bf16[1,2,3,512,128]{4,3,2,1,0:T(8,128)(2,1)S(1)} %maximum_bitcast_fusion.refs_0_.refs_4_), channel_id=1, source_target_pairs={{0,4},{1,17},{2,6},{3,19},{4,0},{5,21},{6,2},{7,23},{8,12},{9,25},... | collective-permute-start | bytes 2359304 | tf_op jit(solution)/shard_map/ppermute | solution.py:236
  21.2 25.3 %collective-permute-start.5 = (bf16[2,2,3,512,128]{4,3,2,1,0:T(8,128)(2,1)}, bf16[2,2,3,512,128]{4,3,2,1,0:T(8,128)(2,1)}, u32[]{:S(2)}, u32[]{:S(2)}) collective-permute-start(bf16[2,2,3,512,128]{4,3,2,1,0:T(8,128)(2,1)} %join.1), channel_id=1, source_target_pairs={{0,4},{1,17},{2,6},{3,19},{4,0},{5,21},{6,2},{7,23},{8,12},{9,25},... | collective-permute-start | bytes 4718600 | tf_op jit(solution)/shard_map/ppermute | solution.py:236
  21.7 24.7 %collective-permute-start.4 = (bf16[2,2,3,512,128]{4,3,2,1,0:T(8,128)(2,1)}, bf16[2,2,3,512,128]{4,3,2,1,0:T(8,128)(2,1)}, u32[]{:S(2)}, u32[]{:S(2)}) collective-permute-start(bf16[2,2,3,512,128]{4,3,2,1,0:T(8,128)(2,1)} %join.1), channel_id=1, source_target_pairs={{4,8},{6,10},{8,4},{10,6},{17,33},{19,35},{20,24},{21,37},{22,26},... | collective-permute-start | bytes 4718600 | tf_op jit(solution)/shard_map/ppermute | solution.py:236
  59.7 22.3 %collective-permute-start.8 = (bf16[2,2,3,512,128]{4,3,2,1,0:T(8,128)(2,1)S(1)}, bf16[2,2,3,512,128]{4,3,2,1,0:T(8,128)(2,1)S(1)}, u32[]{:S(2)}, u32[]{:S(2)}) collective-permute-start(bf16[2,2,3,512,128]{4,3,2,1,0:T(8,128)(2,1)S(1)} %get-tuple-element.31), channel_id=1, source_target_pairs={{4,8},{6,10},{8,4},{10,6},{17,33},{19,35},{20,24},{21,37},{22,26},... | collective-permute-start | bytes 4718600 | tf_op jit(solution)/shard_map/ppermute | solution.py:236
  62.1 20.5 %collective-permute-start.9 = (bf16[2,2,3,512,128]{4,3,2,1,0:T(8,128)(2,1)S(1)}, bf16[2,2,3,512,128]{4,3,2,1,0:T(8,128)(2,1)S(1)}, u32[]{:S(2)}, u32[]{:S(2)}) collective-permute-start(bf16[2,2,3,512,128]{4,3,2,1,0:T(8,128)(2,1)S(1)} %get-tuple-element.32), channel_id=1, source_target_pairs={{0,4},{1,17},{2,6},{3,19},{4,0},{5,21},{6,2},{7,23},{8,12},{9,25},... | collective-permute-start | bytes 4718600 | tf_op jit(solution)/shard_map/ppermute | solution.py:236
  73.0 18.5 %collective-permute-start.6 = (bf16[1,2,3,512,128]{4,3,2,1,0:T(8,128)(2,1)S(1)}, bf16[1,2,3,512,128]{4,3,2,1,0:T(8,128)(2,1)S(1)}, u32[]{:S(2)}, u32[]{:S(2)}) collective-permute-start(bf16[1,2,3,512,128]{4,3,2,1,0:T(8,128)(2,1)S(1)} %get-tuple-element.27), channel_id=1, source_target_pairs={{4,8},{6,10},{8,4},{10,6},{17,33},{19,35},{20,24},{21,37},{22,26},... | collective-permute-start | bytes 2359304 | tf_op jit(solution)/shard_map/ppermute | solution.py:236
  76.4 15.1 %collective-permute-start.7 = (bf16[1,2,3,512,128]{4,3,2,1,0:T(8,128)(2,1)S(1)}, bf16[1,2,3,512,128]{4,3,2,1,0:T(8,128)(2,1)S(1)}, u32[]{:S(2)}, u32[]{:S(2)}) collective-permute-start(bf16[1,2,3,512,128]{4,3,2,1,0:T(8,128)(2,1)S(1)} %get-tuple-element.28), channel_id=1, source_target_pairs={{0,4},{1,17},{2,6},{3,19},{4,0},{5,21},{6,2},{7,23},{8,12},{9,25},... | collective-permute-start | bytes 2359304 | tf_op jit(solution)/shard_map/ppermute | solution.py:236
  83.1 18.2 %collective-permute-start.10 = (bf16[1,2,3,512,128]{4,3,2,1,0:T(8,128)(2,1)S(1)}, bf16[1,2,3,512,128]{4,3,2,1,0:T(8,128)(2,1)S(1)}, u32[]{:S(2)}, u32[]{:S(2)}) collective-permute-start(bf16[1,2,3,512,128]{4,3,2,1,0:T(8,128)(2,1)S(1)} %get-tuple-element.33), channel_id=1, source_target_pairs={{5,9},{7,11},{9,5},{11,7},{16,32},{18,34},{20,36},{21,25},{22,38},... | collective-permute-start | bytes 2359304 | tf_op jit(solution)/shard_map/ppermute | solution.py:236
  88.1 13.2 %collective-permute-start.11 = (bf16[1,2,3,512,128]{4,3,2,1,0:T(8,128)(2,1)S(1)}, bf16[1,2,3,512,128]{4,3,2,1,0:T(8,128)(2,1)S(1)}, u32[]{:S(2)}, u32[]{:S(2)}) collective-permute-start(bf16[1,2,3,512,128]{4,3,2,1,0:T(8,128)(2,1)S(1)} %get-tuple-element.34), channel_id=1, source_target_pairs={{0,16},{1,5},{2,18},{3,7},{4,20},{5,1},{6,22},{7,3},{8,24},{9,13},... | collective-permute-start | bytes 2359304 | tf_op jit(solution)/shard_map/ppermute | solution.py:236
